TPU v7x, 32 devices: a whole 2x2x4 slice. The times are simulated.
32 devices in a mesh: dp: 8 (over z, y), seq: 4 (over x, core).
Axes of the slice: x: 2, y: 2, z: 4, core: 2. Of those that a mesh axis runs over, the one named last changes fastest.
Arguments:
- tokens: bfloat16 [24, 1024, 768], P('dp', 'seq'), may hold values from -6 to 6
- prefix_len: int32 [24], P('dp'), may hold values from 0 to 1023
- timestep: int32 [24], P('dp'), may hold values from 1 to 1023
- norm_gain: bfloat16 [768], P('dp'), may hold values from 0.25 to 1.75
- norm_bias: bfloat16 [768], P('dp'), may hold values from -4 to 4
- proj_in: bfloat16 [768, 2304], P('dp'), may hold values from -0.21875 to 0.21875
- proj_in_bias: bfloat16 [2304], P('dp'), may hold values from -4 to 4
- proj_out: bfloat16 [768, 768], P('dp'), may hold values from -0.875 to 0.875
- proj_out_bias: bfloat16 [768], P('dp'), may hold values from -4 to 4
- time_table: bfloat16 [1024, 768], P('dp'), may hold values from -6 to 6
- ada_weight: bfloat16 [768, 2304], P('dp'), may hold values from -0.21875 to 0.21875
- ada_bias: bfloat16 [2304], P('dp'), may hold values from -6 to 6
- mlp_up: bfloat16 [768, 3072], P('dp'), may hold values from -0.21875 to 0.21875
- mlp_up_bias: bfloat16 [3072], P('dp'), may hold values from -4 to 4
- mlp_down: bfloat16 [3072, 768], P('dp'), may hold values from -0.109375 to 0.109375
- mlp_down_bias: bfloat16 [768], P('dp'), may hold values from -4 to 4
- out_grad: bfloat16 [24, 1024, 768], P('dp', 'seq'), may hold values from -6 to 6
Outputs:
- block_out: bfloat16 [24, 1024, 768], P('dp', 'seq')
- tokens_grad: float32 [24, 1024, 768], P('dp', 'seq')
- norm_gain_grad: float32 [768], P('dp')
- norm_bias_grad: float32 [768], P('dp')
- proj_in_grad: float32 [768, 2304], P('dp')
- proj_in_bias_grad: float32 [2304], P('dp')
- proj_out_grad: float32 [768, 768], P('dp')
- proj_out_bias_grad: float32 [768], P('dp')
- time_table_grad: float32 [1024, 768], P('dp')
- ada_weight_grad: float32 [768, 2304], P('dp')
- ada_bias_grad: float32 [2304], P('dp')
- mlp_up_grad: float32 [768, 3072], P('dp')
- mlp_up_bias_grad: float32 [3072], P('dp')
- mlp_down_grad: float32 [3072, 768], P('dp')
- mlp_down_bias_grad: float32 [768], P('dp')
All inputs are finite; a program needn't handle non-finite values.
Results may differ from a plain program's by a relative error of at most 0.012.
Values may be sent and summed in bfloat16 or wider, within the bound.
No kernel may reach another device: no remote copies, remote signals or barrier semaphores. Data moves between devices by JAX's collectives and lax.ppermute only.
A program may use at most 192 MiB of HBM per device.

v0:
```python
import math

import jax
import jax.numpy as jnp
from jax import lax
from jax.sharding import PartitionSpec as P

H = 12
HD = 64


eps = 1e-05
neg_fill = -1e30
highest = lax.Precision.HIGHEST


def standardize(values):
    centred = values - jnp.mean(values, axis=-1, keepdims=True)
    inverse = lax.rsqrt(jnp.mean(centred * centred, axis=-1, keepdims=True) + eps)
    return (centred * inverse, inverse)


def norm_back(gradient, normed, inverse):
    return inverse * (
        gradient
        - jnp.mean(gradient, axis=-1, keepdims=True)
        - normed * jnp.mean(gradient * normed, axis=-1, keepdims=True)
    )


def rotary_tables(positions, half_width):
    frequency = jnp.exp(
        jnp.arange(half_width, dtype=jnp.float32) * (-math.log(10000.0) / half_width)
    )
    angles = positions.astype(jnp.float32)[:, None] * frequency[None, :]
    return (jnp.cos(angles), jnp.sin(angles))


def rotate(values, cosine, sine_table):
    half_width = cosine.shape[-1]
    front_half = values[..., :half_width]
    back_half = values[..., half_width:]
    cos_wide = cosine[:, None, :]
    sin_wide = sine_table[:, None, :]
    return jnp.concatenate(
        [
            front_half * cos_wide - back_half * sin_wide,
            back_half * cos_wide + front_half * sin_wide,
        ],
        axis=-1,
    )


def outer_sum(left, right):
    return lax.dot_general(
        left, right, (((0,), (0,)), ((), ())), preferred_element_type=jnp.float32
    )


def outer_exact(left, right):
    return lax.dot_general(
        left, right, (((0,), (0,)), ((), ())), precision=highest, preferred_element_type=jnp.float32
    )


def back_dot(gradient, weight):
    return lax.dot_general(
        gradient, weight, (((1,), (1,)), ((), ())), preferred_element_type=jnp.float32
    )


def gelu_exact(values):
    return jax.nn.gelu(values, approximate=False)


def visible_mask(prefix, length):
    places = jnp.arange(length, dtype=jnp.int32)
    clean = places < prefix
    return jnp.logical_or(jnp.logical_not(clean)[:, None], clean[None, :])


def masked_scores(queries, key_rows, prefix):
    scores = jnp.einsum(
        "qhd,khd->hqk", queries, key_rows, preferred_element_type=jnp.float32
    ) * HD ** (-0.5)
    return jnp.where(visible_mask(prefix, key_rows.shape[0])[None], scores, neg_fill)


def attend_forward(packed):
    heads_qkv, prefix = packed
    scores = masked_scores(heads_qkv[:, 0], heads_qkv[:, 1], prefix)
    row_max = jnp.max(scores, axis=-1, keepdims=True)
    exponent = jnp.exp(scores - row_max)
    row_total = jnp.sum(exponent, axis=-1, keepdims=True)
    weights = (exponent / row_total).astype(jnp.bfloat16)
    mixed_out = jnp.einsum(
        "hqk,khd->qhd", weights, heads_qkv[:, 2], preferred_element_type=jnp.float32
    )
    length = mixed_out.shape[0]
    return (
        mixed_out.astype(jnp.bfloat16).reshape(length, -1),
        (row_max + jnp.log(row_total))[..., 0],
    )


def attend_backward(packed):
    heads_qkv, log_total, mixed_grad, prefix = packed
    queries = heads_qkv[:, 0]
    key_rows = heads_qkv[:, 1]
    values = heads_qkv[:, 2]
    scores = masked_scores(queries, key_rows, prefix)
    weights = jnp.exp(scores - log_total[..., None])
    weight_grad = jnp.einsum("qhd,khd->hqk", mixed_grad, values, preferred_element_type=jnp.float32)
    centre = jnp.sum(weights * weight_grad, axis=-1, keepdims=True)
    score_grad = (weights * (weight_grad - centre)).astype(jnp.bfloat16)
    score_scale = HD ** (-0.5)
    query_grad = (
        jnp.einsum("hqk,khd->qhd", score_grad, key_rows, preferred_element_type=jnp.float32)
        * score_scale
    )
    key_grad = (
        jnp.einsum("hqk,qhd->khd", score_grad, queries, preferred_element_type=jnp.float32)
        * score_scale
    )
    value_grad = jnp.einsum(
        "hqk,qhd->khd", weights.astype(jnp.bfloat16), mixed_grad, preferred_element_type=jnp.float32
    )
    stacked = jnp.stack([query_grad, key_grad, value_grad], axis=1).astype(jnp.bfloat16)
    return stacked.reshape(stacked.shape[0], 3, -1)


def shards(
    tokens,
    prefix_len,
    timestep,
    norm_gain,
    norm_bias,
    proj_in,
    proj_in_bias,
    proj_out,
    proj_out_bias,
    time_table,
    ada_weight,
    ada_bias,
    mlp_up,
    mlp_up_bias,
    mlp_down,
    mlp_down_bias,
    out_grad,
):
    seq_count, local_len, model_width = tokens.shape
    seq_devices = lax.axis_size("seq")
    full_len = local_len * seq_devices
    local_heads = H // seq_devices
    (
        gain_full,
        bias_full,
        in_full,
        in_bias_full,
        out_full,
        out_bias_full,
        table_full,
        ada_full,
        ada_bias_full,
        up_full,
        up_bias_full,
        down_full,
        down_bias_full,
    ) = (
        lax.all_gather(norm_gain, "dp", axis=0, tiled=True),
        lax.all_gather(norm_bias, "dp", axis=0, tiled=True),
        lax.all_gather(proj_in, "dp", axis=0, tiled=True),
        lax.all_gather(proj_in_bias, "dp", axis=0, tiled=True),
        lax.all_gather(proj_out, "dp", axis=0, tiled=True),
        lax.all_gather(proj_out_bias, "dp", axis=0, tiled=True),
        lax.all_gather(time_table, "dp", axis=0, tiled=True),
        lax.all_gather(ada_weight, "dp", axis=0, tiled=True),
        lax.all_gather(ada_bias, "dp", axis=0, tiled=True),
        lax.all_gather(mlp_up, "dp", axis=0, tiled=True),
        lax.all_gather(mlp_up_bias, "dp", axis=0, tiled=True),
        lax.all_gather(mlp_down, "dp", axis=0, tiled=True),
        lax.all_gather(mlp_down_bias, "dp", axis=0, tiled=True),
    )
    inputs = tokens.astype(jnp.float32).reshape(-1, model_width)
    normed_one, inverse_one = standardize(inputs)
    attn_input = (
        normed_one * gain_full.astype(jnp.float32) + bias_full.astype(jnp.float32)
    ).astype(jnp.bfloat16)
    projected = jnp.dot(
        attn_input, in_full, preferred_element_type=jnp.float32
    ) + in_bias_full.astype(jnp.float32)
    projected = projected.reshape(seq_count, local_len, 3, H, HD)
    positions = lax.axis_index("seq") * local_len + jnp.arange(local_len, dtype=jnp.int32)
    cosine, sine_table = rotary_tables(positions, HD // 2)
    query_rot = rotate(projected[:, :, 0], cosine, sine_table)
    key_rot = rotate(projected[:, :, 1], cosine, sine_table)
    packed_qkv = (
        jnp.stack([query_rot, key_rot, projected[:, :, 2]], axis=2)
        .astype(jnp.bfloat16)
        .reshape(seq_count, local_len, 3, model_width)
    )
    head_qkv = lax.all_to_all(packed_qkv, "seq", split_axis=3, concat_axis=1, tiled=True).reshape(
        seq_count, full_len, 3, local_heads, HD
    )
    head_mixed, log_total = lax.map(attend_forward, (head_qkv, prefix_len))
    attn_mixed = lax.all_to_all(head_mixed, "seq", split_axis=1, concat_axis=2, tiled=True).reshape(
        -1, model_width
    )
    attn_out = jnp.dot(
        attn_mixed, out_full, preferred_element_type=jnp.float32
    ) + out_bias_full.astype(jnp.float32)
    residual_one = inputs + attn_out
    clean_tok = positions[None, :] < prefix_len[:, None]
    chosen = jnp.stack([jnp.zeros_like(timestep), timestep], axis=1).reshape(-1)
    selector = (
        chosen[:, None] == jnp.arange(table_full.shape[0], dtype=jnp.int32)[None, :]
    ).astype(jnp.bfloat16)
    embedded = jnp.dot(selector, table_full, preferred_element_type=jnp.float32)
    activated = jax.nn.silu(embedded).astype(jnp.bfloat16)
    modulation = (
        jnp.dot(activated, ada_full, preferred_element_type=jnp.float32)
        + ada_bias_full.astype(jnp.float32)
    ).reshape(seq_count, 2, 3 * model_width)
    token_mod = jnp.where(clean_tok[:, :, None], modulation[:, 0:1], modulation[:, 1:2]).reshape(
        -1, 3 * model_width
    )
    shift_mod = token_mod[:, :model_width]
    scale_mod = token_mod[:, model_width : 2 * model_width]
    gate_mod = token_mod[:, 2 * model_width :]
    normed_two, inverse_two = standardize(residual_one)
    mlp_input = (normed_two * (1.0 + scale_mod) + shift_mod).astype(jnp.bfloat16)
    pre_act = jnp.dot(mlp_input, up_full, preferred_element_type=jnp.float32) + up_bias_full.astype(
        jnp.float32
    )
    hidden = gelu_exact(pre_act).astype(jnp.bfloat16)
    branch = jnp.dot(hidden, down_full, preferred_element_type=jnp.float32) + down_bias_full.astype(
        jnp.float32
    )
    block_out = (
        (residual_one + gate_mod * branch)
        .astype(jnp.bfloat16)
        .reshape(seq_count, local_len, model_width)
    )
    gain_back, in_back, out_back, ada_back, up_back, down_back = (
        lax.all_gather(norm_gain, "dp", axis=0, tiled=True),
        lax.all_gather(proj_in, "dp", axis=0, tiled=True),
        lax.all_gather(proj_out, "dp", axis=0, tiled=True),
        lax.all_gather(ada_weight, "dp", axis=0, tiled=True),
        lax.all_gather(mlp_up, "dp", axis=0, tiled=True),
        lax.all_gather(mlp_down, "dp", axis=0, tiled=True),
    )
    incoming = out_grad.astype(jnp.float32).reshape(-1, model_width)
    gate_grad = incoming * branch
    branch_grad = (incoming * gate_mod).astype(jnp.bfloat16)
    down_bias_grad = jnp.sum(branch_grad, axis=0, dtype=jnp.float32)
    down_grad = outer_sum(hidden, branch_grad)
    act_grad = back_dot(branch_grad, down_back)
    pre_grad = jax.vjp(gelu_exact, pre_act)[1](act_grad)[0].astype(jnp.bfloat16)
    up_bias_grad = jnp.sum(pre_grad, axis=0, dtype=jnp.float32)
    up_grad = outer_sum(mlp_input, pre_grad)
    input_two = back_dot(pre_grad, up_back)
    resid_grad = incoming + norm_back(input_two * (1.0 + scale_mod), normed_two, inverse_two)
    mod_grad = (
        jnp.concatenate([input_two, input_two * normed_two, gate_grad], axis=-1)
        .astype(jnp.bfloat16)
        .reshape(seq_count, local_len, 3 * model_width)
    )
    group_weights = jnp.stack([clean_tok, jnp.logical_not(clean_tok)], axis=-1).astype(jnp.bfloat16)
    row_grad = jnp.einsum(
        "slc,slj->scj", group_weights, mod_grad, preferred_element_type=jnp.float32
    ).reshape(2 * seq_count, 3 * model_width)
    ada_bias_grad = jnp.sum(row_grad, axis=0)
    ada_grad = outer_exact(activated.astype(jnp.float32), row_grad)
    rows_act_grad = jnp.dot(
        row_grad,
        ada_back.astype(jnp.float32).T,
        precision=highest,
        preferred_element_type=jnp.float32,
    )
    embed_grad = jax.vjp(jax.nn.silu, embedded)[1](rows_act_grad)[0]
    table_grad = outer_exact(selector.astype(jnp.float32), embed_grad)
    attn_grad = resid_grad.astype(jnp.bfloat16)
    out_bias_grad = jnp.sum(attn_grad, axis=0, dtype=jnp.float32)
    out_weight_grad = outer_sum(attn_mixed, attn_grad)
    mixed_grad = (
        back_dot(attn_grad, out_back)
        .astype(jnp.bfloat16)
        .reshape(seq_count, local_len, model_width)
    )
    head_grad = lax.all_to_all(mixed_grad, "seq", split_axis=2, concat_axis=1, tiled=True).reshape(
        seq_count, full_len, local_heads, HD
    )
    head_back = lax.map(attend_backward, (head_qkv, log_total, head_grad, prefix_len))
    token_back = lax.all_to_all(head_back, "seq", split_axis=1, concat_axis=3, tiled=True).reshape(
        seq_count, local_len, 3, H, HD
    )
    query_back = rotate(token_back[:, :, 0].astype(jnp.float32), cosine, -sine_table)
    key_back = rotate(token_back[:, :, 1].astype(jnp.float32), cosine, -sine_table)
    value_back = token_back[:, :, 2].astype(jnp.float32)
    proj_grad = (
        jnp.stack([query_back, key_back, value_back], axis=2)
        .reshape(-1, 3 * model_width)
        .astype(jnp.bfloat16)
    )
    in_bias_grad = jnp.sum(proj_grad, axis=0, dtype=jnp.float32)
    in_grad = outer_sum(attn_input, proj_grad)
    normed_grad = back_dot(proj_grad, in_back)
    gain_grad = jnp.sum(normed_grad * normed_one, axis=0)
    bias_grad = jnp.sum(normed_grad, axis=0)
    input_grad = (
        resid_grad + norm_back(normed_grad * gain_back.astype(jnp.float32), normed_one, inverse_one)
    ).reshape(seq_count, local_len, model_width)
    (
        red_gain,
        red_bias,
        red_in,
        red_in_bias,
        red_out,
        red_out_bias,
        red_table,
        red_ada,
        red_ada_bias,
        red_up,
        red_up_bias,
        red_down,
        red_down_bias,
    ) = (
        lax.psum_scatter(gain_grad, "dp", scatter_dimension=0, tiled=True),
        lax.psum_scatter(bias_grad, "dp", scatter_dimension=0, tiled=True),
        lax.psum_scatter(in_grad, "dp", scatter_dimension=0, tiled=True),
        lax.psum_scatter(in_bias_grad, "dp", scatter_dimension=0, tiled=True),
        lax.psum_scatter(out_weight_grad, "dp", scatter_dimension=0, tiled=True),
        lax.psum_scatter(out_bias_grad, "dp", scatter_dimension=0, tiled=True),
        lax.psum_scatter(table_grad, "dp", scatter_dimension=0, tiled=True),
        lax.psum_scatter(ada_grad, "dp", scatter_dimension=0, tiled=True),
        lax.psum_scatter(ada_bias_grad, "dp", scatter_dimension=0, tiled=True),
        lax.psum_scatter(up_grad, "dp", scatter_dimension=0, tiled=True),
        lax.psum_scatter(up_bias_grad, "dp", scatter_dimension=0, tiled=True),
        lax.psum_scatter(down_grad, "dp", scatter_dimension=0, tiled=True),
        lax.psum_scatter(down_bias_grad, "dp", scatter_dimension=0, tiled=True),
    )
    summed = lax.psum(
        (
            red_gain,
            red_bias,
            red_in,
            red_in_bias,
            red_out,
            red_out_bias,
            red_table,
            red_ada,
            red_ada_bias,
            red_up,
            red_up_bias,
            red_down,
            red_down_bias,
        ),
        "seq",
    )
    return (
        block_out,
        input_grad,
        summed[0],
        summed[1],
        summed[2],
        summed[3],
        summed[4],
        summed[5],
        summed[6],
        summed[7],
        summed[8],
        summed[9],
        summed[10],
        summed[11],
        summed[12],
    )


def solution(mesh):
    in_specs = (
        P("dp", "seq", None),
        P("dp"),
        P("dp"),
        P("dp"),
        P("dp"),
        P("dp", None),
        P("dp"),
        P("dp", None),
        P("dp"),
        P("dp", None),
        P("dp", None),
        P("dp"),
        P("dp", None),
        P("dp"),
        P("dp", None),
        P("dp"),
        P("dp", "seq", None),
    )
    out_specs = (
        P("dp", "seq", None),
        P("dp", "seq", None),
        P("dp"),
        P("dp"),
        P("dp", None),
        P("dp"),
        P("dp", None),
        P("dp"),
        P("dp", None),
        P("dp", None),
        P("dp"),
        P("dp", None),
        P("dp"),
        P("dp", None),
        P("dp"),
    )
    return jax.shard_map(shards, mesh=mesh, in_specs=in_specs, out_specs=out_specs, check_vma=False)
```

profile of v0, /device:TPU:0, one launch (start us, length us, event | category | flops | bytes accessed | tf_op | source)
XLA Modules:
  0.0 1309.7 jit_solution(13434812604561325661)
XLA Ops:
  18.3 39.6 %all-reduce.17 = (bf16[768]{0:T(1024)(128)(2,1)S(1)}, bf16[768]{0:T(1024)(128)(2,1)S(1)}, bf16[2304]{0:T(1024)(128)(2,1)S(1)}, bf16[768]{0:T(1024)(128)(2,1)S(1)...) all-reduce(bf16[768]{0:T(1024)(128)(2,1)S(1)} %dynamic-update-slice, ...), channel_id=1, replica_groups=mesh['dp'=8,'seq'=4] {'dp'}, use_global_device_ids=true, to_apply=%add.2 | all-reduce | flops 7680 | bytes 30720
  60.6 18.0 %all-gather.8.cloned.1.call-done = bf16[768,2304]{1,0:T(8,128)(2,1)} async-done(((bf16[96,2304]{1,0:T(8,128)(2,1)}), bf16[768,2304]{1,0:T(8,128)(2,1)}) %all-gather.8.cloned.1.call-update) | async-done | bytes 3538960 | tf_op jit(solution)/shard_map/all_gather | solution.py:172
  78.6 6.9 convolution_add_fusion
  85.5 8.1 copy.77
  93.6 11.4 reshape.528
  107.5 3.9 slice_bitcast_fusion.15
  116.9 5.3 copy.81
  122.2 5.1 all-to-all-start
  128.3 26.0 %all-gather = bf16[8,1,384]{2,1,0:T(2,128)(2,1)S(1)} all-gather(bf16[1,1,384]{2,1,0:T(2,128)(2,1)S(1)} %reshape.562), channel_id=1, replica_groups=mesh['dp'=8,'seq'=4] {'dp'}, dimensions={0}, use_global_device_ids=true | all-gather | bytes 6912 | tf_op jit(solution)/shard_map/all_gather | solution.py:180
  157.4 32.5 %all-gather.14.cloned.1.call-done = bf16[768,2304]{1,0:T(8,128)(2,1)} async-done(((bf16[96,2304]{1,0:T(8,128)(2,1)}), bf16[768,2304]{1,0:T(8,128)(2,1)}) %all-gather.14.cloned.1.call-update) | async-done | bytes 3538960 | tf_op jit(solution)/shard_map/all_gather | solution.py:177
  193.2 2.9 copy.82
  198.8 4.4 reshape.529
  203.2 49.5 %while.22 = (s32[]{:T(128)}, bf16[3,1024,192]{1,2,0:T(8,128)(2,1)}, f32[3,3,1024]{2,1,0:T(4,128)}, bf16[3,1024,3,3,64]{1,4,3,2,0:T(8,128)(2,1)}, s32[3]{0:T(128)S(1)}, /*index=5*/s32[]{:T(128)}) while((s32[]{:T(128)}, bf16[3,1024,192]{1,2,0:T(8,128)(2,1)}, f32[3,3,1024]{2,1,0:T(4,128)}, bf16[3,1024,3,3,64]{1,4,3,2,0:T(8,128)(2,1)}, ...), condition=%wide.region_5.6_spmd, body=%wide.region_2.5_spmd.sunk | while | flops 844299264 | bytes 55682192 | solution.py:205
  209.4 3.9 fusion.141
  213.9 5.0 fusion.142
  225.9 3.9 fusion.141
  230.4 5.0 fusion.142
  242.4 3.9 fusion.141
  246.9 5.0 fusion.142
  252.7 4.1 copy.84
  256.8 3.7 all-to-all-start.1
  260.7 3.4 bitcast_select_fusion
  264.1 22.1 %all-to-all-done.1 = bf16[3,1024,192]{2,0,1:T(4,128)(2,1)S(1)} async-done(((bf16[3,1024,192]{2,0,1:T(4,128)(2,1)}), bf16[3,1024,192]{2,0,1:T(4,128)(2,1)S(1)}, u32[]{:S(2)}, u32[]{:S(2)}) %all-to-all-start.1) | async-done | bytes 1179680 | tf_op jit(solution)/shard_map/all_to_all | solution.py:206
  288.8 4.2 reshape.530
  297.1 5.0 convert_reduce_fusion.3
  302.1 10.1 all-gather.16.cloned.1.call-done
  312.3 8.5 fusion.95
  320.8 71.6 %all-gather.18.cloned.1.call-done = bf16[3072,768]{1,0:T(8,128)(2,1)} async-done(((bf16[384,768]{1,0:T(8,128)(2,1)}), bf16[3072,768]{1,0:T(8,128)(2,1)}) %all-gather.18.cloned.1.call-update) | async-done | bytes 4718608 | tf_op jit(solution)/shard_map/all_gather | solution.py:181
  392.4 29.9 %convert_reduce_fusion = (f32[3072]{0:T(1024)}, bf16[768,3072]{1,0:T(8,128)(2,1)}, f32[768,3072]{1,0:T(8,128)}) fusion(f32[768,3072]{1,0:T(8,128)} %fusion.95, f32[3072]{0:T(1024)S(1)} %bitcast.247, bf16[768,768]{1,0:T(8,128)(2,1)} %get-tuple-element.133, bf16[3072,768]{1,0:T(8,128)(2,1)} %all-gather.18.cloned.1.call-done), kind=kOutput, calls=%fused_computation.52 | convolution fusion | flops 3800822784 | bytes 29515776 | tf_op jit(solution)/shard_map/dot_general | solution.py:67
  422.3 10.9 multiply_convert_fusion.1
  433.2 8.8 fusion.86
  442.1 9.8 convert_reduce_fusion.4
  456.7 3.9 fusion.94
  462.2 3.7 fusion.97
  465.9 3.2 fusion.64
  475.4 3.6 all-to-all-start.2
  479.0 5.0 fusion.85
  484.0 14.9 %all-to-all-done.2 = bf16[3,256,768]{1,0,2:T(4,128)(2,1)S(1)} async-done(((bf16[3,256,768]{1,0,2:T(4,128)(2,1)}), bf16[3,256,768]{1,0,2:T(4,128)(2,1)S(1)}, u32[]{:S(2)}, u32[]{:S(2)}) %all-to-all-start.2) | async-done | bytes 1179680 | tf_op jit(solution)/shard_map/all_to_all | solution.py:290
  500.9 84.1 %while.23 = (s32[]{:T(128)}, bf16[3,1024,3,192]{1,3,2,0:T(8,128)(2,1)}, bf16[3,1024,3,3,64]{1,4,3,2,0:T(8,128)(2,1)}, s32[3]{0:T(128)S(1)}, f32[3,3,1024]{2,1,0:...) while((s32[]{:T(128)}, bf16[3,1024,3,192]{1,3,2,0:T(8,128)(2,1)}, ...), condition=%wide.region_12.13_spmd, body=%wide.region_10.12_spmd.sunk | while | flops 2066021376 | bytes 107315824 | solution.py:293
  506.9 7.0 multiply_reduce_fusion.5
  513.9 7.0 multiply_convert_fusion.7
  524.2 3.7 fusion.148
  534.8 7.0 multiply_reduce_fusion.5
  541.8 7.0 multiply_convert_fusion.7
  552.2 3.7 fusion.148
  562.8 7.0 multiply_reduce_fusion.5
  569.8 7.0 multiply_convert_fusion.7
  580.1 3.7 fusion.148
  585.0 9.9 copy.90
  595.0 5.4 all-to-all-start.3
  601.0 70.1 %all-to-all-done.3 = bf16[3,1024,3,192]{3,2,0,1:T(4,128)(2,1)} async-done(((bf16[3,1024,3,192]{3,2,0,1:T(4,128)(2,1)}), bf16[3,1024,3,192]{3,2,0,1:T(4,128)(2,1)}, u32[]{:S(2)}, u32[]{:S(2)}) %all-to-all-start.3) | async-done | bytes 3538976 | tf_op jit(solution)/shard_map/all_to_all | solution.py:294
  671.1 10.1 copy.92
  690.5 17.4 %convert_reduce_fusion.1 = (f32[3,12,64]{2,1,0:T(8,128)S(1)}, bf16[3,256,3,12,64]{1,0,4,3,2:T(4,128)(2,1)S(1)}) fusion(bf16[3,256,1,12,64]{1,0,4,3,2:T(4,128)(2,1)S(1)} %copy.119, bf16[3,256,1,12,64]{1,0,4,3,2:T(4,128)(2,1)S(1)} %maximum_bitcast_fusion.1, bf16[3,256,1,12,64]{1,0,4,3,2:T(4,128)(2,1)S(1)} %maximum_bitcast_fusion), kind=kLoop, calls=%fused_computation.53 | loop fusion | flops 7075584 | bytes 7087104 | tf_op jit(solution)/shard_map/reduce_sum | solution.py:305
  710.7 5.2 fusion.96
  717.2 8.7 fusion.99
  727.2 8.6 fusion.98
  735.9 128.3 %reduce-scatter.7.cloned.1.call-done = f32[96,2304]{1,0:T(8,128)} async-done(((f32[768,2304]{1,0:T(8,128)}), f32[96,2304]{1,0:T(8,128)}) %reduce-scatter.7.cloned.1.call-update) | async-done | bytes 884752 | tf_op jit(solution)/shard_map/reduce_scatter | solution.py:330
  864.2 166.1 %reduce-scatter.17.cloned.1.call-done = f32[384,768]{1,0:T(8,128)} async-done(((f32[3072,768]{1,0:T(8,128)}), f32[384,768]{1,0:T(8,128)}) %reduce-scatter.17.cloned.1.call-update) | async-done | bytes 1179664 | tf_op jit(solution)/shard_map/reduce_scatter | solution.py:339
  1030.3 166.0 %reduce-scatter.15.cloned.1.call-done = f32[96,3072]{1,0:T(8,128)} async-done(((f32[768,3072]{1,0:T(8,128)}), f32[96,3072]{1,0:T(8,128)}) %reduce-scatter.15.cloned.1.call-update) | async-done | bytes 1179664 | tf_op jit(solution)/shard_map/reduce_scatter | solution.py:337
  1198.4 8.7 fusion.60
  1207.1 36.8 %all-reduce.14 = (f32[768]{0:T(1024)}, f32[768]{0:T(1024)}, f32[2304]{0:T(1024)}, f32[768]{0:T(1024)}, f32[2304]{0:T(1024)}, /*index=5*/f32[3072]{0:T(1024)}, f32[768]{0:T(1024)}) all-reduce(f32[768]{0:T(1024)} %get-tuple-element.80, f32[768]{0:T(1024)} %get-tuple-element.83, ...), channel_id=2, replica_groups=mesh['dp'=8,'seq'=4] {'dp'}, use_global_device_ids=true, to_apply=%region_16.17.clone | all-reduce | flops 10752 | bytes 86016
  1251.3 7.0 all-reduce.15
  1259.6 3.9 fusion.59
  1263.5 31.6 %all-reduce.20.cloned.1.call-done = (f32[96,2304]{1,0:T(8,128)}, f32[96,768]{1,0:T(8,128)}, f32[128,768]{1,0:T(8,128)}, f32[96,2304]{1,0:T(8,128)}, f32[96,3072]{1,0:T(8,128)}, /*index=5*/f32[384,768]{1,0:T(8,128)}) async-done(((f32[96,2304]{1,0:T(8,128)}, f32[96,768]{1,0:T(8,128)}, f32[128,768]{1,0:T(8,128)}, f32[96,2304]{1,0:T(8,128)}, f32[96,3072]{1,0:T(8,128)}, /*index=5*/f32[384,768]{1,0:T(8,128)}), ...) | async-done | bytes 4816912 | tf_op jit(solution)/shard_map/psum | solution.py:342
  (286 shorter events, 136.4 us)
Async XLA Ops:
  7.2 50.8 %copy-start.1 = (bf16[3,256,768]{2,1,0:T(8,128)(2,1)S(1)}, bf16[3,256,768]{2,1,0:T(8,128)(2,1)}, u32[]{:S(2)}) copy-start(bf16[3,256,768]{2,1,0:T(8,128)(2,1)} %param.21) | copy-start | bytes 3538948
  7.2 71.4 %all-gather.8.cloned.1.call-start = ((), (), s32[]{:S(2)}) async-start(), calls=%async_computation.10 | async-start | bytes 3981312 | tf_op jit(solution)/shard_map/all_gather | solution.py:172
  7.9 147.6 %all-gather.12.cloned.1.call-start = ((), (), s32[]{:S(2)}) async-start(), calls=%async_computation.12 | async-start | bytes 1769472 | tf_op jit(solution)/shard_map/all_gather | solution.py:176
  8.7 181.3 %all-gather.14.cloned.1.call-start = ((), (), s32[]{:S(2)}) async-start(), calls=%async_computation.13 | async-start | bytes 3981312 | tf_op jit(solution)/shard_map/all_gather | solution.py:177
  9.4 283.6 %all-gather.10.cloned.1.call-start = ((), (), s32[]{:S(2)}) async-start(), calls=%async_computation.11 | async-start | bytes 1327104 | tf_op jit(solution)/shard_map/all_gather | solution.py:174
  10.0 302.3 %all-gather.16.cloned.1.call-start = ((), (), s32[]{:S(2)}) async-start(), calls=%async_computation.14 | async-start | bytes 5308416 | tf_op jit(solution)/shard_map/all_gather | solution.py:179
  57.9 2.7 copy-start.29
  57.9 2.7 copy-start.36
  58.2 27.3 %copy-start.34 = (f32[768]{0:T(1024)}, f32[768]{0:T(1024)S(1)}, u32[]{:S(2)}) copy-start(f32[768]{0:T(1024)S(1)} %div.41) | copy-start | bytes 9220
  58.7 26.8 %copy-start.35 = (f32[768]{0:T(1024)}, f32[768]{0:T(1024)S(1)}, u32[]{:S(2)}) copy-start(f32[768]{0:T(1024)S(1)} %rsqrt.21) | copy-start | bytes 9220
  58.8 69.4 %copy-start.42 = (s32[256]{0:T(256)}, s32[256]{0:T(256)S(1)}, u32[]{:S(2)}) copy-start(s32[256]{0:T(256)S(1)} %get-tuple-element.188) | copy-start | bytes 3076
  60.1 51.4 %copy-start.25 = (f32[256,32]{0,1:T(8,128)}, f32[256,32]{0,1:T(8,128)S(1)}, u32[]{:S(2)}) copy-start(f32[256,32]{0,1:T(8,128)S(1)} %get-tuple-element.177) | copy-start | bytes 98308
  122.2 5.7 copy-start.50
  122.2 6.0 copy-start.47
  122.2 6.1 copy-start.49
  122.2 71.0 %all-to-all-start = ((bf16[3,256,3,768]{1,0,2,3:T(4,128)(2,1)}), bf16[3,256,3,768]{1,0,2,3:T(4,128)(2,1)}, u32[]{:S(2)}, u32[]{:S(2)}) async-start(bf16[3,256,3,768]{1,0,2,3:T(4,128)(2,1)} %copy.81), calls=%async_computation | async-start | bytes 9437184 | tf_op jit(solution)/shard_map/all_to_all | solution.py:202
  127.2 265.1 %all-gather.18.cloned.1.call-start = ((), (), s32[]{:S(2)}) async-start(), calls=%async_computation.15 | async-start | bytes 5308416 | tf_op jit(solution)/shard_map/all_gather | solution.py:181
  128.1 29.3 %copy-start.44 = (s32[6]{0:T(128)}, s32[6]{0:T(128)S(1)}, u32[]{:S(2)}) copy-start(s32[6]{0:T(128)S(1)} %eq.15) | copy-start | bytes 76
  157.4 38.7 %copy-start.21 = (f32[6,768]{1,0:T(8,128)}, f32[6,768]{1,0:T(8,128)S(1)}, u32[]{:S(2)}) copy-start(f32[6,768]{1,0:T(8,128)S(1)} %fusion.65) | copy-start | bytes 55300
  205.0 4.4 copy-start
  206.8 2.6 copy-start.4
  221.5 4.4 copy-start
  223.2 2.6 copy-start.4
  237.9 4.4 copy-start
  239.8 2.6 copy-start.4
  256.8 3.8 copy-start.27
  256.8 29.4 %all-to-all-start.1 = ((bf16[3,1024,192]{2,0,1:T(4,128)(2,1)}), bf16[3,1024,192]{2,0,1:T(4,128)(2,1)S(1)}, u32[]{:S(2)}, u32[]{:S(2)}) async-start(bf16[3,1024,192]{2,0,1:T(4,128)(2,1)} %copy.84), calls=%async_computation.1 | async-start | bytes 4194304 | tf_op jit(solution)/shard_map/all_to_all | solution.py:206
  260.5 475.4 %reduce-scatter.9.cloned.1.call-start = ((), (), s32[]{:S(2)}) async-start(), calls=%async_computation.17 | async-start | bytes 2654208 | tf_op jit(solution)/shard_map/reduce_scatter | solution.py:332
  286.2 6.8 copy-start.2
  295.8 1.3 copy-start.15
  297.1 5.0 copy-start.40
  302.1 18.6 %copy-start.7 = (bf16[768,768]{1,0:T(8,128)(2,1)}, bf16[768,768]{1,0:T(8,128)(2,1)S(1)}, u32[]{:S(2)}) copy-start(bf16[768,768]{1,0:T(8,128)(2,1)S(1)} %get-tuple-element.154) | copy-start | bytes 3538948
  312.3 80.1 %copy-start.33 = (f32[8,1,384]{2,1,0:T(1,128)S(1)}, f32[8,1,384]{2,1,0:T(1,128)}, u32[]{:S(2)}) copy-start(f32[8,1,384]{2,1,0:T(1,128)} %convert_element_type.173) | copy-start | bytes 36868
  422.3 10.9 copy-start.41
  433.2 8.8 copy-start.6
  433.2 8.9 copy-start.16
  433.2 8.9 copy-start.46
  442.1 11.2 copy-start.18
  451.9 1.4 copy-start.10
  455.9 280.0 %reduce-scatter.11.cloned.1.call-start = ((), (), s32[]{:S(2)}) async-start(), calls=%async_computation.18 | async-start | bytes 3538944 | tf_op jit(solution)/shard_map/reduce_scatter | solution.py:334
  456.7 5.5 copy-start.5
  460.6 5.3 copy-start.45
  462.2 3.7 copy-start.22
  469.1 1.7 copy-start.11
  473.2 5.8 copy-start.20
  473.2 5.8 copy-start.23
  475.4 23.6 %all-to-all-start.2 = ((bf16[3,256,768]{1,0,2:T(4,128)(2,1)}), bf16[3,256,768]{1,0,2:T(4,128)(2,1)S(1)}, u32[]{:S(2)}, u32[]{:S(2)}) async-start(bf16[3,256,768]{1,0,2:T(4,128)(2,1)} %copy.87), calls=%async_computation.2 | async-start | bytes 3145728 | tf_op jit(solution)/shard_map/all_to_all | solution.py:290
  478.9 257.0 %reduce-scatter.13.cloned.1.call-start = ((), (), s32[]{:S(2)}) async-start(), calls=%async_computation.19 | async-start | bytes 7962624 | tf_op jit(solution)/shard_map/reduce_scatter | solution.py:335
  594.9 5.5 copy-start.3
  594.9 5.5 copy-start.30
  594.9 5.5 copy-start.32
  594.9 5.5 copy-start.37
  594.9 5.5 copy-start.39
  595.0 76.1 %all-to-all-start.3 = ((bf16[3,1024,3,192]{3,2,0,1:T(4,128)(2,1)}), bf16[3,1024,3,192]{3,2,0,1:T(4,128)(2,1)}, u32[]{:S(2)}, u32[]{:S(2)}) async-start(bf16[3,1024,3,192]{3,2,0,1:T(4,128)(2,1)} %copy.90), calls=%async_computation.3 | async-start | bytes 12582912 | tf_op jit(solution)/shard_map/all_to_all | solution.py:294
  600.4 263.8 %reduce-scatter.7.cloned.1.call-start = ((), (), s32[]{:S(2)}) async-start(), calls=%async_computation.16 | async-start | bytes 7962624 | tf_op jit(solution)/shard_map/reduce_scatter | solution.py:330
  708.9 1.8 copy-start.9
  716.0 314.4 %reduce-scatter.17.cloned.1.call-start = ((), (), s32[]{:S(2)}) async-start(), calls=%async_computation.21 | async-start | bytes 10616832 | tf_op jit(solution)/shard_map/reduce_scatter | solution.py:339
  725.9 470.4 %reduce-scatter.15.cloned.1.call-start = ((), (), s32[]{:S(2)}) async-start(), calls=%async_computation.20 | async-start | bytes 10616832 | tf_op jit(solution)/shard_map/reduce_scatter | solution.py:337
  735.8 559.3 %all-reduce.20.cloned.1.call-start = ((), (), s32[]{:S(2)}) async-start(), calls=%async_computation.22 | async-start | bytes 9633792 | tf_op jit(solution)/shard_map/psum | solution.py:342
  1198.4 61.2 %copy-start.12 = (f32[768,768]{1,0:T(8,128)S(1)}, f32[768,768]{1,0:T(8,128)}, u32[]{:S(2)}) copy-start(f32[768,768]{1,0:T(8,128)} %copy-done.10) | copy-start | bytes 7077892
  1295.1 4.0 copy-start.24
  1295.1 4.7 copy-start.19
  1295.1 5.6 copy-start.14
  1299.1 2.7 copy-start.13
  (8 other events, 7.2 us)
Sparse Core Ops, SparseCore 0:
  10.2 68.3 all-gather.7
  80.8 42.7 all-gather.11
  125.8 64.1 all-gather.13
  192.0 39.5 all-gather.9
  233.6 78.6 all-gather.15
  314.3 78.0 all-gather.17
  456.1 67.1 reduce-scatter.8
  526.8 73.4 reduce-scatter.10
  604.0 128.0 reduce-scatter.12
  736.1 128.0 reduce-scatter.6
  867.8 162.4 reduce-scatter.16
  1033.8 162.5 reduce-scatter.14
  1199.1 95.8 all-reduce.19
where the time goes:
time: 1320 us; the launch traced here: 1310 us
  waiting for transfers between devices  735 us (56%)
  matrix products  194 us (15%)
  local copies, waits for them, and re-layouts  132 us (10%)
  blocking collectives  109 us (8%)
  other arithmetic  102 us (8%)
  starting transfers between devices  18.8 us (1%)
  between operations  18.3 us (1%)
    reduce_scatter x1, waiting for transfers between devices, shards(): lax.psum_scatter(down_grad, 'dp', scatter_dimension=0, tiled=True)  166 us
    reduce_scatter x1, waiting for transfers between devices, shards(): lax.psum_scatter(up_grad, 'dp', scatter_dimension=0, tiled=True)  166 us
    reduce_scatter x1, waiting for transfers between devices, shards(): lax.psum_scatter(in_grad, 'dp', scatter_dimension=0, tiled=True)  128 us
    unnamed x2, blocking collectives  76.4 us
    all_gather x1, waiting for transfers between devices, shards(): lax.all_gather(mlp_down, 'dp', axis=0, tiled=True)  71.6 us
    all_to_all x1, waiting for transfers between devices, shards(): lax.all_to_all(head_back, 'seq', split_axis=1, concat_axis=3, tiled=True)  70.1 us
    dot_general x4, matrix products, back_dot(): lax.dot_general(gradient, weight, (((1,), (1,)), ((), ())), preferred_ele...  49.8 us
    unnamed x129, local copies, waits for them, and re-layouts  32.6 us
  transfers between devices with their start and end apart: 17, of which 11 were waited for; matrix products, arithmetic and copies ran while one was open for 27% of the time, Pallas kernels for 0%

commit v1 on v0

v1 whole, which is shorter than its diff:
```python
import math

import jax
import jax.numpy as jnp
from jax import lax
from jax.sharding import PartitionSpec as P

H = 12
HD = 64
EPS = 1e-05
NEG = -1e30
F32 = jnp.float32
BF16 = jnp.bfloat16
HIGHEST = lax.Precision.HIGHEST


def standardize(values):
    centred = values - jnp.mean(values, axis=-1, keepdims=True)
    inverse = lax.rsqrt(jnp.mean(centred * centred, axis=-1, keepdims=True) + EPS)
    return centred * inverse, inverse


def norm_back(gradient, normed, inverse):
    return inverse * (
        gradient
        - jnp.mean(gradient, axis=-1, keepdims=True)
        - normed * jnp.mean(gradient * normed, axis=-1, keepdims=True)
    )


def dot(left, right):
    return jnp.dot(left, right, preferred_element_type=F32)


def dot_bt(left, right):
    return lax.dot_general(left, right, (((1,), (1,)), ((), ())), preferred_element_type=F32)


def dot_at(left, right):
    return lax.dot_general(left, right, (((0,), (0,)), ((), ())), preferred_element_type=F32)


def gelu_exact(values):
    return jax.nn.gelu(values, approximate=False)


def seq_swap(value, mask):
    return lax.ppermute(value, "seq", [(s, s ^ mask) for s in range(lax.axis_size("seq"))])


def dp_swap(value):
    return lax.ppermute(value, "dp", [(d, d ^ 1) for d in range(lax.axis_size("dp"))])


def dp_shift(value, step):
    count = lax.axis_size("dp")
    outer = count // 2
    return lax.ppermute(
        value,
        "dp",
        [(((o + step) % outer) * 2 + i, o * 2 + i) for o in range(outer) for i in range(2)],
    )


def dp_gather(block):
    outer = lax.axis_size("dp") // 2
    me = lax.axis_index("dp")
    mine = [block] + [dp_shift(block, k) for k in range(1, outer)]
    theirs = [dp_swap(piece) for piece in mine]
    mine, theirs = jnp.stack(mine), jnp.stack(theirs)
    even = me % 2 == 0
    pairs = jnp.where(even, jnp.stack([mine, theirs], 1), jnp.stack([theirs, mine], 1))
    whole = lax.dynamic_slice_in_dim(
        jnp.concatenate([pairs, pairs], 0), outer - me // 2, outer, 0
    )
    return whole.reshape((-1,) + block.shape[1:])


def dp_reduce(blocks):
    outer = lax.axis_size("dp") // 2
    me = lax.axis_index("dp")
    o, i = me // 2, me % 2
    pairs = blocks.reshape((outer, 2) + blocks.shape[1:])
    away = lax.dynamic_index_in_dim(pairs, 1 - i, 1, keepdims=False).astype(BF16)
    here = lax.dynamic_index_in_dim(pairs, i, 1, keepdims=False).astype(F32)
    half = (here + dp_swap(away).astype(F32)).astype(BF16)
    total = lax.dynamic_index_in_dim(half, o, 0, keepdims=False).astype(F32)
    for k in range(1, outer):
        piece = lax.dynamic_index_in_dim(half, (o - k) % outer, 0, keepdims=False)
        total = total + dp_shift(piece, k).astype(F32)
    return total


def dp_all(value):
    count = lax.axis_size("dp")
    return lax.all_to_all(
        jnp.broadcast_to(value[None], (count,) + value.shape),
        "dp",
        split_axis=0,
        concat_axis=0,
        tiled=True,
    )


def dp_turn(value):
    return lax.all_to_all(value, "dp", split_axis=0, concat_axis=0, tiled=True)


def rotary_tables(positions):
    half_width = HD // 2
    frequency = jnp.exp(jnp.arange(half_width, dtype=F32) * (-math.log(10000.0) / half_width))
    angles = positions.astype(F32)[:, None] * frequency[None, :]
    return jnp.cos(angles), jnp.sin(angles)


def rotate(values, cosine, sine_table):
    half_width = cosine.shape[-1]
    front = values[..., :half_width]
    back = values[..., half_width:]
    cos_wide = cosine[:, None, :]
    sin_wide = sine_table[:, None, :]
    return jnp.concatenate(
        [front * cos_wide - back * sin_wide, back * cos_wide + front * sin_wide], axis=-1
    )


def masked_scores(queries, key_rows, clean):
    scores = jnp.einsum("qhd,khd->hqk", queries, key_rows, preferred_element_type=F32)
    scores = scores * HD ** (-0.5)
    visible = jnp.logical_or(jnp.logical_not(clean)[:, None], clean[None, :])
    return jnp.where(visible[None], scores, NEG)


def attend_forward(packed):
    queries, key_rows, values, clean = packed
    scores = masked_scores(queries, key_rows, clean)
    row_max = jnp.max(scores, axis=-1, keepdims=True)
    exponent = jnp.exp(scores - row_max)
    row_total = jnp.sum(exponent, axis=-1, keepdims=True)
    weights = (exponent / row_total).astype(BF16)
    mixed = jnp.einsum("hqk,khd->qhd", weights, values, preferred_element_type=F32)
    return mixed.astype(BF16), (row_max + jnp.log(row_total))[..., 0]


def attend_backward(packed):
    queries, key_rows, values, clean, log_total, mixed_grad = packed
    scores = masked_scores(queries, key_rows, clean)
    weights = jnp.exp(scores - log_total[..., None])
    weight_grad = jnp.einsum("qhd,khd->hqk", mixed_grad, values, preferred_element_type=F32)
    centre = jnp.sum(weights * weight_grad, axis=-1, keepdims=True)
    score_grad = (weights * (weight_grad - centre)).astype(BF16)
    scale = HD ** (-0.5)
    query_grad = jnp.einsum("hqk,khd->qhd", score_grad, key_rows, preferred_element_type=F32)
    key_grad = jnp.einsum("hqk,qhd->khd", score_grad, queries, preferred_element_type=F32)
    value_grad = jnp.einsum(
        "hqk,qhd->khd", weights.astype(BF16), mixed_grad, preferred_element_type=F32
    )
    return (
        (query_grad * scale).astype(BF16),
        (key_grad * scale).astype(BF16),
        value_grad.astype(BF16),
    )


def shards(
    tokens,
    prefix_len,
    timestep,
    norm_gain,
    norm_bias,
    proj_in,
    proj_in_bias,
    proj_out,
    proj_out_bias,
    time_table,
    ada_weight,
    ada_bias,
    mlp_up,
    mlp_up_bias,
    mlp_down,
    mlp_down_bias,
    out_grad,
):
    count, local_len, width = tokens.shape
    members = lax.axis_size("seq")
    ranks = lax.axis_size("dp")
    s = lax.axis_index("seq")
    d = lax.axis_index("dp")
    c = s % 2
    local_heads = H // members
    head_width = local_heads * HD
    local_rows = count * local_len
    order = [s ^ j for j in range(members)]

    vectors = [
        norm_gain,
        norm_bias,
        proj_in_bias,
        proj_out_bias,
        ada_bias,
        mlp_up_bias,
        mlp_down_bias,
        timestep,
    ]
    packed = dp_all(jnp.concatenate([v.astype(F32) for v in vectors]))
    unpacked, start = [], 0
    for v in vectors:
        unpacked.append(packed[:, start : start + v.shape[0]].reshape(-1))
        start += v.shape[0]
    gain, bias, in_bias, out_bias, ada_bias_full, up_bias, down_bias, steps = unpacked
    steps = steps.astype(jnp.int32).reshape(ranks, count)

    tok_x = seq_swap(tokens, 2)
    tok_c = seq_swap(tokens, 1)
    tok_d = seq_swap(tok_x, 1)
    og_c = seq_swap(out_grad, 1)

    in_local = lax.dynamic_slice_in_dim(
        proj_in.reshape(-1, 3, width), s * head_width, head_width, 2
    ).reshape(-1, 3 * head_width)
    in_w = dp_gather(in_local)
    in_b = lax.dynamic_slice_in_dim(
        in_bias.reshape(3, width), s * head_width, head_width, 1
    ).reshape(-1)
    half_out = width // 2
    out_half = dp_gather(lax.dynamic_slice_in_dim(proj_out, c * half_out, half_out, 1))
    out_other = seq_swap(out_half, 1)
    out_w = jnp.where(
        c == 0,
        jnp.concatenate([out_half, out_other], 1),
        jnp.concatenate([out_other, out_half], 1),
    )
    out_blocks = out_w.reshape(members, head_width, width)
    out_rel = jnp.concatenate([lax.dynamic_index_in_dim(out_blocks, p, 0, False) for p in order], 0)
    own_ff = mlp_down.shape[0]
    half_ff = own_ff // 2
    up_w = dp_gather(
        lax.dynamic_index_in_dim(mlp_up.reshape(-1, ranks, 2, half_ff), c, 2, False).reshape(
            -1, ranks * half_ff
        )
    )
    down_w = dp_gather(lax.dynamic_slice_in_dim(mlp_down, c * half_ff, half_ff, 0))
    up_b = lax.dynamic_index_in_dim(up_bias.reshape(ranks, 2, half_ff), c, 1, False).reshape(-1)

    group = jnp.stack([tokens, tok_c, tok_x, tok_d], axis=1)
    group_rows = group.astype(F32).reshape(-1, width)
    normed_group, _ = standardize(group_rows)
    attn_input = (normed_group * gain + bias).astype(BF16)
    projected = (dot(attn_input, in_w) + in_b).reshape(count, -1, 3, local_heads, HD)
    offsets = jnp.arange(local_len, dtype=jnp.int32)
    positions = jnp.concatenate([p * local_len + offsets for p in order])
    cosine, sine_table = rotary_tables(positions)
    queries = rotate(projected[:, :, 0], cosine, sine_table).astype(BF16)
    key_rows = rotate(projected[:, :, 1], cosine, sine_table).astype(BF16)
    values = projected[:, :, 2].astype(BF16)
    clean_group = positions[None, :] < prefix_len[:, None]
    mixed_heads, log_total = lax.map(
        attend_forward, (queries, key_rows, values, clean_group)
    )
    mixed_heads = mixed_heads.reshape(count, members, local_len, head_width)
    mixed_parts = [mixed_heads[:, 0]] + [
        seq_swap(mixed_heads[:, j], j) for j in range(1, members)
    ]
    mixed = jnp.concatenate(mixed_parts, axis=-1).reshape(local_rows, width)

    table_rows = time_table.shape[0]
    wanted = jnp.concatenate([steps, jnp.zeros((ranks, 1), jnp.int32)], axis=1).reshape(-1)
    kinds = count + 1
    selector = (
        wanted[:, None] == d * table_rows + jnp.arange(table_rows, dtype=jnp.int32)[None, :]
    )
    chosen = dot(selector.astype(BF16), time_table).astype(BF16)
    own_cols = width // ranks
    chosen = dp_turn(
        chosen.reshape(ranks * kinds, ranks, own_cols).transpose(1, 0, 2)
    )
    embedded = jnp.sum(chosen.astype(F32), axis=0)
    activated = jax.nn.silu(embedded).astype(BF16)
    mod_parts = dp_turn(dot(activated, ada_weight).reshape(ranks, kinds, 3 * width))
    modulation = jnp.sum(mod_parts, axis=0) + ada_bias_full

    def token_mod(place, part):
        rows = modulation[:, part * width : (part + 1) * width]
        clean = (place * local_len + offsets)[None, :] < prefix_len[:, None]
        return jnp.where(clean[:, :, None], rows[count][None, None], rows[:count, None]).reshape(
            -1, width
        )

    inputs = tokens.astype(F32).reshape(-1, width)
    residual_one = inputs + (dot(mixed, out_rel) + out_bias)
    shift_mod, scale_mod, gate_mod = (token_mod(s, part) for part in range(3))
    gate_other = token_mod(s ^ 1, 2)
    normed_two, inverse_two = standardize(residual_one)
    mlp_own = (normed_two * (1.0 + scale_mod) + shift_mod).astype(BF16)
    mlp_other = seq_swap(mlp_own, 1)
    mlp_input = jnp.concatenate([mlp_own, mlp_other], 0)
    incoming = out_grad.astype(F32).reshape(-1, width)
    branch_grad_own = (incoming * gate_mod).astype(BF16)
    branch_grad = jnp.concatenate(
        [branch_grad_own, (og_c.astype(F32).reshape(-1, width) * gate_other).astype(BF16)], 0
    )
    pre_act = dot(mlp_input, up_w) + up_b
    hidden = gelu_exact(pre_act).astype(BF16)
    branch_part = dot(hidden, down_w)
    act_grad = dot_bt(branch_grad, down_w)
    pre_grad = jax.vjp(gelu_exact, pre_act)[1](act_grad)[0].astype(BF16)
    input_part = dot_bt(pre_grad, up_w)
    down_grad = dot_at(hidden, branch_grad)
    up_grad = dot_at(mlp_input, pre_grad)
    branch = (
        branch_part[:local_rows]
        + seq_swap(branch_part[local_rows:].astype(BF16), 1).astype(F32)
        + down_bias
    )
    input_two = input_part[:local_rows] + seq_swap(
        input_part[local_rows:].astype(BF16), 1
    ).astype(F32)
    block_out = (residual_one + gate_mod * branch).astype(BF16).reshape(tokens.shape)

    resid_grad = incoming + norm_back(input_two * (1.0 + scale_mod), normed_two, inverse_two)
    attn_grad = resid_grad.astype(BF16)
    mixed_grad = dot_bt(attn_grad, out_rel).astype(BF16).reshape(count, local_len, members, -1)
    grad_parts = [mixed_grad[:, :, 0]] + [
        seq_swap(mixed_grad[:, :, j], j) for j in range(1, members)
    ]
    head_grad = jnp.stack(grad_parts, axis=1).reshape(count, -1, local_heads, HD)
    out_rel_grad = dot_at(mixed, attn_grad).reshape(members, head_width, width)

    mod_grad = (
        jnp.concatenate([input_two, input_two * normed_two, incoming * branch], axis=-1)
        .astype(BF16)
        .reshape(count, local_len, 3 * width)
    )
    clean_own = (s * local_len + offsets)[None, :] < prefix_len[:, None]
    noisy_rows = jnp.einsum(
        "sl,slj->sj",
        jnp.logical_not(clean_own).astype(BF16),
        mod_grad,
        preferred_element_type=F32,
    )
    clean_row = jnp.einsum(
        "sl,slj->j", clean_own.astype(BF16), mod_grad, preferred_element_type=F32
    )
    row_grad = jnp.concatenate([noisy_rows, clean_row[None]], axis=0)
    row_grad = row_grad + seq_swap(row_grad, 1)
    row_grad = row_grad + seq_swap(row_grad, 2)
    all_rows = dp_all(row_grad).reshape(ranks * kinds, 3 * width)
    ada_bias_grad = lax.dynamic_slice_in_dim(
        jnp.sum(all_rows, axis=0), d * ada_bias.shape[0], ada_bias.shape[0], 0
    )
    ada_grad = lax.dot_general(
        activated.astype(F32),
        all_rows,
        (((0,), (0,)), ((), ())),
        precision=HIGHEST,
        preferred_element_type=F32,
    )
    act_rows_grad = lax.dot_general(
        all_rows,
        ada_weight.astype(F32),
        (((1,), (1,)), ((), ())),
        precision=HIGHEST,
        preferred_element_type=F32,
    )
    embed_grad = jax.vjp(jax.nn.silu, embedded)[1](act_rows_grad)[0]
    embed_all = dp_all(embed_grad).transpose(1, 0, 2).reshape(ranks * kinds, width)
    table_grad = lax.dot_general(
        selector.astype(F32),
        embed_all,
        (((0,), (0,)), ((), ())),
        precision=HIGHEST,
        preferred_element_type=F32,
    )

    query_grad, key_grad, value_grad = lax.map(
        attend_backward, (queries, key_rows, values, clean_group, log_total, head_grad)
    )
    proj_grad = (
        jnp.stack(
            [
                rotate(query_grad.astype(F32), cosine, -sine_table),
                rotate(key_grad.astype(F32), cosine, -sine_table),
                value_grad.astype(F32),
            ],
            axis=2,
        )
        .astype(BF16)
        .reshape(-1, 3 * head_width)
    )
    in_grad = dot_at(attn_input, proj_grad)
    normed_part = dot_bt(proj_grad, in_w)
    gain_grad = jnp.sum(normed_part * normed_group, axis=0)
    bias_grad = jnp.sum(normed_part, axis=0)
    parts = normed_part.reshape(count, members, local_len, width)
    got = seq_swap(jnp.stack([parts[:, 1], parts[:, 3]]).astype(BF16), 1).astype(F32)
    mine = parts[:, 0] + got[0]
    across = (parts[:, 2] + got[1]).astype(BF16)
    normed_grad = (mine + seq_swap(across, 2).astype(F32)).reshape(-1, width)
    normed_own, inverse_own = standardize(inputs)
    tokens_grad = (resid_grad + norm_back(normed_grad * gain, normed_own, inverse_own)).reshape(
        tokens.shape
    )

    down_red = dp_reduce(down_grad.reshape(ranks, half_ff, width)).astype(BF16)
    up_red = dp_reduce(up_grad.reshape(ranks, -1, ranks * half_ff)).astype(BF16)
    out_grad_w = jnp.concatenate(
        [lax.dynamic_index_in_dim(out_rel_grad, p, 0, False) for p in order], 0
    )
    out_away = lax.dynamic_slice_in_dim(out_grad_w, (1 - c) * half_out, half_out, 1).astype(BF16)
    out_here = lax.dynamic_slice_in_dim(out_grad_w, c * half_out, half_out, 1)
    out_sum = out_here + seq_swap(out_away, 1).astype(F32)
    out_red = dp_reduce(out_sum.reshape(ranks, -1, half_out)).astype(BF16)
    in_red = dp_reduce(in_grad.reshape(ranks, -1, 3 * head_width)).astype(BF16)

    def both(value, axis):
        total = value.astype(F32) + seq_swap(value, 2).astype(F32)
        other = seq_swap(total, 1)
        return jnp.where(
            c == 0, jnp.stack([total, other], axis), jnp.stack([other, total], axis)
        )

    down_final = both(down_red, 0).reshape(mlp_down.shape)
    up_final = both(up_red.reshape(-1, ranks, half_ff), 2).reshape(mlp_up.shape)
    out_final = both(out_red, 1).reshape(proj_out.shape)
    in_x = seq_swap(in_red, 2)
    in_pair = jnp.stack([in_red, in_x])
    in_pair_c = seq_swap(in_pair, 1)
    in_rel = jnp.stack([in_red, in_pair_c[0], in_x, in_pair_c[1]])
    in_final = (
        jnp.stack([lax.dynamic_index_in_dim(in_rel, p, 0, False) for p in order])
        .reshape(members, -1, 3, head_width)
        .transpose(1, 2, 0, 3)
        .reshape(proj_in.shape)
        .astype(F32)
    )

    in_bias_grad = lax.dynamic_update_slice_in_dim(
        jnp.zeros((3, width), F32),
        jnp.sum(proj_grad, axis=0, dtype=F32).reshape(3, head_width),
        s * head_width,
        1,
    ).reshape(-1)
    up_bias_grad = lax.dynamic_update_slice_in_dim(
        jnp.zeros((ranks, 2, half_ff), F32),
        jnp.sum(pre_grad, axis=0, dtype=F32).reshape(ranks, 1, half_ff),
        c,
        1,
    ).reshape(-1)
    down_bias_grad = jnp.sum(branch_grad_own, axis=0, dtype=F32)
    out_bias_grad = jnp.sum(attn_grad, axis=0, dtype=F32)
    vector_grads = [gain_grad, bias_grad, in_bias_grad, out_bias_grad, up_bias_grad, down_bias_grad]
    vec = jnp.concatenate([g.reshape(ranks, -1) for g in vector_grads], axis=1)
    vec = jnp.sum(dp_turn(vec), axis=0)
    vec = vec + seq_swap(vec, 1)
    vec = vec + seq_swap(vec, 2)
    finals, start = [], 0
    for g in vector_grads:
        size = g.shape[0] // ranks
        finals.append(vec[start : start + size])
        start += size
    gain_f, bias_f, in_bias_f, out_bias_f, up_bias_f, down_bias_f = finals
    return (
        block_out,
        tokens_grad,
        gain_f,
        bias_f,
        in_final,
        in_bias_f,
        out_final,
        out_bias_f,
        table_grad,
        ada_grad,
        ada_bias_grad,
        up_final,
        up_bias_f,
        down_final,
        down_bias_f,
    )


def solution(mesh):
    rows = P("dp", None)
    vector = P("dp")
    stream = P("dp", "seq", None)
    in_specs = (
        stream,
        vector,
        vector,
        vector,
        vector,
        rows,
        vector,
        rows,
        vector,
        rows,
        rows,
        vector,
        rows,
        vector,
        rows,
        vector,
        stream,
    )
    out_specs = (
        stream,
        stream,
        vector,
        vector,
        rows,
        vector,
        rows,
        vector,
        rows,
        rows,
        vector,
        rows,
        vector,
        rows,
        vector,
    )
    return jax.shard_map(shards, mesh=mesh, in_specs=in_specs, out_specs=out_specs, check_vma=False)
```

time: 1320 us -> 715 us (0.54)
  waiting for transfers between devices: 735 us -> 81.6 us
  blocking collectives: 109 us -> 0 us
  starting transfers between devices: 18.8 us -> 107 us
  other arithmetic: 102 us -> 162 us
  local copies, waits for them, and re-layouts: 132 us -> 148 us
  between operations: 18.3 us -> 2.78 us
    reduce_scatter x6 -> x0, waiting for transfers between devices: 460 us -> none  [the longest x1 166 us: shards(): lax.psum_scatter(down_grad, 'dp', scatter_dimension=0, tiled=True)]
    all_gather x6 -> x0, waiting for transfers between devices: 132 us -> none  [the longest x1 71.6 us: shards(): lax.all_gather(mlp_down, 'dp', axis=0, tiled=True)]
    all_to_all x4 -> x6, waiting for transfers between devices: 107 us -> 0.02 us  [the longest x3 0.01 us: dp_all(): lax.all_to_all(jnp.broadcast_to(value[None], (count,) + value.shape), 'dp...]
    ppermute x0 -> x73, waiting for transfers between devices: none -> 81.6 us  [the longest x24 38.6 us: dp_shift(): lax.ppermute(value, 'dp', [((o + step) % outer * 2 + i, o * 2 + i) for o...]
    ppermute x0 -> x73, starting transfers between devices: none -> 80.6 us  [the longest x24 42.4 us: dp_shift(): lax.ppermute(value, 'dp', [((o + step) % outer * 2 + i, o * 2 + i) for o...]
    unnamed x2 -> x0, blocking collectives: 76.4 us -> none
    psum x1 -> x0, waiting for transfers between devices: 31.6 us -> none  [shards(): lax.psum((red_gain, red_bias, red_in, red_in_bias, red_out, red_out_bias,...]
    all_gather x1 -> x0, blocking collectives: 26 us -> none  [shards(): lax.all_gather(mlp_up_bias, 'dp', axis=0, tiled=True)]
  transfers between devices with their start and end apart: 17 -> 79, of which waited for: 11 -> 17; matrix products, arithmetic and copies ran while one was open for 27% -> 65% of each run, Pallas kernels for 0% -> 0%
where the time goes in v1:
time: 715 us; the launch traced here: 704 us
  matrix products  202 us (28%)
  other arithmetic  162 us (23%)
  local copies, waits for them, and re-layouts  148 us (21%)
  starting transfers between devices  107 us (15%)
  waiting for transfers between devices  81.6 us (11%)
    ppermute x24, starting transfers between devices, dp_shift(): lax.ppermute(value, 'dp', [((o + step) % outer * 2 + i, o * 2 + i) for o...  42.4 us
    dot_general x6, matrix products, dot(): return jnp.dot(left, right, preferred_element_type=F32)  40.6 us
    ppermute x24, waiting for transfers between devices, dp_shift(): lax.ppermute(value, 'dp', [((o + step) % outer * 2 + i, o * 2 + i) for o...  38.6 us
    dot_general x4, matrix products, dot_bt(): lax.dot_general(left, right, (((1,), (1,)), ((), ())), preferred_element_...  30.2 us
    dot_general x3, matrix products, attend_forward(): jnp.einsum('hqk,khd->qhd', weights, values, preferred_element_type=F32)  27.7 us
    ppermute x29, waiting for transfers between devices, seq_swap(): lax.ppermute(value, 'seq', [(s, s ^ mask) for s in range(lax.axis_size('s...  26.5 us
    dot_general x3, matrix products, attend_backward(): jnp.einsum('qhd,khd->hqk', mixed_grad, values, preferred_element_type=F32)  24.7 us
    ppermute x20, starting transfers between devices, dp_swap(): lax.ppermute(value, 'dp', [(d, d ^ 1) for d in range(lax.axis_size('dp'))])  24.1 us
  transfers between devices with their start and end apart: 79, of which 17 were waited for; matrix products, arithmetic and copies ran while one was open for 65% of the time, Pallas kernels for 0%

profile of v1, /device:TPU:0, one launch (start us, length us, event | category | flops | bytes accessed | tf_op | source)
XLA Modules:
  0.0 704.4 jit_solution(2359735466230700246)
XLA Ops:
  3.4 5.0 collective-permute-start.3
  15.6 4.8 concatenate.94
  21.0 4.0 all-to-all-start
  44.3 4.5 all-to-all-start.1
  70.9 5.1 all-to-all-start.2
  80.9 12.2 %collective-permute-done.23 = bf16[96,1536]{1,0:T(8,128)(2,1)} collective-permute-done((bf16[96,1536]{1,0:T(8,128)(2,1)}, bf16[96,1536]{1,0:T(8,128)(2,1)}, u32[]{:S(2)}, u32[]{:S(2)}) %collective-permute-start.23) | collective-permute-done | bytes 294944 | tf_op jit(solution)/shard_map/ppermute | solution.py:58
  101.0 12.6 %collective-permute-done.30 = bf16[192,768]{1,0:T(8,128)(2,1)} collective-permute-done((bf16[192,768]{1,0:T(8,128)(2,1)}, bf16[192,768]{1,0:T(8,128)(2,1)}, u32[]{:S(2)}, u32[]{:S(2)}) %collective-permute-start.30) | collective-permute-done | bytes 294944 | tf_op jit(solution)/shard_map/ppermute | solution.py:58
  123.2 5.9 collective-permute-done.28
  139.7 3.8 add_convert_fusion.2
  143.5 5.1 convolution_add_fusion.1
  148.6 12.2 %reshape.743 = f32[3,1024,3,3,64]{1,0,4,3,2:T(4,128)} reshape(f32[3072,576]{0,1:T(8,128)} %convolution_add_fusion.1) | data formatting | bytes 14155776 | tf_op jit(solution)/shard_map/reshape | solution.py:249
  160.8 4.3 slice_bitcast_fusion
  175.2 71.3 %while.26 = (s32[]{:T(128)}, bf16[3,1024,3,64]{1,3,2,0:T(8,128)(2,1)}, f32[3,3,1024]{2,1,0:T(4,128)}, bf16[3,1024,3,64]{1,3,2,0:T(8,128)(2,1)}, pred[3,1024]{1,0...) while((s32[]{:T(128)}, ...), condition=%wide.region_5.6_spmd, body=%wide.region_2.5_spmd.sunk | while | flops 844298240 | bytes 43627096 | solution.py:257
  176.1 5.9 fusion.221
  182.1 7.3 %fusion.222 = f32[3,1024]{1,0:T(4,128)S(1)} fusion(f32[3,1024,1024]{1,2,0:T(8,128)} %get-tuple-element.483, f32[3,1024]{1,0:T(4,128)S(1)} %get-tuple-element.484, pred[1024,1024]{0,1:T(8,128)(4,1)S(1)} %broadcast_or_fusion.4), kind=kLoop, calls=%fused_computation.4.clone.1 | loop fusion | flops 12579840 | bytes 13656064 | tf_op jit(solution)/shard_map/while/body/eval_jaxpr/reduce_sum | solution.py:139
  190.0 9.2 %fusion.223 = bf16[3,1024,3,64]{1,3,2,0:T(8,128)(2,1)} fusion(bf16[3,1024,3,64]{1,3,2,0:T(8,128)(2,1)} %get-tuple-element.506, s32[]{:T(128)} %get-tuple-element.505, f32[3,1024,1024]{1,2,0:T(8,128)} %get-tuple-element.483, f32[3,1024]{1,0:T(4,128)S(1)} %fusion.222, f32[3,1024]{1,0:T(4,128)S(1)} %get-tuple-element.484, ...), kind=kOutput, calls=%fused_computation.9.clone.1 | convolution fusion | flops 418578432 | bytes 14443520 | tf_op jit(solution)/shard_map/while/body/eval_jaxpr/hqk,khd->qhd/dot_general | solution.py:141
  199.8 5.9 fusion.221
  205.7 7.3 %fusion.222 = f32[3,1024]{1,0:T(4,128)S(1)} fusion(f32[3,1024,1024]{1,2,0:T(8,128)} %get-tuple-element.483, f32[3,1024]{1,0:T(4,128)S(1)} %get-tuple-element.484, pred[1024,1024]{0,1:T(8,128)(4,1)S(1)} %broadcast_or_fusion.4), kind=kLoop, calls=%fused_computation.4.clone.1 | loop fusion | flops 12579840 | bytes 13656064 | tf_op jit(solution)/shard_map/while/body/eval_jaxpr/reduce_sum | solution.py:139
  213.6 9.2 %fusion.223 = bf16[3,1024,3,64]{1,3,2,0:T(8,128)(2,1)} fusion(bf16[3,1024,3,64]{1,3,2,0:T(8,128)(2,1)} %get-tuple-element.506, s32[]{:T(128)} %get-tuple-element.505, f32[3,1024,1024]{1,2,0:T(8,128)} %get-tuple-element.483, f32[3,1024]{1,0:T(4,128)S(1)} %fusion.222, f32[3,1024]{1,0:T(4,128)S(1)} %get-tuple-element.484, ...), kind=kOutput, calls=%fused_computation.9.clone.1 | convolution fusion | flops 418578432 | bytes 14443520 | tf_op jit(solution)/shard_map/while/body/eval_jaxpr/hqk,khd->qhd/dot_general | solution.py:141
  223.4 5.9 fusion.221
  229.4 7.3 %fusion.222 = f32[3,1024]{1,0:T(4,128)S(1)} fusion(f32[3,1024,1024]{1,2,0:T(8,128)} %get-tuple-element.483, f32[3,1024]{1,0:T(4,128)S(1)} %get-tuple-element.484, pred[1024,1024]{0,1:T(8,128)(4,1)S(1)} %broadcast_or_fusion.4), kind=kLoop, calls=%fused_computation.4.clone.1 | loop fusion | flops 12579840 | bytes 13656064 | tf_op jit(solution)/shard_map/while/body/eval_jaxpr/reduce_sum | solution.py:139
  237.3 9.2 %fusion.223 = bf16[3,1024,3,64]{1,3,2,0:T(8,128)(2,1)} fusion(bf16[3,1024,3,64]{1,3,2,0:T(8,128)(2,1)} %get-tuple-element.506, s32[]{:T(128)} %get-tuple-element.505, f32[3,1024,1024]{1,2,0:T(8,128)} %get-tuple-element.483, f32[3,1024]{1,0:T(4,128)S(1)} %fusion.222, f32[3,1024]{1,0:T(4,128)S(1)} %get-tuple-element.484, ...), kind=kOutput, calls=%fused_computation.9.clone.1 | convolution fusion | flops 418578432 | bytes 14443520 | tf_op jit(solution)/shard_map/while/body/eval_jaxpr/hqk,khd->qhd/dot_general | solution.py:141
  246.5 3.9 reshape.744
  250.4 4.3 fusion.165
  261.1 3.9 collective-permute-done.11
  266.6 3.4 collective-permute-done.12
  273.9 5.0 fusion.72
  289.7 27.4 %multiply_convert_fusion.1 = (bf16[1536,1536]{1,0:T(8,128)(2,1)S(1)}, f32[1536,1536]{1,0:T(8,128)}, f32[1536,1536]{1,0:T(8,128)}) fusion(f32[1536]{0:T(1024)S(1)} %copy-done.100, bf16[768,1536]{1,0:T(8,128)(2,1)} %bitcast.512, bf16[768,768]{1,0:T(8,128)(2,1)} %collective-permute-done.21, bf16[768,768]{1,0:T(8,128)(2,1)} %get-tuple-element.374), kind=kOutput, calls=%fused_computation.75 | convolution fusion | flops 3784310784 | bytes 28317696 | tf_op jit(solution)/shard_map/dot_general | solution.py:32
  317.2 3.9 fusion.104
  325.7 13.1 %convert_reduce_fusion = (f32[1536]{0:T(1024)S(1)}, bf16[1536,1536]{1,0:T(8,128)(2,1)}) fusion(f32[1536,1536]{1,0:T(8,128)} %get-tuple-element.282, f32[1536,1536]{1,0:T(8,128)} %get-tuple-element.377, bf16[1536,768]{1,0:T(8,128)(2,1)S(1)} %bitcast.514, bf16[768,768]{1,0:T(8,128)(2,1)S(1)} %copy-done.43, bf16[768,768]{1,0:T(8,128)(2,1)S(1)} %copy-done.42), kind=kOutput, calls=%fused_computation.71 | convolution fusion | flops 3666344448 | bytes 28317696 | tf_op jit(solution)/shard_map/dot_general | solution.py:36
  338.8 6.4 fusion.174
  345.2 7.2 %fusion.105 = f32[768,1536]{1,0:T(8,128)S(1)} fusion(bf16[1536,1536]{1,0:T(8,128)(2,1)S(1)} %copy-done.110, bf16[768,768]{1,0:T(8,128)(2,1)} %collective-permute-done.21, bf16[768,768]{1,0:T(8,128)(2,1)} %get-tuple-element.374), kind=kOutput, calls=%fused_computation.200 | convolution fusion | flops 3628597248 | bytes 11796480 | tf_op jit(solution)/shard_map/dot_general | solution.py:40
  355.9 5.7 fusion.173
  369.6 4.3 collective-permute-start.69
  374.0 7.4 %collective-permute-done.61 = bf16[4,96,1536]{2,1,0:T(8,128)(2,1)} collective-permute-done((bf16[4,96,1536]{2,1,0:T(8,128)(2,1)}, bf16[4,96,1536]{2,1,0:T(8,128)(2,1)}, u32[]{:S(2)}, u32[]{:S(2)}) %collective-permute-start.61) | collective-permute-done | bytes 1179680 | tf_op jit(solution)/shard_map/ppermute | solution.py:52
  392.3 5.0 convert_reduce_fusion.5
  404.6 3.8 fusion.164
  426.6 7.2 %collective-permute-done.63 = bf16[96,1536]{1,0:T(8,128)(2,1)S(1)} collective-permute-done((bf16[96,1536]{1,0:T(8,128)(2,1)S(1)}, bf16[96,1536]{1,0:T(8,128)(2,1)S(1)}, u32[]{:S(2)}, u32[]{:S(2)}) %collective-permute-start.63) | collective-permute-done | bytes 294944 | tf_op jit(solution)/shard_map/ppermute | solution.py:58
  439.0 4.0 collective-permute-done.41
  449.3 86.1 %while.27 = (s32[]{:T(128)}, bf16[3,1024,3,64]{1,3,2,0:T(8,128)(2,1)}, bf16[3,1024,3,64]{1,3,2,0:T(8,128)(2,1)}, bf16[3,1024,3,64]{1,3,2,0:T(8,128)(2,1)}, bf16[...) while((s32[]{:T(128)}, ...), condition=%wide.region_16.17_spmd, body=%wide.region_14.16_spmd.sunk | while | flops 2062481408 | bytes 102595696 | solution.py:375
  452.6 8.2 %multiply_reduce_fusion.7 = (f32[3,1024]{1,0:T(4,128)S(1)}, f32[3,1024,1024]{1,2,0:T(8,128)}) fusion(f32[3,1024,1024]{1,2,0:T(8,128)S(1)} %fusion.232, f32[3,1024]{1,0:T(4,128)S(1)} %dynamic-slice_bitcast_fusion.22, pred[1024,1024]{0,1:T(8,128)(4,1)S(1)} %broadcast_or_fusion.5, bf16[3,1024,3,64]{1,3,2,0:T(8,128)(2,1)} %get-tuple-element.552, ...), kind=kOutput, calls=%fused_computation.24.clone.1 | convolution fusion | flops 418378752 | bytes 27026432 | tf_op jit(solution)/shard_map/while/body/eval_jaxpr/qhd,khd->hqk/dot_general | solution.py:149
  460.9 6.9 multiply_convert_fusion.7
  472.6 5.4 fusion.235
  481.1 8.2 %multiply_reduce_fusion.7 = (f32[3,1024]{1,0:T(4,128)S(1)}, f32[3,1024,1024]{1,2,0:T(8,128)}) fusion(f32[3,1024,1024]{1,2,0:T(8,128)S(1)} %fusion.232, f32[3,1024]{1,0:T(4,128)S(1)} %dynamic-slice_bitcast_fusion.22, pred[1024,1024]{0,1:T(8,128)(4,1)S(1)} %broadcast_or_fusion.5, bf16[3,1024,3,64]{1,3,2,0:T(8,128)(2,1)} %get-tuple-element.552, ...), kind=kOutput, calls=%fused_computation.24.clone.1 | convolution fusion | flops 418378752 | bytes 27026432 | tf_op jit(solution)/shard_map/while/body/eval_jaxpr/qhd,khd->hqk/dot_general | solution.py:149
  489.3 6.9 multiply_convert_fusion.7
  501.1 5.4 fusion.235
  509.6 8.2 %multiply_reduce_fusion.7 = (f32[3,1024]{1,0:T(4,128)S(1)}, f32[3,1024,1024]{1,2,0:T(8,128)}) fusion(f32[3,1024,1024]{1,2,0:T(8,128)S(1)} %fusion.232, f32[3,1024]{1,0:T(4,128)S(1)} %dynamic-slice_bitcast_fusion.22, pred[1024,1024]{0,1:T(8,128)(4,1)S(1)} %broadcast_or_fusion.5, bf16[3,1024,3,64]{1,3,2,0:T(8,128)(2,1)} %get-tuple-element.552, ...), kind=kOutput, calls=%fused_computation.24.clone.1 | convolution fusion | flops 418378752 | bytes 27026432 | tf_op jit(solution)/shard_map/while/body/eval_jaxpr/qhd,khd->hqk/dot_general | solution.py:149
  517.9 6.9 multiply_convert_fusion.7
  529.6 5.4 fusion.235
  543.9 6.0 convert_reduce_fusion.1
  549.9 10.4 %reshape.779 = bf16[3072,576,1,1]{0,1,2,3:T(8,128)(2,1)} reshape(bf16[3,1024,3,3,64]{1,0,4,3,2:T(4,128)(2,1)} %get-tuple-element.279) | data formatting | bytes 7077888 | tf_op jit(solution)/shard_map/convert_element_type | solution.py:387
  560.4 4.8 copy.326
  565.3 9.5 %fusion.161 = (f32[768]{0:T(1024)S(1)}, f32[768]{0:T(1024)S(1)}, bf16[3072,768]{1,0:T(8,128)(2,1)}, f32[3072,768]{1,0:T(8,128)}) fusion(f32[3072]{0:T(1024)S(1)} %bitcast.570, f32[3072]{0:T(1024)S(1)} %bitcast.571, bf16[3,1,256,768]{3,2,1,0:T(8,128)(2,1)} %bitcast.22, bf16[3,1,256,768]{3,2,1,0:T(8,128)(2,1)S(1)} %bitcast.491, ...), kind=kOutput, calls=%fused_computation.367 | convolution fusion | flops 2746219008 | bytes 23334912 | tf_op jit(solution)/shard_map/dot_general | solution.py:36
  574.8 6.6 copy.300
  586.1 6.8 fusion.66
  597.7 4.6 all-to-all-start.4
  620.8 4.5 all-to-all-start.5
  631.6 3.8 collective-permute-start.47
  639.5 4.3 collective-permute-start.54
  643.8 4.0 collective-permute-done.48
  661.4 4.7 fusion.78
  685.9 8.5 %collective-permute-done.43 = bf16[3,256,768]{2,1,0:T(8,128)(2,1)} collective-permute-done((bf16[3,256,768]{2,1,0:T(8,128)(2,1)}, bf16[3,256,768]{2,1,0:T(8,128)(2,1)}, u32[]{:S(2)}, u32[]{:S(2)}) %collective-permute-start.43) | collective-permute-done | bytes 1179680 | tf_op jit(solution)/shard_map/ppermute | solution.py:48
  694.4 5.1 multiply_reduce_fusion.5
  699.5 4.6 fusion.87
  (627 shorter events, 287.6 us)
Async XLA Ops:
  3.4 47.0 %collective-permute-start.3 = (bf16[96,576]{0,1:T(8,128)(2,1)}, bf16[96,576]{0,1:T(8,128)(2,1)}, u32[]{:S(2)}, u32[]{:S(2)}) collective-permute-start(bf16[96,576]{0,1:T(8,128)(2,1)} %bitcast.25), channel_id=1, source_target_pairs={{8,0},{12,4},{16,8},{20,12},{24,16},{28,20},{0,24},{4,28},{9,1},{1... | collective-permute-start | bytes 331784 | tf_op jit(solution)/shard_map/ppermute | solution.py:58
  8.4 44.0 %collective-permute-start.4 = (bf16[96,576]{0,1:T(8,128)(2,1)}, bf16[96,576]{0,1:T(8,128)(2,1)}, u32[]{:S(2)}, u32[]{:S(2)}) collective-permute-start(bf16[96,576]{0,1:T(8,128)(2,1)} %bitcast.25), channel_id=1, source_target_pairs={{16,0},{20,4},{24,8},{28,12},{0,16},{4,20},{8,24},{12,28},{17,1},{... | collective-permute-start | bytes 331784 | tf_op jit(solution)/shard_map/ppermute | solution.py:58
  10.0 26.1 %collective-permute-start.13 = (bf16[96,384]{1,0:T(8,128)(2,1)}, bf16[96,384]{1,0:T(8,128)(2,1)}, u32[]{:S(2)}, u32[]{:S(2)}) collective-permute-start(bf16[96,384]{1,0:T(8,128)(2,1)} %constant_dynamic-slice_fusion.7), channel_id=1, source_target_pairs={{8,0},{12,4},{16,8},{20,12},{24,16},{28,20},{0,24},{4,28},{9,1},{1... | collective-permute-start | bytes 221192 | tf_op jit(solution)/shard_map/ppermute | solution.py:58
  10.4 27.8 %collective-permute-start.14 = (bf16[96,384]{1,0:T(8,128)(2,1)}, bf16[96,384]{1,0:T(8,128)(2,1)}, u32[]{:S(2)}, u32[]{:S(2)}) collective-permute-start(bf16[96,384]{1,0:T(8,128)(2,1)} %constant_dynamic-slice_fusion.7), channel_id=1, source_target_pairs={{16,0},{20,4},{24,8},{28,12},{0,16},{4,20},{8,24},{12,28},{17,1},{... | collective-permute-start | bytes 221192 | tf_op jit(solution)/shard_map/ppermute | solution.py:58
  12.9 26.8 %collective-permute-start.15 = (bf16[96,384]{1,0:T(8,128)(2,1)}, bf16[96,384]{1,0:T(8,128)(2,1)S(1)}, u32[]{:S(2)}, u32[]{:S(2)}) collective-permute-start(bf16[96,384]{1,0:T(8,128)(2,1)} %constant_dynamic-slice_fusion.7), channel_id=1, source_target_pairs={{24,0},{28,4},{0,8},{4,12},{8,16},{12,20},{16,24},{20,28},{25,1},{... | collective-permute-start | bytes 221192 | tf_op jit(solution)/shard_map/ppermute | solution.py:58
  21.0 20.9 %all-to-all-start = ((f32[8,1,1347]{2,1,0:T(1,128)}), f32[8,1,1347]{2,1,0:T(1,128)S(1)}, u32[]{:S(2)}, u32[]{:S(2)}) async-start(f32[8,1,1347]{2,1,0:T(1,128)} %broadcast_in_dim.186), calls=%async_computation | async-start | bytes 90112 | tf_op jit(solution)/shard_map/all_to_all | solution.py:96
  36.1 16.4 %collective-permute-start.5 = (bf16[96,576]{0,1:T(8,128)(2,1)}, bf16[96,576]{0,1:T(8,128)(2,1)S(1)}, u32[]{:S(2)}, u32[]{:S(2)}) collective-permute-start(bf16[96,576]{0,1:T(8,128)(2,1)} %bitcast.25), channel_id=1, source_target_pairs={{24,0},{28,4},{0,8},{4,12},{8,16},{12,20},{16,24},{20,28},{25,1},{... | collective-permute-start | bytes 331784 | tf_op jit(solution)/shard_map/ppermute | solution.py:58
  38.2 27.0 %collective-permute-start.6 = (bf16[96,576]{0,1:T(8,128)(2,1)}, bf16[96,576]{0,1:T(8,128)(2,1)}, u32[]{:S(2)}, u32[]{:S(2)}) collective-permute-start(bf16[96,576]{0,1:T(8,128)(2,1)} %bitcast.25), channel_id=1, source_target_pairs={{0,4},{4,0},{8,12},{12,8},{16,20},{20,16},{24,28},{28,24},{1,5},{5... | collective-permute-start | bytes 331784 | tf_op jit(solution)/shard_map/ppermute | solution.py:52
  39.6 16.0 %collective-permute-start.16 = (bf16[96,384]{1,0:T(8,128)(2,1)}, bf16[96,384]{1,0:T(8,128)(2,1)}, u32[]{:S(2)}, u32[]{:S(2)}) collective-permute-start(bf16[96,384]{1,0:T(8,128)(2,1)} %constant_dynamic-slice_fusion.7), channel_id=1, source_target_pairs={{0,4},{4,0},{8,12},{12,8},{16,20},{20,16},{24,28},{28,24},{1,5},{5... | collective-permute-start | bytes 221192 | tf_op jit(solution)/shard_map/ppermute | solution.py:52
  44.3 20.0 %all-to-all-start.1 = ((bf16[8,32,96]{2,1,0:T(8,128)(2,1)}), bf16[8,32,96]{2,1,0:T(8,128)(2,1)}, u32[]{:S(2)}, u32[]{:S(2)}) async-start(bf16[8,32,96]{2,1,0:T(8,128)(2,1)} %bitcast.444), calls=%async_computation.1 | async-start | bytes 131072 | tf_op jit(solution)/shard_map/all_to_all | solution.py:106
  55.7 73.4 %collective-permute-start.1 = (bf16[3,256,768]{2,1,0:T(8,128)(2,1)S(1)}, bf16[3,256,768]{2,1,0:T(8,128)(2,1)S(1)}, u32[]{:S(2)}, u32[]{:S(2)}) collective-permute-start(bf16[3,256,768]{2,1,0:T(8,128)(2,1)S(1)} %copy-done.2), channel_id=1, source_target_pairs={{0,2},{1,3},{2,0},{3,1},{4,6},{5,7},{6,4},{7,5},{8,10},{9,11},{10,... | collective-permute-start | bytes 3538952 | tf_op jit(solution)/shard_map/ppermute | solution.py:48
  57.3 22.6 %collective-permute-start.22 = (bf16[96,1536]{1,0:T(8,128)(2,1)}, bf16[96,1536]{1,0:T(8,128)(2,1)}, u32[]{:S(2)}, u32[]{:S(2)}) collective-permute-start(bf16[96,1536]{1,0:T(8,128)(2,1)} %reshape.749), channel_id=1, source_target_pairs={{8,0},{12,4},{16,8},{20,12},{24,16},{28,20},{0,24},{4,28},{9,1},{1... | collective-permute-start | bytes 884744 | tf_op jit(solution)/shard_map/ppermute | solution.py:58
  60.5 32.6 %collective-permute-start.23 = (bf16[96,1536]{1,0:T(8,128)(2,1)}, bf16[96,1536]{1,0:T(8,128)(2,1)}, u32[]{:S(2)}, u32[]{:S(2)}) collective-permute-start(bf16[96,1536]{1,0:T(8,128)(2,1)} %reshape.749), channel_id=1, source_target_pairs={{16,0},{20,4},{24,8},{28,12},{0,16},{4,20},{8,24},{12,28},{17,1},{... | collective-permute-start | bytes 884744 | tf_op jit(solution)/shard_map/ppermute | solution.py:58
  65.2 10.8 %collective-permute-start.8 = (bf16[96,576]{0,1:T(8,128)(2,1)}, bf16[96,576]{0,1:T(8,128)(2,1)}, u32[]{:S(2)}, u32[]{:S(2)}) collective-permute-start(bf16[96,576]{0,1:T(8,128)(2,1)} %collective-permute-done.4), channel_id=1, source_target_pairs={{0,4},{4,0},{8,12},{12,8},{16,20},{20,16},{24,28},{28,24},{1,5},{5... | collective-permute-start | bytes 331784 | tf_op jit(solution)/shard_map/ppermute | solution.py:52
  67.7 10.3 %collective-permute-start.9 = (bf16[96,576]{0,1:T(8,128)(2,1)}, bf16[96,576]{0,1:T(8,128)(2,1)}, u32[]{:S(2)}, u32[]{:S(2)}) collective-permute-start(bf16[96,576]{0,1:T(8,128)(2,1)} %copy-done.72), channel_id=1, source_target_pairs={{0,4},{4,0},{8,12},{12,8},{16,20},{20,16},{24,28},{28,24},{1,5},{5... | collective-permute-start | bytes 331784 | tf_op jit(solution)/shard_map/ppermute | solution.py:52
  70.9 59.9 %all-to-all-start.2 = ((f32[8,4,2304]{2,1,0:T(4,128)}), f32[8,4,2304]{2,1,0:T(4,128)}, u32[]{:S(2)}, u32[]{:S(2)}) async-start(f32[8,4,2304]{2,1,0:T(4,128)} %reshape.747), calls=%async_computation.2 | async-start | bytes 589824 | tf_op jit(solution)/shard_map/all_to_all | solution.py:106
  76.0 23.0 %collective-permute-start.24 = (bf16[96,1536]{1,0:T(8,128)(2,1)}, bf16[96,1536]{1,0:T(8,128)(2,1)}, u32[]{:S(2)}, u32[]{:S(2)}) collective-permute-start(bf16[96,1536]{1,0:T(8,128)(2,1)} %reshape.749), channel_id=1, source_target_pairs={{24,0},{28,4},{0,8},{4,12},{8,16},{12,20},{16,24},{20,28},{25,1},{... | collective-permute-start | bytes 884744 | tf_op jit(solution)/shard_map/ppermute | solution.py:58
  78.0 21.0 %collective-permute-start.29 = (bf16[192,768]{1,0:T(8,128)(2,1)}, bf16[192,768]{1,0:T(8,128)(2,1)}, u32[]{:S(2)}, u32[]{:S(2)}) collective-permute-start(bf16[192,768]{1,0:T(8,128)(2,1)} %constant_dynamic-slice_fusion.4), channel_id=1, source_target_pairs={{8,0},{12,4},{16,8},{20,12},{24,16},{28,20},{0,24},{4,28},{9,1},{1... | collective-permute-start | bytes 884744 | tf_op jit(solution)/shard_map/ppermute | solution.py:58
  79.9 33.8 %collective-permute-start.30 = (bf16[192,768]{1,0:T(8,128)(2,1)}, bf16[192,768]{1,0:T(8,128)(2,1)}, u32[]{:S(2)}, u32[]{:S(2)}) collective-permute-start(bf16[192,768]{1,0:T(8,128)(2,1)} %constant_dynamic-slice_fusion.4), channel_id=1, source_target_pairs={{16,0},{20,4},{24,8},{28,12},{0,16},{4,20},{8,24},{12,28},{17,1},{... | collective-permute-start | bytes 884744 | tf_op jit(solution)/shard_map/ppermute | solution.py:58
  93.1 21.1 %collective-permute-start.31 = (bf16[192,768]{1,0:T(8,128)(2,1)}, bf16[192,768]{1,0:T(8,128)(2,1)}, u32[]{:S(2)}, u32[]{:S(2)}) collective-permute-start(bf16[192,768]{1,0:T(8,128)(2,1)} %constant_dynamic-slice_fusion.4), channel_id=1, source_target_pairs={{24,0},{28,4},{0,8},{4,12},{8,16},{12,20},{16,24},{20,28},{25,1},{... | collective-permute-start | bytes 884744 | tf_op jit(solution)/shard_map/ppermute | solution.py:58
  99.0 21.3 %collective-permute-start.25 = (bf16[96,1536]{1,0:T(8,128)(2,1)}, bf16[96,1536]{1,0:T(8,128)(2,1)S(1)}, u32[]{:S(2)}, u32[]{:S(2)}) collective-permute-start(bf16[96,1536]{1,0:T(8,128)(2,1)} %reshape.749), channel_id=1, source_target_pairs={{0,4},{4,0},{8,12},{12,8},{16,20},{20,16},{24,28},{28,24},{1,5},{5... | collective-permute-start | bytes 884744 | tf_op jit(solution)/shard_map/ppermute | solution.py:52
  99.0 21.3 %collective-permute-start.26 = (bf16[96,1536]{1,0:T(8,128)(2,1)}, bf16[96,1536]{1,0:T(8,128)(2,1)S(1)}, u32[]{:S(2)}, u32[]{:S(2)}) collective-permute-start(bf16[96,1536]{1,0:T(8,128)(2,1)} %collective-permute-done.22), channel_id=1, source_target_pairs={{0,4},{4,0},{8,12},{12,8},{16,20},{20,16},{24,28},{28,24},{1,5},{5... | collective-permute-start | bytes 884744 | tf_op jit(solution)/shard_map/ppermute | solution.py:52
  113.7 9.6 %collective-permute-start.27 = (bf16[96,1536]{1,0:T(8,128)(2,1)}, bf16[96,1536]{1,0:T(8,128)(2,1)S(1)}, u32[]{:S(2)}, u32[]{:S(2)}) collective-permute-start(bf16[96,1536]{1,0:T(8,128)(2,1)} %collective-permute-done.23), channel_id=1, source_target_pairs={{0,4},{4,0},{8,12},{12,8},{16,20},{20,16},{24,28},{28,24},{1,5},{5... | collective-permute-start | bytes 884744 | tf_op jit(solution)/shard_map/ppermute | solution.py:52
  114.2 14.9 %collective-permute-start.28 = (bf16[96,1536]{1,0:T(8,128)(2,1)}, bf16[96,1536]{1,0:T(8,128)(2,1)S(1)}, u32[]{:S(2)}, u32[]{:S(2)}) collective-permute-start(bf16[96,1536]{1,0:T(8,128)(2,1)} %collective-permute-done.24), channel_id=1, source_target_pairs={{0,4},{4,0},{8,12},{12,8},{16,20},{20,16},{24,28},{28,24},{1,5},{5... | collective-permute-start | bytes 884744 | tf_op jit(solution)/shard_map/ppermute | solution.py:52
  120.3 12.8 %collective-permute-start = (bf16[3,256,768]{2,1,0:T(8,128)(2,1)S(1)}, bf16[3,256,768]{2,1,0:T(8,128)(2,1)}, u32[]{:S(2)}, u32[]{:S(2)}) collective-permute-start(bf16[3,256,768]{2,1,0:T(8,128)(2,1)S(1)} %copy-done.2), channel_id=1, source_target_pairs={{0,1},{1,0},{2,3},{3,2},{4,5},{5,4},{6,7},{7,6},{8,9},{9,8},{10,11... | collective-permute-start | bytes 3538952 | tf_op jit(solution)/shard_map/ppermute | solution.py:48
  120.3 161.8 %collective-permute-start.32 = (bf16[192,768]{1,0:T(8,128)(2,1)}, bf16[192,768]{1,0:T(8,128)(2,1)}, u32[]{:S(2)}, u32[]{:S(2)}) collective-permute-start(bf16[192,768]{1,0:T(8,128)(2,1)} %constant_dynamic-slice_fusion.4), channel_id=1, source_target_pairs={{0,4},{4,0},{8,12},{12,8},{16,20},{20,16},{24,28},{28,24},{1,5},{5... | collective-permute-start | bytes 884744 | tf_op jit(solution)/shard_map/ppermute | solution.py:52
  123.2 150.4 %collective-permute-start.37 = (bf16[3,256,768]{2,1,0:T(8,128)(2,1)}, bf16[3,256,768]{2,1,0:T(8,128)(2,1)}, u32[]{:S(2)}, u32[]{:S(2)}) collective-permute-start(bf16[3,256,768]{2,1,0:T(8,128)(2,1)} %param.37), channel_id=1, source_target_pairs={{0,1},{1,0},{2,3},{3,2},{4,5},{5,4},{6,7},{7,6},{8,9},{9,8},{10,11... | collective-permute-start | bytes 3538952 | tf_op jit(solution)/shard_map/ppermute | solution.py:48
  129.1 126.8 %collective-permute-start.20 = (bf16[768,384]{1,0:T(8,128)(2,1)}, bf16[768,384]{1,0:T(8,128)(2,1)}, u32[]{:S(2)}, u32[]{:S(2)}) collective-permute-start(bf16[768,384]{1,0:T(8,128)(2,1)} %bitcast.50), channel_id=1, source_target_pairs={{0,1},{1,0},{2,3},{3,2},{4,5},{5,4},{6,7},{7,6},{8,9},{9,8},{10,11... | collective-permute-start | bytes 1769480 | tf_op jit(solution)/shard_map/ppermute | solution.py:48
  255.1 9.9 %collective-permute-start.11 = (bf16[3,256,192]{1,2,0:T(8,128)(2,1)S(1)}, bf16[3,256,192]{1,2,0:T(8,128)(2,1)S(1)}, u32[]{:S(2)}, u32[]{:S(2)}) collective-permute-start(bf16[3,256,192]{1,2,0:T(8,128)(2,1)S(1)} %bitcast.551), channel_id=1, source_target_pairs={{0,2},{1,3},{2,0},{3,1},{4,6},{5,7},{6,4},{7,5},{8,10},{9,11},{10,... | collective-permute-start | bytes 884744 | tf_op jit(solution)/shard_map/ppermute | solution.py:48
  255.9 14.1 %collective-permute-start.12 = (bf16[3,256,192]{1,2,0:T(8,128)(2,1)S(1)}, bf16[3,256,192]{1,2,0:T(8,128)(2,1)S(1)}, u32[]{:S(2)}, u32[]{:S(2)}) collective-permute-start(bf16[3,256,192]{1,2,0:T(8,128)(2,1)S(1)} %bitcast.550), channel_id=1, source_target_pairs={{0,3},{1,2},{2,1},{3,0},{4,7},{5,6},{6,5},{7,4},{8,11},{9,10},{10,... | collective-permute-start | bytes 884744 | tf_op jit(solution)/shard_map/ppermute | solution.py:48
  259.5 22.7 %collective-permute-start.33 = (bf16[192,768]{1,0:T(8,128)(2,1)}, bf16[192,768]{1,0:T(8,128)(2,1)S(1)}, u32[]{:S(2)}, u32[]{:S(2)}) collective-permute-start(bf16[192,768]{1,0:T(8,128)(2,1)} %collective-permute-done.29), channel_id=1, source_target_pairs={{0,4},{4,0},{8,12},{12,8},{16,20},{20,16},{24,28},{28,24},{1,5},{5... | collective-permute-start | bytes 884744 | tf_op jit(solution)/shard_map/ppermute | solution.py:52
  265.0 17.1 %collective-permute-start.34 = (bf16[192,768]{1,0:T(8,128)(2,1)}, bf16[192,768]{1,0:T(8,128)(2,1)S(1)}, u32[]{:S(2)}, u32[]{:S(2)}) collective-permute-start(bf16[192,768]{1,0:T(8,128)(2,1)} %collective-permute-done.30), channel_id=1, source_target_pairs={{0,4},{4,0},{8,12},{12,8},{16,20},{20,16},{24,28},{28,24},{1,5},{5... | collective-permute-start | bytes 884744 | tf_op jit(solution)/shard_map/ppermute | solution.py:52
  270.0 12.1 %collective-permute-start.35 = (bf16[192,768]{1,0:T(8,128)(2,1)}, bf16[192,768]{1,0:T(8,128)(2,1)S(1)}, u32[]{:S(2)}, u32[]{:S(2)}) collective-permute-start(bf16[192,768]{1,0:T(8,128)(2,1)} %collective-permute-done.31), channel_id=1, source_target_pairs={{0,4},{4,0},{8,12},{12,8},{16,20},{20,16},{24,28},{28,24},{1,5},{5... | collective-permute-start | bytes 884744 | tf_op jit(solution)/shard_map/ppermute | solution.py:52
  278.9 10.9 %collective-permute-start.21 = (bf16[768,768]{1,0:T(8,128)(2,1)}, bf16[768,768]{1,0:T(8,128)(2,1)}, u32[]{:S(2)}, u32[]{:S(2)}) collective-permute-start(bf16[768,768]{1,0:T(8,128)(2,1)} %get-tuple-element.374), channel_id=1, source_target_pairs={{0,1},{1,0},{2,3},{3,2},{4,5},{5,4},{6,7},{7,6},{8,9},{9,8},{10,11... | collective-permute-start | bytes 3538952 | tf_op jit(solution)/shard_map/ppermute | solution.py:48
  324.7 41.5 %collective-permute-start.67 = (bf16[4,192,768]{2,1,0:T(8,128)(2,1)}, bf16[4,192,768]{2,1,0:T(8,128)(2,1)}, u32[]{:S(2)}, u32[]{:S(2)}) collective-permute-start(bf16[4,192,768]{2,1,0:T(8,128)(2,1)} %fusion.108), channel_id=1, source_target_pairs={{0,4},{4,0},{8,12},{12,8},{16,20},{20,16},{24,28},{28,24},{1,5},{5... | collective-permute-start | bytes 3538952 | tf_op jit(solution)/shard_map/ppermute | solution.py:52
  353.7 27.6 %collective-permute-start.61 = (bf16[4,96,1536]{2,1,0:T(8,128)(2,1)}, bf16[4,96,1536]{2,1,0:T(8,128)(2,1)}, u32[]{:S(2)}, u32[]{:S(2)}) collective-permute-start(bf16[4,96,1536]{2,1,0:T(8,128)(2,1)} %fusion.107), channel_id=1, source_target_pairs={{0,4},{4,0},{8,12},{12,8},{16,20},{20,16},{24,28},{28,24},{1,5},{5... | collective-permute-start | bytes 3538952 | tf_op jit(solution)/shard_map/ppermute | solution.py:52
  355.9 32.2 %collective-permute-start.38 = (bf16[768,768]{1,0:T(8,128)(2,1)}, bf16[768,768]{1,0:T(8,128)(2,1)}, u32[]{:S(2)}, u32[]{:S(2)}) collective-permute-start(bf16[768,768]{1,0:T(8,128)(2,1)} %slice.335), channel_id=1, source_target_pairs={{0,1},{1,0},{2,3},{3,2},{4,5},{5,4},{6,7},{7,6},{8,9},{9,8},{10,11... | collective-permute-start | bytes 3538952 | tf_op jit(solution)/shard_map/ppermute | solution.py:48
  364.9 27.4 %collective-permute-start.36 = (bf16[768,768]{1,0:T(8,128)(2,1)}, bf16[768,768]{1,0:T(8,128)(2,1)}, u32[]{:S(2)}, u32[]{:S(2)}) collective-permute-start(bf16[768,768]{1,0:T(8,128)(2,1)} %slice.336), channel_id=1, source_target_pairs={{0,1},{1,0},{2,3},{3,2},{4,5},{5,4},{6,7},{7,6},{8,9},{9,8},{10,11... | collective-permute-start | bytes 3538952 | tf_op jit(solution)/shard_map/ppermute | solution.py:48
  369.6 45.4 %collective-permute-start.68 = (bf16[192,768]{1,0:T(8,128)(2,1)}, bf16[192,768]{1,0:T(8,128)(2,1)}, u32[]{:S(2)}, u32[]{:S(2)}) collective-permute-start(bf16[192,768]{1,0:T(8,128)(2,1)} %get-tuple-element.314), channel_id=1, source_target_pairs={{8,0},{12,4},{16,8},{20,12},{24,16},{28,20},{0,24},{4,28},{9,1},{1... | collective-permute-start | bytes 884744 | tf_op jit(solution)/shard_map/ppermute | solution.py:58
  369.6 53.9 %collective-permute-start.69 = (bf16[192,768]{1,0:T(8,128)(2,1)}, bf16[192,768]{1,0:T(8,128)(2,1)}, u32[]{:S(2)}, u32[]{:S(2)}) collective-permute-start(bf16[192,768]{1,0:T(8,128)(2,1)} %get-tuple-element.316), channel_id=1, source_target_pairs={{16,0},{20,4},{24,8},{28,12},{0,16},{4,20},{8,24},{12,28},{17,1},{... | collective-permute-start | bytes 884744 | tf_op jit(solution)/shard_map/ppermute | solution.py:58
  381.3 42.2 %collective-permute-start.70 = (bf16[192,768]{1,0:T(8,128)(2,1)}, bf16[192,768]{1,0:T(8,128)(2,1)}, u32[]{:S(2)}, u32[]{:S(2)}) collective-permute-start(bf16[192,768]{1,0:T(8,128)(2,1)} %get-tuple-element.315), channel_id=1, source_target_pairs={{24,0},{28,4},{0,8},{4,12},{8,16},{12,20},{16,24},{20,28},{25,1},{... | collective-permute-start | bytes 884744 | tf_op jit(solution)/shard_map/ppermute | solution.py:58
  388.0 38.1 %collective-permute-start.62 = (bf16[96,1536]{1,0:T(8,128)(2,1)}, bf16[96,1536]{1,0:T(8,128)(2,1)}, u32[]{:S(2)}, u32[]{:S(2)}) collective-permute-start(bf16[96,1536]{1,0:T(8,128)(2,1)} %get-tuple-element.317), channel_id=1, source_target_pairs={{8,0},{12,4},{16,8},{20,12},{24,16},{28,20},{0,24},{4,28},{9,1},{1... | collective-permute-start | bytes 884744 | tf_op jit(solution)/shard_map/ppermute | solution.py:58
  398.6 9.9 %collective-permute-start.59 = (f32[4,2304]{1,0:T(4,128)S(1)}, f32[4,2304]{1,0:T(4,128)S(1)}, u32[]{:S(2)}, u32[]{:S(2)}) collective-permute-start(f32[4,2304]{1,0:T(4,128)S(1)} %pad_maximum_fusion.21), channel_id=1, source_target_pairs={{0,1},{1,0},{2,3},{3,2},{4,5},{5,4},{6,7},{7,6},{8,9},{9,8},{10,11... | collective-permute-start | bytes 110600 | tf_op jit(solution)/shard_map/ppermute | solution.py:48
  412.6 21.1 %collective-permute-start.63 = (bf16[96,1536]{1,0:T(8,128)(2,1)S(1)}, bf16[96,1536]{1,0:T(8,128)(2,1)S(1)}, u32[]{:S(2)}, u32[]{:S(2)}) collective-permute-start(bf16[96,1536]{1,0:T(8,128)(2,1)S(1)} %copy-done.56), channel_id=1, source_target_pairs={{16,0},{20,4},{24,8},{28,12},{0,16},{4,20},{8,24},{12,28},{17,1},{... | collective-permute-start | bytes 884744 | tf_op jit(solution)/shard_map/ppermute | solution.py:58
  415.0 18.7 %collective-permute-start.64 = (bf16[96,1536]{1,0:T(8,128)(2,1)S(1)}, bf16[96,1536]{1,0:T(8,128)(2,1)}, u32[]{:S(2)}, u32[]{:S(2)}) collective-permute-start(bf16[96,1536]{1,0:T(8,128)(2,1)S(1)} %copy-done.55), channel_id=1, source_target_pairs={{24,0},{28,4},{0,8},{4,12},{8,16},{12,20},{16,24},{20,28},{25,1},{... | collective-permute-start | bytes 884744 | tf_op jit(solution)/shard_map/ppermute | solution.py:58
  423.5 187.2 %collective-permute-start.52 = (bf16[768,384]{1,0:T(8,128)(2,1)}, bf16[768,384]{1,0:T(8,128)(2,1)}, u32[]{:S(2)}, u32[]{:S(2)}) collective-permute-start(bf16[768,384]{1,0:T(8,128)(2,1)} %dynamic-slice_convert_fusion.2), channel_id=1, source_target_pairs={{0,1},{1,0},{2,3},{3,2},{4,5},{5,4},{6,7},{7,6},{8,9},{9,8},{10,11... | collective-permute-start | bytes 1769480 | tf_op jit(solution)/shard_map/ppermute | solution.py:48
  423.5 14.4 %collective-permute-start.39 = (bf16[3,256,192]{1,2,0:T(8,128)(2,1)}, bf16[3,256,192]{1,2,0:T(8,128)(2,1)S(1)}, u32[]{:S(2)}, u32[]{:S(2)}) collective-permute-start(bf16[3,256,192]{1,2,0:T(8,128)(2,1)} %bitcast.559), channel_id=1, source_target_pairs={{0,1},{1,0},{2,3},{3,2},{4,5},{5,4},{6,7},{7,6},{8,9},{9,8},{10,11... | collective-permute-start | bytes 884744 | tf_op jit(solution)/shard_map/ppermute | solution.py:48
  426.1 12.9 %collective-permute-start.40 = (bf16[3,256,192]{1,2,0:T(8,128)(2,1)S(1)}, bf16[3,256,192]{1,2,0:T(8,128)(2,1)S(1)}, u32[]{:S(2)}, u32[]{:S(2)}) collective-permute-start(bf16[3,256,192]{1,2,0:T(8,128)(2,1)S(1)} %bitcast.558), channel_id=1, source_target_pairs={{0,2},{1,3},{2,0},{3,1},{4,6},{5,7},{6,4},{7,5},{8,10},{9,11},{10,... | collective-permute-start | bytes 884744 | tf_op jit(solution)/shard_map/ppermute | solution.py:48
  433.8 9.2 %collective-permute-start.41 = (bf16[3,256,192]{1,2,0:T(8,128)(2,1)S(1)}, bf16[3,256,192]{1,2,0:T(8,128)(2,1)S(1)}, u32[]{:S(2)}, u32[]{:S(2)}) collective-permute-start(bf16[3,256,192]{1,2,0:T(8,128)(2,1)S(1)} %bitcast.557), channel_id=1, source_target_pairs={{0,3},{1,2},{2,1},{3,0},{4,7},{5,6},{6,5},{7,4},{8,11},{9,10},{10,... | collective-permute-start | bytes 884744 | tf_op jit(solution)/shard_map/ppermute | solution.py:48
  434.5 191.6 %collective-permute-start.71 = (bf16[192,768]{1,0:T(8,128)(2,1)}, bf16[192,768]{1,0:T(8,128)(2,1)}, u32[]{:S(2)}, u32[]{:S(2)}) collective-permute-start(bf16[192,768]{1,0:T(8,128)(2,1)} %fusion.116), channel_id=1, source_target_pairs={{0,2},{1,3},{2,0},{3,1},{4,6},{5,7},{6,4},{7,5},{8,10},{9,11},{10,... | collective-permute-start | bytes 884744 | tf_op jit(solution)/shard_map/ppermute | solution.py:48
  437.9 176.8 %collective-permute-start.65 = (bf16[96,8,192]{2,1,0:T(8,128)(2,1)}, bf16[96,8,192]{2,1,0:T(8,128)(2,1)}, u32[]{:S(2)}, u32[]{:S(2)}) collective-permute-start(bf16[96,8,192]{2,1,0:T(8,128)(2,1)} %reshape.769), channel_id=1, source_target_pairs={{0,2},{1,3},{2,0},{3,1},{4,6},{5,7},{6,4},{7,5},{8,10},{9,11},{10,... | collective-permute-start | bytes 884744 | tf_op jit(solution)/shard_map/ppermute | solution.py:48
  582.7 14.2 %all-to-all-start.3 = ((f32[8,1,1056]{2,1,0:T(1,128)}), f32[8,1,1056]{2,1,0:T(1,128)S(1)}, u32[]{:S(2)}, u32[]{:S(2)}) async-start(f32[8,1,1056]{2,1,0:T(1,128)} %all_to_all.28), calls=%async_computation.3 | async-start | bytes 73728 | tf_op jit(solution)/shard_map/all_to_all | solution.py:106
  595.0 34.7 %collective-permute-start.46 = (bf16[4,96,576]{2,1,0:T(8,128)(2,1)}, bf16[4,96,576]{2,1,0:T(8,128)(2,1)}, u32[]{:S(2)}, u32[]{:S(2)}) collective-permute-start(bf16[4,96,576]{2,1,0:T(8,128)(2,1)} %fusion.121), channel_id=1, source_target_pairs={{0,4},{4,0},{8,12},{12,8},{16,20},{20,16},{24,28},{28,24},{1,5},{5... | collective-permute-start | bytes 1327112 | tf_op jit(solution)/shard_map/ppermute | solution.py:52
  597.7 19.3 %all-to-all-start.4 = ((f32[8,4,2304]{2,1,0:T(4,128)}), f32[8,4,2304]{2,1,0:T(4,128)S(1)}, u32[]{:S(2)}, u32[]{:S(2)}) async-start(f32[8,4,2304]{2,1,0:T(4,128)} %broadcast_in_dim.206), calls=%async_computation.4 | async-start | bytes 589824 | tf_op jit(solution)/shard_map/all_to_all | solution.py:96
  608.7 50.6 %collective-permute-start.42 = (bf16[2,3,256,768]{3,2,1,0:T(8,128)(2,1)}, bf16[2,3,256,768]{3,2,1,0:T(8,128)(2,1)}, u32[]{:S(2)}, u32[]{:S(2)}) collective-permute-start(bf16[2,3,256,768]{3,2,1,0:T(8,128)(2,1)} %pad_maximum_fusion.5), channel_id=1, source_target_pairs={{0,1},{1,0},{2,3},{3,2},{4,5},{5,4},{6,7},{7,6},{8,9},{9,8},{10,11... | collective-permute-start | bytes 7077896 | tf_op jit(solution)/shard_map/ppermute | solution.py:48
  612.7 24.2 %collective-permute-start.53 = (bf16[4,96,384]{2,1,0:T(8,128)(2,1)}, bf16[4,96,384]{2,1,0:T(8,128)(2,1)}, u32[]{:S(2)}, u32[]{:S(2)}) collective-permute-start(bf16[4,96,384]{2,1,0:T(8,128)(2,1)} %fusion.122), channel_id=1, source_target_pairs={{0,4},{4,0},{8,12},{12,8},{16,20},{20,16},{24,28},{28,24},{1,5},{5... | collective-permute-start | bytes 884744 | tf_op jit(solution)/shard_map/ppermute | solution.py:52
  616.8 51.1 %collective-permute-start.66 = (f32[96,8,192]{2,1,0:T(8,128)}, f32[96,8,192]{2,1,0:T(8,128)}, u32[]{:S(2)}, u32[]{:S(2)}) collective-permute-start(f32[96,8,192]{2,1,0:T(8,128)} %convert_add_fusion.1), channel_id=1, source_target_pairs={{0,1},{1,0},{2,3},{3,2},{4,5},{5,4},{6,7},{7,6},{8,9},{9,8},{10,11... | collective-permute-start | bytes 1769480 | tf_op jit(solution)/shard_map/ppermute | solution.py:48
  620.8 14.6 %all-to-all-start.5 = ((f32[8,32,96]{2,1,0:T(8,128)}), f32[8,32,96]{2,1,0:T(8,128)S(1)}, u32[]{:S(2)}, u32[]{:S(2)}) async-start(f32[8,32,96]{2,1,0:T(8,128)} %broadcast_in_dim.207), calls=%async_computation.5 | async-start | bytes 262144 | tf_op jit(solution)/shard_map/all_to_all | solution.py:96
  635.4 12.4 %collective-permute-start.48 = (bf16[96,576]{1,0:T(8,128)(2,1)S(1)}, bf16[96,576]{1,0:T(8,128)(2,1)}, u32[]{:S(2)}, u32[]{:S(2)}) collective-permute-start(bf16[96,576]{1,0:T(8,128)(2,1)S(1)} %get-tuple-element.336), channel_id=1, source_target_pairs={{16,0},{20,4},{24,8},{28,12},{0,16},{4,20},{8,24},{12,28},{17,1},{... | collective-permute-start | bytes 331784 | tf_op jit(solution)/shard_map/ppermute | solution.py:58
  636.8 11.0 %collective-permute-start.49 = (bf16[96,576]{1,0:T(8,128)(2,1)S(1)}, bf16[96,576]{1,0:T(8,128)(2,1)S(1)}, u32[]{:S(2)}, u32[]{:S(2)}) collective-permute-start(bf16[96,576]{1,0:T(8,128)(2,1)S(1)} %get-tuple-element.335), channel_id=1, source_target_pairs={{24,0},{28,4},{0,8},{4,12},{8,16},{12,20},{16,24},{20,28},{25,1},{... | collective-permute-start | bytes 331784 | tf_op jit(solution)/shard_map/ppermute | solution.py:58
  639.5 11.4 %collective-permute-start.54 = (bf16[96,384]{1,0:T(8,128)(2,1)S(1)}, bf16[96,384]{1,0:T(8,128)(2,1)S(1)}, u32[]{:S(2)}, u32[]{:S(2)}) collective-permute-start(bf16[96,384]{1,0:T(8,128)(2,1)S(1)} %get-tuple-element.337), channel_id=1, source_target_pairs={{8,0},{12,4},{16,8},{20,12},{24,16},{28,20},{0,24},{4,28},{9,1},{1... | collective-permute-start | bytes 221192 | tf_op jit(solution)/shard_map/ppermute | solution.py:58
  650.9 24.2 %collective-permute-start.72 = (f32[192,768]{1,0:T(8,128)}, f32[192,768]{1,0:T(8,128)}, u32[]{:S(2)}, u32[]{:S(2)}) collective-permute-start(f32[192,768]{1,0:T(8,128)} %get-tuple-element.329), channel_id=1, source_target_pairs={{0,1},{1,0},{2,3},{3,2},{4,5},{5,4},{6,7},{7,6},{8,9},{9,8},{10,11... | collective-permute-start | bytes 1769480 | tf_op jit(solution)/shard_map/ppermute | solution.py:48
  658.7 18.8 %collective-permute-start.51 = (bf16[2,96,576]{2,1,0:T(8,128)(2,1)}, bf16[2,96,576]{2,1,0:T(8,128)(2,1)}, u32[]{:S(2)}, u32[]{:S(2)}) collective-permute-start(bf16[2,96,576]{2,1,0:T(8,128)(2,1)} %pad_maximum_fusion.18), channel_id=1, source_target_pairs={{0,1},{1,0},{2,3},{3,2},{4,5},{5,4},{6,7},{7,6},{8,9},{9,8},{10,11... | collective-permute-start | bytes 663560 | tf_op jit(solution)/shard_map/ppermute | solution.py:48
  666.1 28.2 %collective-permute-start.43 = (bf16[3,256,768]{2,1,0:T(8,128)(2,1)}, bf16[3,256,768]{2,1,0:T(8,128)(2,1)}, u32[]{:S(2)}, u32[]{:S(2)}) collective-permute-start(bf16[3,256,768]{2,1,0:T(8,128)(2,1)} %fusion.78), channel_id=1, source_target_pairs={{0,2},{1,3},{2,0},{3,1},{4,6},{5,7},{6,4},{7,5},{8,10},{9,11},{10,... | collective-permute-start | bytes 3538952 | tf_op jit(solution)/shard_map/ppermute | solution.py:48
  (131 other events, 1208.8 us)

commit v2 on v1

v2 whole, which is shorter than its diff:
```python
import functools
import math

import jax
import jax.numpy as jnp
from jax import lax
from jax.experimental import pallas as pl
from jax.experimental.pallas import tpu as pltpu
from jax.sharding import PartitionSpec as P

H = 12
HD = 64
EPS = 1e-05
NEG = -1e30
COST = 1.0
F32 = jnp.float32
BF16 = jnp.bfloat16
HIGHEST = lax.Precision.HIGHEST
VMEM_LIMIT = 62 * 1024 * 1024
EXTRA = 16


def standardize(values):
    centred = values - jnp.mean(values, axis=-1, keepdims=True)
    inverse = lax.rsqrt(jnp.mean(centred * centred, axis=-1, keepdims=True) + EPS)
    return centred * inverse, inverse


def norm_back(gradient, normed, inverse):
    return inverse * (
        gradient
        - jnp.mean(gradient, axis=-1, keepdims=True)
        - normed * jnp.mean(gradient * normed, axis=-1, keepdims=True)
    )


def dot(left, right):
    return jnp.dot(left, right, preferred_element_type=F32)


def dot_bt(left, right):
    return lax.dot_general(left, right, (((1,), (1,)), ((), ())), preferred_element_type=F32)


def dot_at(left, right):
    return lax.dot_general(left, right, (((0,), (0,)), ((), ())), preferred_element_type=F32)


TAIL_P = 0.55
TAIL = (
    0.001045374169866761,
    0.2933056852691112,
    0.41788788917041303,
    -0.08811700935317877,
    0.8046529189842585,
    -0.5409110079247637,
    0.11213617568673577,
)


def gelu_both(values):
    bell = jnp.exp(values * values * -0.5)
    inner = 1.0 / (1.0 + (TAIL_P / math.sqrt(2.0)) * jnp.abs(values))
    tail = TAIL[6]
    for coefficient in TAIL[5::-1]:
        tail = tail * inner + coefficient
    tail = tail * bell * 0.5
    cumulative = jnp.where(values >= 0.0, 1.0 - tail, tail)
    return values * cumulative, cumulative + values * bell * (1.0 / math.sqrt(2.0 * math.pi))


def after(value, *others):
    return lax.optimization_barrier((value, others))[0]


def seq_swap(value, mask):
    return lax.ppermute(value, "seq", [(s, s ^ mask) for s in range(lax.axis_size("seq"))])


def dp_swap(value, mask):
    return lax.ppermute(value, "dp", [(d, d ^ mask) for d in range(lax.axis_size("dp"))])


def dp_collect(value):
    mine = [value] + [dp_swap(value, m) for m in range(2, lax.axis_size("dp"), 2)]
    return mine, dp_swap(jnp.stack(mine), 1)


def quad(value):
    across = seq_swap(value, 2)
    return value, across, seq_swap(jnp.stack([value, across]), 1)


def dp_turn(value, outer_only=False):
    groups = None
    if outer_only:
        outer = lax.axis_size("dp") // 2
        groups = [[o * 2 + i for o in range(outer)] for i in range(2)]
    return lax.all_to_all(
        value, "dp", split_axis=0, concat_axis=0, tiled=True, axis_index_groups=groups
    )


def dp_all(value):
    return dp_turn(jnp.broadcast_to(value[None], (lax.axis_size("dp"),) + value.shape))


def run(body, grid, meta, ins, outs, scratch=(), cost=(0, 0, 0), name=None, held=()):
    specs = [pl.BlockSpec(block, index) for _, block, index in ins]
    specs += [pl.BlockSpec(memory_space=pl.ANY) for _ in held]
    first = 1 + len(ins)
    kernel = body
    if held:

        def kernel(meta, *refs):
            return body(meta, *refs[: len(ins)], *refs[len(ins) + len(held) :])

    return pl.pallas_call(
        kernel,
        grid_spec=pltpu.PrefetchScalarGridSpec(
            num_scalar_prefetch=1,
            grid=grid,
            in_specs=specs,
            out_specs=[pl.BlockSpec(block, index) for _, _, block, index in outs],
            scratch_shapes=list(scratch),
        ),
        out_shape=[jax.ShapeDtypeStruct(shape, dtype) for shape, dtype, _, _ in outs],
        input_output_aliases={first + n: k for n, (_, k) in enumerate(held)},
        compiler_params=pltpu.CompilerParams(
            dimension_semantics=("arbitrary",) * len(grid), vmem_limit_bytes=VMEM_LIMIT
        ),
        cost_estimate=pl.CostEstimate(
            flops=int(cost[0] * COST), bytes_accessed=int(cost[1] * COST), transcendentals=0
        ),
        name=name,
    )(meta, *[array for array, _, _ in ins], *[array for array, _ in held])


def whole(array):
    zeros = (0,) * array.ndim
    return (array, array.shape, lambda *_: zeros)


def out_whole(shape, dtype):
    zeros = (0,) * len(shape)
    return (shape, dtype, shape, lambda *_: zeros)


def partner_lanes(tile):
    lane = lax.broadcasted_iota(jnp.int32, tile.shape, 1)
    ahead = pltpu.roll(tile, 96, 1)
    behind = pltpu.roll(tile, 32, 1)
    return jnp.where((lane & (HD // 2)) == 0, ahead, behind)


def qkv_kernel(meta, x0, x1, gain, bias, w, b, cosine, sine, out):
    half = w.shape[1] // 3
    tokens = jnp.where(pl.program_id(0) == 0, x0[0], x1[0]).astype(F32)
    normed, _ = standardize(tokens)
    attn_input = (normed * gain[...] + bias[...]).astype(BF16)
    projected = dot(attn_input, w[...]) + b[...]
    cos, sin = cosine[...], sine[...]
    scale = HD**-0.5
    lane = lax.broadcasted_iota(jnp.int32, cos.shape, 1)
    for t in range(2 * half // 128):
        tile = projected[:, t * 128 : (t + 1) * 128]
        turned = tile * cos + partner_lanes(tile) * sin
        if (t + 1) * 128 <= half:
            turned = turned * scale
        elif t * 128 < half:
            turned = turned * jnp.where(lane < half - t * 128, scale, 1.0)
        out[0, :, t * 128 : (t + 1) * 128] = turned.astype(BF16)
    out[0, :, 2 * half :] = projected[:, 2 * half :].astype(BF16)


def qkv_call(meta, base, x0, x1, gain, bias, w, b, cosine, sine):
    count, rows, width = x0.shape
    last = count - 1
    return run(
        qkv_kernel,
        (2, count),
        meta,
        [
            (x0, (1, rows, width), lambda p, q, m: (jnp.where(p == 0, q, last), 0, 0)),
            (x1, (1, rows, width), lambda p, q, m: (jnp.where(p == 0, 0, q), 0, 0)),
            whole(gain),
            whole(bias),
            whole(w),
            whole(b),
            (cosine, (rows, 128), lambda p, q, m: (base + p, 0)),
            (sine, (rows, 128), lambda p, q, m: (base + p, 0)),
        ],
        [
            (
                (count, 2 * rows, w.shape[1]),
                BF16,
                (1, rows, w.shape[1]),
                lambda p, q, m: (q, p, 0),
            )
        ],
        cost=(4 * count * rows * width * w.shape[1], 10 * count * rows * width, 0),
        name="qkv",
    )[0]


def fold(rows):
    half = rows.shape[0] // 2
    return jnp.concatenate([rows[:half], rows[half:]], axis=1)


def unfold(pair):
    width = pair.shape[1] // 2
    return jnp.concatenate([pair[:, :width], pair[:, width:]], axis=0)


def attend_kernel(base, meta, qa, qb, o0, o1, weights, recips):
    b, k = pl.program_id(0), pl.program_id(1)
    j = base + k
    s, prefix = meta[0], meta[4 + b]
    rows = o0.shape[1] * 2
    hw = o0.shape[2] // 2
    heads = hw // HD
    half = qa.shape[1]
    source = qb if base else qa
    mine = source[0, pl.ds(pl.multiple_of(k * rows, rows), rows), :hw]
    at = (s ^ j) * rows + lax.broadcasted_iota(jnp.int32, (rows, 1), 0)
    hidden_from = jnp.where(at < prefix, 1.0, 0.0)
    lane = lax.broadcasted_iota(jnp.int32, (1, rows), 1)
    fills = []
    for side in range(2):
        places = [(s ^ (2 * side + piece)) * rows + lane for piece in range(half // rows)]
        where = jnp.concatenate(places, axis=1)
        fills.append(jnp.where(where < prefix, 0.0, NEG))
    lane128 = lax.broadcasted_iota(jnp.int32, (rows, 128), 1)
    kept = jnp.zeros((rows, 128), F32)
    outs = []
    for h in range(heads):
        q = mine[:, h * HD : (h + 1) * HD]
        scores = []
        for side, ref in enumerate((qa, qb)):
            keys = ref[0, :, hw + h * HD : hw + (h + 1) * HD]
            scores.append(dot_bt(q, keys) + hidden_from * fills[side])
        top = jnp.maximum(
            jnp.max(scores[0], axis=1, keepdims=True), jnp.max(scores[1], axis=1, keepdims=True)
        )
        sums = jnp.zeros((rows, 1), F32)
        mixed = jnp.zeros((rows, HD), F32)
        for side, ref in enumerate((qa, qb)):
            v = ref[0, :, 2 * hw + h * HD : 2 * hw + (h + 1) * HD]
            e = jnp.exp(scores[side] - top)
            sums = sums + jnp.sum(e, axis=1, keepdims=True)
            e = e.astype(BF16)
            weights[0, h, :, side * half : (side + 1) * half] = e
            mixed = mixed + dot(e, v)
        recip = 1.0 / sums
        kept = jnp.where(lane128 == h, recip, kept)
        outs.append((mixed * recip).astype(BF16))
    recips[0] = kept
    folded = fold(jnp.concatenate(outs, axis=1))
    for n, ref in enumerate((o0, o1)):

        @pl.when(k == n)
        def _(ref=ref):
            ref[0] = folded


def attend_call(meta, base, qa, qb, rows, held=()):
    count, half, cols = qa.shape
    hw = cols // 3
    heads = hw // HD
    keys = 2 * half
    block = (1, rows // 2, 2 * hw)
    return run(
        functools.partial(attend_kernel, base),
        (count, half // rows),
        meta,
        [
            (qa, (1, half, cols), lambda b, k, m: (b, 0, 0)),
            (qb, (1, half, cols), lambda b, k, m: (b, 0, 0)),
        ],
        [((count,) + block[1:], BF16, block, lambda b, k, m: (b, 0, 0)) for _ in range(2)]
        + [
            (
                (count, heads, keys, keys),
                BF16,
                (1, heads, rows, keys),
                lambda b, k, m: (b, 0, base + k, 0),
            ),
            ((count, keys, 128), F32, (1, rows, 128), lambda b, k, m: (b, base + k, 0)),
        ],
        cost=(
            2 * count * heads * keys * keys * HD * 4,
            count * heads * keys * keys,
            count * heads * keys * keys // 2,
        ),
        name="attend",
        held=[(x, 2 + n) for n, x in enumerate(held)],
    )


def back_kernel(meta, qa, qb, weights, recips, o0, o1, o2, o3, g0, g1, g2, g3, out, dk, dv, og, go):
    j = pl.program_id(0)
    rows = o0.shape[1] * 2
    hw = o0.shape[2] // 2
    heads = hw // HD
    half = qa.shape[1]
    place = lax.rem(j, 2) * rows
    scale = HD**-0.5
    for k, (o, g) in enumerate(((o0, g0), (o1, g1), (o2, g2), (o3, g3))):

        @pl.when(j == k)
        def _(o=o, g=g):
            grad = g[0].astype(F32)
            go[...] = unfold(grad)
            og[...] = unfold(grad * o[0].astype(F32))

    @pl.when(j == 0)
    def _():
        dk[...] = jnp.zeros_like(dk)
        dv[...] = jnp.zeros_like(dv)

    mine = jnp.where(j < 2, qa[0, pl.ds(place, rows), :hw], qb[0, pl.ds(place, rows), :hw])
    query_grads = []
    for h in range(heads):
        cols = slice(h * HD, (h + 1) * HD)
        recip = recips[0, :, h : h + 1]
        grad = (go[:, cols] * recip).astype(BF16)
        centre = jnp.sum(og[:, cols], axis=1, keepdims=True) * recip
        q = mine[:, cols]
        dq = jnp.zeros((rows, HD), F32)
        for side, ref in enumerate((qa, qb)):
            k = ref[0, :, hw + h * HD : hw + (h + 1) * HD]
            v = ref[0, :, 2 * hw + h * HD : 2 * hw + (h + 1) * HD]
            e = weights[0, h, :, side * half : (side + 1) * half]
            ds = (e.astype(F32) * (dot_bt(grad, v) - centre)).astype(BF16)
            dq = dq + dot(ds, k)
            span = pl.ds(side * half, half)
            dk[h, span] += dot_at(ds, q)
            dv[h, span] += dot_at(e, grad)
        query_grads.append((dq * scale).astype(BF16))
    out[0, pl.ds(pl.multiple_of(j * rows, rows), rows), :hw] = jnp.concatenate(query_grads, axis=1)

    @pl.when(j == pl.num_programs(0) - 1)
    def _():
        out[0, :, hw : 2 * hw] = jnp.concatenate(
            [dk[h].astype(BF16) for h in range(heads)], axis=1
        )
        out[0, :, 2 * hw :] = jnp.concatenate([dv[h].astype(BF16) for h in range(heads)], axis=1)


def back_call(meta, b, qa, qb, weights, recips, olds, grads):
    _, half, cols = qa.shape
    hw = cols // 3
    heads = hw // HD
    keys = 2 * half
    rows = olds[0].shape[1] * 2
    block = (1,) + olds[0].shape[1:]
    piece = lambda j, m: (b, 0, 0)
    return run(
        back_kernel,
        (keys // rows,),
        meta,
        [
            (qa, (1, half, cols), piece),
            (qb, (1, half, cols), piece),
            (weights, (1, heads, rows, keys), lambda j, m: (b, 0, j, 0)),
            (recips, (1, rows, 128), lambda j, m: (b, j, 0)),
        ]
        + [(x, block, piece) for x in (*olds, *grads)],
        [((1, keys, cols), BF16, (1, keys, cols), lambda j, m: (0, 0, 0))],
        scratch=[
            pltpu.VMEM((heads, keys, HD), F32),
            pltpu.VMEM((heads, keys, HD), F32),
            pltpu.VMEM((rows, hw), F32),
            pltpu.VMEM((rows, hw), F32),
        ],
        cost=(8 * heads * keys * keys * HD * 4, 2 * heads * keys * keys, 0),
        name="attend_back",
    )[0]


def mix_kernel(meta, m0, m1, m2, m3, tokens, w_own, w_other, out_bias, mods, residual, mlp_in, w):
    b = pl.program_id(0)
    s, c, prefix = meta[0], meta[1], meta[4 + b]
    rows, width = tokens.shape[1:]
    hw = m0.shape[2] // 2

    @pl.when(b == 0)
    def _():
        for j in range(4):
            there = pl.ds(pl.multiple_of((s ^ j) * hw, hw), hw)
            own, other = w_own[there], w_other[there]
            even = c == 0
            w[j * hw : (j + 1) * hw, : width // 2] = jnp.where(even, own, other)
            w[j * hw : (j + 1) * hw, width // 2 :] = jnp.where(even, other, own)

    total = tokens[0].astype(F32) + out_bias[...]
    for j, ref in enumerate((m0, m1, m2, m3)):
        total = total + dot(unfold(ref[0]), w[j * hw : (j + 1) * hw])
    residual[0] = total
    normed, _ = standardize(total)
    at = s * rows + lax.broadcasted_iota(jnp.int32, (rows, 1), 0)
    clean = at < prefix
    count = pl.num_programs(0)
    noisy_row, clean_row = mods[pl.ds(b, 1)], mods[pl.ds(count, 1)]
    shift, scale = (
        jnp.where(
            clean,
            clean_row[:, part * width : (part + 1) * width],
            noisy_row[:, part * width : (part + 1) * width],
        )
        for part in range(2)
    )
    mlp_in[0] = (normed * (1.0 + scale) + shift).astype(BF16)


def mix_call(meta, parts, tokens, w_own, w_other, out_bias, mods):
    count, rows, width = tokens.shape
    seq = lambda b, m: (b, 0, 0)
    block = (1, rows, width)
    return run(
        mix_kernel,
        (count,),
        meta,
        [(p, (1,) + p.shape[1:], seq) for p in parts]
        + [(tokens, block, seq), whole(w_own), whole(w_other), whole(out_bias), whole(mods)],
        [
            (tokens.shape, F32, block, seq),
            (tokens.shape, BF16, block, seq),
            out_whole((width, width), BF16),
        ],
        cost=(2 * count * rows * width * width, 12 * count * rows * width, 0),
        name="mix",
    )


def mlp_kernel(
    meta,
    x0,
    x1,
    og0,
    og1,
    up,
    up_bias,
    down,
    mods,
    own_branch,
    own_input,
    other,
    up_here,
    up_away,
    down_here,
    down_away,
    up_bias_grad,
    up_acc,
    down_acc,
):
    p, b = pl.program_id(0), pl.program_id(1)
    count = pl.num_programs(1)
    s, i, prefix = meta[0], meta[3], meta[4 + b]
    rows, width = x0.shape[1:]
    first = p == 0
    x = jnp.where(first, x0[0], x1[0])
    incoming = jnp.where(first, og0[0], og1[0]).astype(F32)
    at = (s ^ p) * rows + lax.broadcasted_iota(jnp.int32, (rows, 1), 0)
    gate = jnp.where(
        at < prefix, mods[pl.ds(count, 1), 2 * width :], mods[pl.ds(b, 1), 2 * width :]
    )
    grad = (incoming * gate).astype(BF16)
    hidden, slope = gelu_both(dot(x, up[...]) + up_bias[...])
    hidden = hidden.astype(BF16)
    branch = dot(hidden, down[...])
    pre = (dot_bt(grad, down[...]) * slope)
    pre_low = pre.astype(BF16)
    back = dot_bt(pre_low, up[...])
    sums = jnp.sum(pre_low.astype(F32), axis=0, keepdims=True)

    @pl.when(first)
    def _():
        own_branch[0] = branch
        own_input[0] = back

    @pl.when(p == 1)
    def _():
        other[0, 0] = branch.astype(BF16)
        other[1, 0] = back.astype(BF16)

    start = jnp.logical_and(first, b == 0)

    @pl.when(start)
    def _():
        up_acc[...] = dot_at(x, pre_low)
        down_acc[...] = dot_at(hidden, grad)
        up_bias_grad[...] = sums

    @pl.when(jnp.logical_not(start))
    def _():
        up_acc[...] += dot_at(x, pre_low)
        down_acc[...] += dot_at(hidden, grad)
        up_bias_grad[...] += sums

    @pl.when(jnp.logical_and(p == 1, b == count - 1))
    def _():
        outer, deep = up_here.shape[0], up_here.shape[1]
        for d in range(2 * outer):
            upper = up_acc[d * deep : (d + 1) * deep].astype(BF16)
            base = d * 2 * deep
            lower = jnp.concatenate(
                [down_acc[base : base + deep], down_acc[base + deep : base + 2 * deep]], axis=1
            ).astype(BF16)

            @pl.when(i == d % 2)
            def _(d=d, upper=upper, lower=lower):
                up_here[d // 2] = upper
                down_here[d // 2] = lower

            @pl.when(i != d % 2)
            def _(d=d, upper=upper, lower=lower):
                up_away[d // 2] = upper
                down_away[d // 2] = lower


def mlp_call(meta, x0, x1, og0, og1, up, up_bias, down, mods, ranks):
    count, rows, width = x0.shape
    hidden = up.shape[1]
    last = count - 1
    block = (1, rows, width)
    first = lambda p, b, m: (jnp.where(p == 0, b, last), 0, 0)
    second = lambda p, b, m: (jnp.where(p == 0, 0, b), 0, 0)
    shared = (ranks // 2, width // ranks, hidden)
    return run(
        mlp_kernel,
        (2, count),
        meta,
        [
            (x0, block, first),
            (x1, block, second),
            (og0, block, first),
            (og1, block, second),
            whole(up),
            whole(up_bias),
            whole(down),
            whole(mods),
        ],
        [
            (x0.shape, F32, block, first),
            (x0.shape, F32, block, first),
            (
                (2,) + x0.shape,
                BF16,
                (2,) + block,
                lambda p, b, m: (0, jnp.where(p == 0, 0, b), 0, 0),
            ),
            out_whole(shared, BF16),
            out_whole(shared, BF16),
            out_whole(shared, BF16),
            out_whole(shared, BF16),
            out_whole((1, hidden), F32),
        ],
        scratch=[pltpu.VMEM((width, hidden), F32), pltpu.VMEM((hidden, width), F32)],
        cost=(24 * count * rows * width * hidden, 20 * count * rows * width, 0),
        name="mlp",
    )


def turn_kernel(
    meta,
    residual,
    out_grad,
    own_branch,
    own_input,
    got,
    down_bias,
    mods,
    m0,
    m1,
    m2,
    m3,
    w,
    block_out,
    resid_grad,
    g0,
    g1,
    g2,
    g3,
    sums,
    biases,
    out_here,
    out_away,
    acc,
):
    b = pl.program_id(0)
    count = pl.num_programs(0)
    s, c, prefix = meta[0], meta[1], meta[4 + b]
    rows, width = residual.shape[1:]
    hw = m0.shape[2] // 2
    resid = residual[0]
    incoming = out_grad[0].astype(F32)
    at = s * rows + lax.broadcasted_iota(jnp.int32, (rows, 1), 0)
    clean = at < prefix
    noisy_row, clean_row = mods[pl.ds(b, 1)], mods[pl.ds(count, 1)]
    scale, gate = (
        jnp.where(
            clean,
            clean_row[:, part * width : (part + 1) * width],
            noisy_row[:, part * width : (part + 1) * width],
        )
        for part in (1, 2)
    )
    branch = own_branch[0] + got[0, 0].astype(F32) + down_bias[...]
    input_two = own_input[0] + got[1, 0].astype(F32)
    block_out[0] = (resid + gate * branch).astype(BF16)
    normed, inverse = standardize(resid)
    grads = incoming + norm_back(input_two * (1.0 + scale), normed, inverse)
    resid_grad[0] = grads
    low = grads.astype(BF16)
    keep = jnp.where(clean, 1.0, 0.0)
    for part, value in enumerate((input_two, input_two * normed, incoming * branch)):
        value = value.astype(BF16).astype(F32)
        cols = slice(part * width, (part + 1) * width)
        everything = jnp.sum(value, axis=0, keepdims=True)
        old = jnp.sum(value * keep, axis=0, keepdims=True)
        sums[0, 0:1, cols] = everything - old
        sums[0, 1:2, cols] = old
    branch_low = (incoming * gate).astype(BF16).astype(F32)
    down_sum = jnp.sum(branch_low, axis=0, keepdims=True)
    out_sum = jnp.sum(low.astype(F32), axis=0, keepdims=True)

    @pl.when(b == 0)
    def _():
        acc[...] = jnp.zeros_like(acc)
        biases[...] = jnp.zeros_like(biases)

    biases[0:1] += down_sum
    biases[1:2] += out_sum
    for j, (m, g) in enumerate(((m0, g0), (m1, g1), (m2, g2), (m3, g3))):
        g[0] = fold(dot_bt(low, w[j * hw : (j + 1) * hw])).astype(BF16)
        acc[j * hw : (j + 1) * hw] += dot_at(unfold(m[0]), low)

    @pl.when(b == count - 1)
    def _():
        for j in range(4):
            here = pl.ds(pl.multiple_of((s ^ j) * hw, hw), hw)
            block = acc[j * hw : (j + 1) * hw].astype(BF16)
            left, right = block[:, : width // 2], block[:, width // 2 :]
            even = c == 0
            out_here[here] = jnp.where(even, left, right)
            out_away[here] = jnp.where(even, right, left)


def turn_call(meta, residual, out_grad, own_branch, own_input, got, down_bias, mods, parts, w):
    count, rows, width = residual.shape
    seq = lambda b, m: (b, 0, 0)
    block = (1, rows, width)
    return run(
        turn_kernel,
        (count,),
        meta,
        [
            (residual, block, seq),
            (out_grad, block, seq),
            (own_branch, block, seq),
            (own_input, block, seq),
            (got, (2,) + block, lambda b, m: (0, b, 0, 0)),
            whole(down_bias),
            whole(mods),
        ]
        + [(p, (1,) + p.shape[1:], seq) for p in parts]
        + [whole(w)],
        [
            (residual.shape, BF16, block, seq),
            (residual.shape, F32, block, seq),
        ]
        + [(p.shape, BF16, (1,) + p.shape[1:], seq) for p in parts]
        + [
            ((count, 2, 3 * width), F32, (1, 2, 3 * width), seq),
            out_whole((8, width), F32),
            out_whole((width, width // 2), BF16),
            out_whole((width, width // 2), BF16),
        ],
        scratch=[pltpu.VMEM((width, width), F32)],
        cost=(4 * count * rows * width * width, 24 * count * rows * width, 0),
        name="turn",
    )


def proj_back_kernel(pieces, do_in, parts, has_carry, has_got, ranks, meta, *refs):
    refs = list(refs)
    xs = [refs.pop(0) for _ in pieces]
    raws = [refs.pop(0) for _ in pieces]
    tables = [(refs.pop(0), refs.pop(0)) for _ in pieces]
    gain, bias, w = refs.pop(0), refs.pop(0), refs.pop(0)
    do_norm = parts > 0
    kept = 2 * do_in + do_norm
    carry = [refs.pop(0) for _ in range(kept)] if has_carry else None
    got = refs.pop(0) if has_got else None
    extra = [refs.pop(0) for _ in range(2)] if ranks else None
    parts = [refs.pop(0) for _ in range(parts)]
    out = refs.pop(0) if ranks else None
    totals = refs
    acc, in_bias = totals[:2] if do_in else (None, None)
    vec = totals[-1] if do_norm else None
    hw = w.shape[1] // 3
    if has_carry:
        for ref, old in zip(totals, carry):
            ref[...] = old[...]
    else:
        for ref in totals:
            ref[...] = jnp.zeros_like(ref)

    for k, (x, raw, (cosine, sine)) in enumerate(zip(xs, raws, tables)):
        normed, _ = standardize(x[0].astype(F32))
        cos, sin = cosine[...], sine[...]
        tiles = []
        for t in range(2 * hw // 128):
            tile = raw[0, :, t * 128 : (t + 1) * 128].astype(F32)
            tiles.append((tile * cos - partner_lanes(tile) * sin).astype(BF16))
        tiles.append(raw[0, :, 2 * hw :])
        grads = jnp.concatenate(tiles, axis=1)
        if do_in:
            attn_input = (normed * gain[...] + bias[...]).astype(BF16)
            acc[...] += dot_at(attn_input, grads)
            in_bias[...] += jnp.sum(grads.astype(F32), axis=0, keepdims=True)
        if do_norm:
            back = dot_bt(grads, w[...])
            vec[0:1] += jnp.sum(back * normed, axis=0, keepdims=True)
            vec[1:2] += jnp.sum(back, axis=0, keepdims=True)
            if has_got and k == 0:
                back = back + got[1, 0].astype(F32)
            if len(parts) == 1:
                parts[0][k, 0] = back.astype(parts[0].dtype)
            else:
                parts[k][0] = back.astype(parts[k].dtype)

    if ranks:
        deep, cols = acc.shape[0] // ranks, acc.shape[1]
        up_bias, biases = extra
        flat = jnp.concatenate(
            [in_bias[...], up_bias[...], vec[0:1], vec[1:2], biases[1:2], biases[0:1]], axis=1
        )
        count = flat.shape[1] // cols
        extra = jnp.concatenate(
            [flat[:, r * cols : (r + 1) * cols] for r in range(count)]
            + [jnp.zeros((EXTRA - count, cols), F32)],
            axis=0,
        ).astype(BF16)
        for k in range(ranks):
            out[k, :deep] = acc[k * deep : (k + 1) * deep].astype(BF16)
            out[k, deep:] = extra


def proj_back_call(
    meta,
    b,
    pieces,
    xs,
    raw,
    gain,
    bias,
    w,
    cosine,
    sine,
    dtypes,
    carry=(),
    got=None,
    do_in=True,
    ranks=0,
    extra=(),
):
    _, rows, width = xs[0].shape
    cols = w.shape[1]
    do_norm = bool(dtypes)
    ins = [(x, (1, rows, width), lambda i, m: (b, 0, 0)) for x in xs]
    ins += [(raw, (1, rows, cols), lambda i, m, j=j: (0, j, 0)) for j in pieces]
    for j in pieces:
        ins += [(t, (rows, 128), lambda i, m, j=j: (j, 0)) for t in (cosine, sine)]
    ins += [whole(gain), whole(bias), whole(w)]
    ins += [whole(v) for v in carry]
    if got is not None:
        ins.append(whole(got))
    ins += [whole(x) for x in extra]
    n = len(pieces)
    lead = (n,) if len(dtypes) == 1 else ()
    outs = [out_whole(lead + (1, rows, width), dtype) for dtype in dtypes]
    totals = [((width, cols), F32), ((1, cols), F32)] * do_in + [((8, width), F32)] * do_norm
    scratch = []
    if ranks:
        scratch = [pltpu.VMEM(shape, dtype) for shape, dtype in totals]
        outs.append(out_whole((ranks, width // ranks + EXTRA, cols), BF16))
    else:
        outs += [out_whole(*entry) for entry in totals]
    return run(
        functools.partial(
            proj_back_kernel,
            tuple(pieces),
            do_in,
            len(dtypes),
            bool(carry),
            got is not None,
            ranks,
        ),
        (1,),
        meta,
        ins,
        outs,
        scratch=scratch,
        cost=(2 * (do_in + do_norm) * n * rows * width * cols, 6 * n * rows * width, 0),
        name="proj_back",
    )


def last_kernel(meta, tokens, resid_grad, mine, got, across, gain, out):
    normed, inverse = standardize(tokens[0].astype(F32))
    grad = mine[0] + got[0, 0].astype(F32) + across[0].astype(F32)
    out[0] = resid_grad[0] + norm_back(grad * gain[...], normed, inverse)


def last_call(meta, b, tokens, resid_grad, mine, got, across, gain, held):
    _, rows, width = tokens.shape
    seq = lambda i, m: (b, 0, 0)
    one = lambda i, m: (0, 0, 0)
    block = (1, rows, width)
    return run(
        last_kernel,
        (1,),
        meta,
        [
            (tokens, block, seq),
            (resid_grad, block, seq),
            (mine, block, one),
            (got, (1,) + block, lambda i, m: (0, 0, 0, 0)),
            (across, block, one),
            whole(gain),
        ],
        [(tokens.shape, F32, block, seq)],
        cost=(0, 20 * rows * width, 0),
        name="last",
        held=[(x, 0) for x in held],
    )[0]


def pack_in_kernel(meta, proj_in, vec, out):
    s = meta[0]
    deep, width = proj_in.shape[0], proj_in.shape[1] // 3
    cols = out.shape[1]
    hw = cols // 3
    for k in range(width // hw):

        @pl.when(s == k)
        def _(k=k):
            for t in range(3):
                start = t * width + k * hw
                out[:deep, t * hw : (t + 1) * hw] = proj_in[:, start : start + hw]

    out[deep:] = jnp.zeros((out.shape[0] - deep, cols), BF16)
    size = vec.shape[1]
    for r in range(pl.cdiv(size, cols)):
        width_r = min(cols, size - r * cols)
        out[deep + r : deep + r + 1, :width_r] = vec[:, r * cols : r * cols + width_r]


def place_in_kernel(sizes, meta, *refs):
    outer = len(refs) - 13
    pieces, odd, rows, refs = refs[:outer], refs[outer], refs[outer + 1], refs[outer + 2 :]
    w, gain, bias, in_b, out_bias, ada_bias, up_b, down_bias, chosen, wanted, table = refs
    ranks = 2 * outer
    s, c, d = meta[0], meta[1], meta[2]
    deep, cols = w.shape[0] // ranks, w.shape[1]
    hw = cols // 3
    for m in range(ranks):
        piece = odd.at[m // 2] if m % 2 else pieces[m // 2]
        owner = d ^ m
        w[pl.ds(pl.multiple_of(owner * deep, deep), deep)] = piece[:deep]
        table[pl.ds(owner, 1)] = piece[deep:].astype(F32)[None]
    used = -(-sum(sizes) // cols)
    flat = [
        jnp.concatenate([table[k, r : r + 1] for r in range(used)], axis=1) for k in range(ranks)
    ]
    full, start = [], 0
    for size in sizes:
        full.append([f[:, start : start + size] for f in flat])
        start += size
    steps = [high * 32.0 + low for high, low in zip(full[7], full[8])]
    full = [jnp.concatenate(x, axis=1) for x in full]
    gain[...], bias[...], out_bias[...], ada_bias[...], down_bias[...] = (
        full[0],
        full[1],
        full[3],
        full[4],
        full[6],
    )
    width = w.shape[0]
    half = sizes[5] // 2
    for k in range(width // hw):

        @pl.when(s == k)
        def _(k=k):
            in_b[...] = jnp.concatenate(
                [full[2][:, t * width + k * hw : t * width + (k + 1) * hw] for t in range(3)], axis=1
            )

    for k in range(2):

        @pl.when(c == k)
        def _(k=k):
            up_b[...] = jnp.concatenate(
                [full[5][:, (2 * n + k) * half : (2 * n + k + 1) * half] for n in range(ranks)],
                axis=1,
            )

    want = jnp.concatenate([x for step in steps for x in (step, jnp.zeros((1, 1), F32))], axis=1)
    wanted[...] = want
    at = d * rows.shape[0] + lax.broadcasted_iota(jnp.int32, (rows.shape[0], 1), 0)
    picked = dot_at((at.astype(F32) == want).astype(BF16), rows[...]).astype(BF16)
    part = rows.shape[1] // ranks
    for k in range(ranks):
        chosen[k] = picked[:, k * part : (k + 1) * part]


def pack_rest_kernel(meta, up, down, proj_out, out):
    c = meta[1]
    deep = up.shape[0]
    width = down.shape[1]
    half = down.shape[0] // 2
    ff = up.shape[1] // 2
    for k in range(2):

        @pl.when(c == k)
        def _(k=k):
            for d in range(ff // half):
                out[:, d * half : (d + 1) * half] = up[:, (2 * d + k) * half : (2 * d + k + 1) * half]
            out[:, ff : ff + width] = down[k * half : k * half + deep]
            out[:, ff + width : ff + 2 * width] = down[k * half + deep : (k + 1) * half]
            out[:, ff + 2 * width :] = proj_out[:, k * width // 2 : (k + 1) * width // 2]


def place_rest_kernel(meta, *refs):
    *pieces, up, down, out = refs
    d = meta[2]
    deep = up.shape[0] // len(pieces)
    ff, width = up.shape[1], down.shape[1]
    for m, piece in enumerate(pieces):
        owner = d ^ m
        base = pl.multiple_of(owner * deep, deep)
        up[pl.ds(base, deep)] = piece[:, :ff]
        out[pl.ds(base, deep)] = piece[:, ff + 2 * width :]
        base = pl.multiple_of(owner * (2 * deep), deep)
        down[pl.ds(base, deep)] = piece[:, ff : ff + width]
        base = pl.multiple_of(owner * (2 * deep) + deep, deep)
        down[pl.ds(base, deep)] = piece[:, ff + width : ff + 2 * width]


def half_kernel(meta, here, came, *outs):
    o = meta[2] // 2
    for m, out in enumerate(outs):
        at = pl.ds(o ^ m, 1)
        out[...] = (here[at].astype(F32) + came[at].astype(F32))[0].astype(BF16)


def split_kernel(meta, here, came, out):
    out[...] = (here[...].astype(F32) + came[...].astype(F32)).astype(BF16)


def total(refs):
    result = 0.0
    for ref in refs:
        for k in range(ref.shape[0] if len(ref.shape) == 3 else 1):
            result = result + (ref[k] if len(ref.shape) == 3 else ref[...]).astype(F32)
    return result


def gather_kernel(counts, meta, *refs):
    *refs, out = refs
    start, place = 0, 0
    for n in counts:
        value = total(refs[start : start + n])
        out[:, place : place + value.shape[1]] = value.astype(BF16)
        start, place = start + n, place + value.shape[1]


def gather_call(meta, groups):
    refs = [x for g in groups for x in g]
    shape = (groups[0][0].shape[-2], sum(g[0].shape[-1] for g in groups))
    return run(
        functools.partial(gather_kernel, tuple(len(g) for g in groups)),
        (1,),
        meta,
        [whole(x) for x in refs],
        [out_whole(shape, BF16)],
        cost=(0, 2 * sum(x.size for x in refs), 0),
        name="gather",
    )[0]


def close_rest_kernel(meta, own, across, pair, up, down, out):
    c = meta[1]
    deep = own.shape[0]
    width = out.shape[1]
    half = down.shape[0] // 2
    ff = up.shape[1] // 2
    mine = own[...].astype(F32) + across[...].astype(F32)
    other = pair[0].astype(F32) + pair[1].astype(F32)
    for k in range(2):
        value = jnp.where(c == k, mine, other)
        for d in range(ff // half):
            up[:, (2 * d + k) * half : (2 * d + k + 1) * half] = value[:, d * half : (d + 1) * half]
        down[k * half : k * half + deep] = value[:, ff : ff + width]
        down[k * half + deep : (k + 1) * half] = value[:, ff + width : ff + 2 * width]
        out[:, k * width // 2 : (k + 1) * width // 2] = value[:, ff + 2 * width :]


def close_in_kernel(ranks, meta, own, across, pair, w, gain, bias, in_bias, out_bias, up_bias, down_bias, held):
    s, d = meta[0], meta[2]
    deep, width = w.shape[0], w.shape[1] // 3
    cols = own.shape[1]
    hw = cols // 3
    held[pl.ds(s, 1)] = own[...].astype(F32)[None]
    held[pl.ds(s ^ 2, 1)] = across[...].astype(F32)[None]
    held[pl.ds(s ^ 1, 1)] = pair[0].astype(F32)[None]
    held[pl.ds(s ^ 3, 1)] = pair[1].astype(F32)[None]
    for k in range(4):
        for t in range(3):
            w[:, t * width + k * hw : t * width + (k + 1) * hw] = held[k, :deep, t * hw : (t + 1) * hw]
    rows = [
        jnp.concatenate([held[k, deep + r : deep + r + 1] for r in range(EXTRA)], axis=1)
        for k in range(4)
    ]
    biases = jnp.concatenate(
        [rows[k][:, t * hw : (t + 1) * hw] for t in range(3) for k in range(4)], axis=1
    )
    ff = 2 * width
    ups = [rows[0][:, cols : cols + ff] + rows[2][:, cols : cols + ff]]
    ups.append(rows[1][:, cols : cols + ff] + rows[3][:, cols : cols + ff])
    rest = rows[0] + rows[1] + rows[2] + rows[3]
    rest = rest[:, cols + ff :]
    part, third, half = width // ranks, 3 * width // ranks, ff // ranks
    for k in range(ranks):

        @pl.when(d == k)
        def _(k=k):
            for n, out in enumerate((gain, bias, out_bias, down_bias)):
                out[...] = rest[:, n * width + k * part : n * width + (k + 1) * part]
            in_bias[...] = biases[:, k * third : (k + 1) * third]
            up_bias[...] = jnp.concatenate([u[:, k * half : (k + 1) * half] for u in ups], axis=1)


def shards(
    tokens,
    prefix_len,
    timestep,
    norm_gain,
    norm_bias,
    proj_in,
    proj_in_bias,
    proj_out,
    proj_out_bias,
    time_table,
    ada_weight,
    ada_bias,
    mlp_up,
    mlp_up_bias,
    mlp_down,
    mlp_down_bias,
    out_grad,
):
    count, local_len, width = tokens.shape
    members = lax.axis_size("seq")
    ranks = lax.axis_size("dp")
    s = lax.axis_index("seq")
    d = lax.axis_index("dp")
    hw = H // members * HD
    deep = proj_in.shape[0]
    half_ff = mlp_down.shape[0] // 2
    ff = ranks * half_ff
    half_out = width // 2
    meta = jnp.concatenate([jnp.stack([s, s % 2, d, d % 2]).astype(jnp.int32), prefix_len])

    tok_x = seq_swap(tokens, 2)

    vectors = [
        norm_gain,
        norm_bias,
        proj_in_bias,
        proj_out_bias,
        ada_bias,
        mlp_up_bias,
        mlp_down_bias,
        (timestep // 32).astype(BF16),
        (timestep % 32).astype(BF16),
    ]
    sizes = tuple(v.shape[0] for v in vectors)
    pack_in = run(
        pack_in_kernel,
        (1,),
        meta,
        [whole(proj_in), whole(jnp.concatenate(vectors)[None])],
        [out_whole((deep + EXTRA, 3 * hw), BF16)],
        name="pack_in",
    )[0]
    in_even, in_odd = dp_collect(pack_in)
    tok_c = seq_swap(after(tokens, pack_in), 1)
    pack_rest = run(
        pack_rest_kernel,
        (1,),
        meta,
        [whole(after(mlp_up, pack_in)), whole(mlp_down), whole(proj_out)],
        [out_whole((deep, ff + 2 * width + half_out), BF16)],
        name="pack_rest",
    )[0]
    in_odd = after(in_odd, pack_rest)
    kinds = count + 1
    in_w, gain, bias, in_b, out_bias, ada_bias_full, up_b, down_bias, chosen, wanted = run(
        functools.partial(place_in_kernel, sizes),
        (1,),
        meta,
        [whole(x) for x in (*in_even, in_odd, time_table)],
        [
            out_whole((width, 3 * hw), BF16),
            out_whole((1, width), F32),
            out_whole((1, width), F32),
            out_whole((1, 3 * hw), F32),
            out_whole((1, width), F32),
            out_whole((1, 3 * width), F32),
            out_whole((1, ff), F32),
            out_whole((1, width), F32),
            out_whole((ranks, ranks * kinds, width // ranks), BF16),
            out_whole((1, ranks * kinds), F32),
        ],
        scratch=[pltpu.VMEM((ranks, EXTRA, 3 * hw), F32)],
        name="place_in",
    )
    chosen_got = dp_turn(chosen)

    outer = ranks // 2
    early = max(1, outer // 4)
    soon = after(pack_rest, in_even)
    later = after(pack_rest, in_odd)
    rest_even = [pack_rest]
    rest_even += [dp_swap(soon if m <= early else later, 2 * m) for m in range(1, outer)]
    rest_odd = [dp_swap(soon, 1)]

    offsets = jnp.arange(local_len, dtype=jnp.int32)
    positions = jnp.concatenate([(s ^ j) * local_len + offsets for j in range(members)]).astype(F32)
    half_width = HD // 2
    frequency = jnp.exp(jnp.arange(half_width, dtype=F32) * (-math.log(10000.0) / half_width))
    angles = positions[:, None] * frequency[None, :]
    cosine, sine = jnp.cos(angles), jnp.sin(angles)
    cosine = jnp.concatenate([cosine] * 4, axis=1)
    sine = jnp.concatenate([-sine, sine] * 2, axis=1)

    one, two = slice(1, 1 + early), slice(1 + early, 1 + 2 * early)
    three = slice(1 + 2 * early, outer)
    qkv_near = qkv_call(meta, 0, tokens, tok_c, gain, bias, in_w, in_b, cosine, sine)
    rest_odd += [dp_swap(piece, 1) for piece in rest_even[one]]
    tok_x = after(tok_x, qkv_near)
    tok_d = seq_swap(tok_x, 1)
    embedded = jnp.sum(after(chosen_got, qkv_near).astype(F32), axis=0)
    activated = jax.nn.silu(embedded).astype(BF16)
    mod_parts = dot(activated, ada_weight).reshape(ranks, kinds, 3 * width)
    mod_got = dp_turn(mod_parts)
    og_other = seq_swap(after(out_grad, qkv_near), 1)
    qkv_far = qkv_call(
        meta,
        2,
        tok_x,
        tok_d,
        gain,
        bias,
        in_w,
        in_b,
        after(cosine, mod_parts, rest_even[one], rest_odd[0]),
        sine,
    )
    near_again, rest_even[two] = after((qkv_near, rest_even[two]), qkv_far, og_other)
    rest_odd += [dp_swap(piece, 1) for piece in rest_even[two]]
    mixed_2, mixed_3, weights, recips = attend_call(meta, 2, near_again, qkv_far, local_len)
    across_2, across_3 = seq_swap(mixed_2, 2), seq_swap(mixed_3, 3)
    near_again = after(qkv_near, mixed_2, rest_odd[one])
    mixed_0, mixed_1, weights, recips = attend_call(
        meta, 0, near_again, qkv_far, local_len, (weights, recips)
    )
    mixed = [mixed_0, mixed_1, mixed_2, mixed_3]
    mixed_own = [mixed_0, seq_swap(mixed_1, 1), across_2, across_3]
    rest_even[three] = after(rest_even[three], mixed_0)
    rest_odd += [dp_swap(piece, 1) for piece in rest_even[three]]
    mods = jnp.sum(after(mod_got, mixed_0), axis=0) + ada_bias_full
    up_w, down_w, out_own = run(
        place_rest_kernel,
        (1,),
        meta,
        [whole(x) for pair in zip(rest_even, rest_odd) for x in pair],
        [
            out_whole((width, ff), BF16),
            out_whole((ff, width), BF16),
            out_whole((width, half_out), BF16),
        ],
        name="place_rest",
    )
    out_other = seq_swap(out_own, 1)

    residual, mlp_own, out_rel = mix_call(
        meta, mixed_own, tokens, out_own, out_other, out_bias, mods
    )
    mlp_other = seq_swap(mlp_own, 1)
    own_branch, own_input, other, up_here, up_away, down_here, down_away, up_bias_part = mlp_call(
        meta, mlp_own, mlp_other, out_grad, og_other, up_w, up_b, down_w, mods, ranks
    )
    got = seq_swap(other, 1)
    up_came = dp_swap(up_away, 1)
    down_came = dp_swap(down_away, 1)
    block_out, resid_grad, *others = turn_call(
        meta, residual, out_grad, own_branch, own_input, got, down_bias, mods, mixed_own, out_rel
    )
    mixed_grads, (row_sums, biases, out_here, out_away) = others[:4], others[4:]
    head_grads = [mixed_grads[0]] + [seq_swap(mixed_grads[j], j) for j in range(1, members)]

    def halves(here, came):
        pieces = run(
            half_kernel,
            (1,),
            meta,
            [whole(here), whole(came)],
            [out_whole(here.shape[1:], BF16) for _ in range(ranks // 2)],
            name="half",
        )
        return pieces[0], [pieces[0]] + [dp_swap(p, 2 * m) for m, p in enumerate(pieces) if m]

    out_came = seq_swap(out_away, 1)
    row_grad = jnp.concatenate([row_sums[:, 0], jnp.sum(row_sums[:, 1], axis=0)[None]], axis=0)
    row_grad = row_grad + seq_swap(row_grad, 1)
    out_sum = run(
        split_kernel,
        (1,),
        meta,
        [whole(out_here), whole(after(out_came, row_grad))],
        [out_whole(out_here.shape, BF16)],
        name="split",
    )[0]
    out_got = dp_turn(out_sum.reshape(ranks, deep, half_out))
    up_half, up_got = halves(after(up_here, out_sum), up_came)

    shared = (gain, bias, in_w, cosine, sine)
    near, far = (tok_c, tok_d), (tok_x, tokens)

    def attend_back(b, *others):
        return back_call(
            meta, b, after(qkv_near, *others), qkv_far, weights, recips, mixed, head_grads
        )

    row_away = seq_swap(row_grad, 2)
    raw_0 = attend_back(0, up_half, row_grad)
    row_grad = row_grad + after(row_away, raw_0)
    rows_got = dp_all(row_grad)
    sent, *carry = proj_back_call(meta, 0, (1, 3), near, after(raw_0, row_grad), *shared, (BF16,))
    came_0 = seq_swap(sent, 1)
    up_sum = gather_call(meta, [after(up_got, sent)])
    down_half, down_got = halves(after(down_here, up_sum), down_came)
    out_got = after(out_got, down_half)

    raw_1 = attend_back(1, sent, down_half, out_got)
    across, mine_0, *carry = proj_back_call(
        meta, 0, (2, 0), far, after(raw_0, raw_1), *shared, (BF16, F32), carry, came_0
    )
    across_0 = seq_swap(across, 2)
    sent, *carry = proj_back_call(
        meta, 1, (1, 3), near, after(raw_1, across), *shared, (BF16,), carry
    )
    came_1 = seq_swap(sent, 1)

    all_rows = after(rows_got, sent).reshape(ranks * kinds, 3 * width)
    exact = functools.partial(lax.dot_general, precision=HIGHEST, preferred_element_type=F32)
    act_rows_grad = exact(all_rows, ada_weight.astype(F32), (((1,), (1,)), ((), ())))
    embed_grad = jax.vjp(jax.nn.silu, embedded)[1](act_rows_grad)[0]
    embed_got = dp_all(embed_grad)
    rest_sum = gather_call(meta, [(up_sum,), after(down_got, sent), (out_got,)])
    across, mine_1, *carry = proj_back_call(
        meta, 1, (2, 0), far, after(raw_1, rest_sum, embed_grad), *shared, (BF16, F32), carry, came_1
    )
    across_1 = seq_swap(across, 2)
    rest_x = seq_swap(after(rest_sum, across), 2)
    tokens_grad = last_call(
        meta, 0, tokens, after(resid_grad, across), mine_0, came_0, across_0, gain, ()
    )
    raw_2 = attend_back(2, tokens_grad)
    sent, *carry = proj_back_call(meta, 2, (1, 3), near, raw_2, *shared, (BF16,), carry)
    came_2 = seq_swap(sent, 1)
    tokens_grad = last_call(
        meta, 1, tokens, after(resid_grad, sent), mine_1, came_1, across_1, gain, (tokens_grad,)
    )
    across, mine_2, in_sent = proj_back_call(
        meta,
        2,
        (2, 0),
        far,
        after(raw_2, tokens_grad),
        *shared,
        (BF16, F32),
        carry,
        came_2,
        True,
        ranks,
        (up_bias_part, biases),
    )
    across_2 = seq_swap(across, 2)
    in_got = dp_turn(in_sent)
    rest_x = after(rest_x, in_sent)
    rest_pair = seq_swap(jnp.stack([rest_sum, rest_x]), 1)
    all_rows = after(all_rows, in_sent)
    ada_bias_grad = lax.dynamic_slice_in_dim(
        jnp.sum(all_rows, axis=0), d * ada_bias.shape[0], ada_bias.shape[0], 0
    )
    ada_grad = exact(activated.astype(F32), all_rows, (((0,), (0,)), ((), ())))
    table_at = d * time_table.shape[0] + jnp.arange(time_table.shape[0], dtype=jnp.int32)
    selector = (table_at.astype(F32)[:, None] == wanted).astype(F32)
    embed_all = after(embed_got, in_sent).transpose(1, 0, 2).reshape(ranks * kinds, width)
    table_grad = exact(selector, embed_all, (((1,), (0,)), ((), ())))
    up_final, down_final, out_final = run(
        close_rest_kernel,
        (1,),
        meta,
        [whole(x) for x in (rest_sum, rest_x, rest_pair)],
        [
            out_whole(mlp_up.shape, F32),
            out_whole(mlp_down.shape, F32),
            out_whole(proj_out.shape, F32),
        ],
        name="close_rest",
    )

    in_sum = gather_call(meta, [(after(in_got, up_final, table_grad, ada_grad),)])
    in_x = seq_swap(in_sum, 2)
    tokens_grad = last_call(
        meta, 2, tokens, after(resid_grad, in_sum), mine_2, came_2, across_2, gain, (tokens_grad,)
    )
    in_pair = seq_swap(jnp.stack([in_sum, after(in_x, tokens_grad)]), 1)
    part, third, ff_part = width // ranks, 3 * width // ranks, 4 * width // ranks
    in_final, gain_f, bias_f, in_bias_f, out_bias_f, up_bias_f, down_bias_f = run(
        functools.partial(close_in_kernel, ranks),
        (1,),
        meta,
        [whole(x) for x in (in_sum, in_x, in_pair)],
        [
            out_whole(proj_in.shape, F32),
            out_whole((1, part), F32),
            out_whole((1, part), F32),
            out_whole((1, third), F32),
            out_whole((1, part), F32),
            out_whole((1, ff_part), F32),
            out_whole((1, part), F32),
        ],
        scratch=[pltpu.VMEM((members, deep + EXTRA, 3 * hw), F32)],
        name="close_in",
    )
    return (
        block_out,
        tokens_grad,
        gain_f[0],
        bias_f[0],
        in_final,
        in_bias_f[0],
        out_final,
        out_bias_f[0],
        table_grad,
        ada_grad,
        ada_bias_grad,
        up_final,
        up_bias_f[0],
        down_final,
        down_bias_f[0],
    )


def solution(mesh):
    rows = P("dp", None)
    vector = P("dp")
    stream = P("dp", "seq", None)
    in_specs = (
        stream,
        vector,
        vector,
        vector,
        vector,
        rows,
        vector,
        rows,
        vector,
        rows,
        rows,
        vector,
        rows,
        vector,
        rows,
        vector,
        stream,
    )
    out_specs = (
        stream,
        stream,
        vector,
        vector,
        rows,
        vector,
        rows,
        vector,
        rows,
        rows,
        vector,
        rows,
        vector,
        rows,
        vector,
    )
    return jax.shard_map(shards, mesh=mesh, in_specs=in_specs, out_specs=out_specs, check_vma=False)
```

time: 715 us -> 506 us (0.71)
  Pallas kernels: 0 us -> 243 us
  matrix products: 202 us -> 3.28 us
  other arithmetic: 162 us -> 12.7 us
  local copies, waits for them, and re-layouts: 148 us -> 18.2 us
  waiting for transfers between devices: 81.6 us -> 136 us
  starting transfers between devices: 107 us -> 82 us
    pallas_call x0 -> x31, Pallas kernels: none -> 243 us  [run(): pl.pallas_call(kernel, grid_spec=pltpu.PrefetchScalarGridSpec(num_scalar_...]
    dot_general x34 -> x3, matrix products: 161 us -> 3.09 us  [the longest x1 1.48 us: shards(): ada_grad = exact(activated.astype(F32), all_rows, (((0,), (0,)), ((), ())))]
    all_to_all x6, waiting for transfers between devices: 0.02 us -> 52.4 us  [dp_turn(): lax.all_to_all(value, 'dp', split_axis=0, concat_axis=0, tiled=True, axis...]
    convert_element_type x21 -> x3, other arithmetic: 52.5 us -> 0.73 us  [the longest x1 0.72 us: shards(): (timestep % 32).astype(BF16)]
    reduce_sum x16 -> x2, other arithmetic: 51.5 us -> 0.07 us  [the longest x1 0.05 us: shards(): mods = jnp.sum(after(mod_got, mixed_0), axis=0) + ada_bias_full]
    dot_general x6 -> x1, matrix products: 40.6 us -> 0.19 us  [dot(): return jnp.dot(left, right, preferred_element_type=F32)]
    ppermute x44 -> x19, starting transfers between devices: 66.4 us -> 31.2 us  [dp_swap(): lax.ppermute(value, 'dp', [(d, d ^ mask) for d in range(lax.axis_size('dp...]
    reshape x19 -> x3, local copies, waits for them, and re-layouts: 28.1 us -> 1.01 us  [the longest x1 0.81 us: shards(): mod_parts = dot(activated, ada_weight).reshape(ranks, kinds, 3 * width)]
  transfers between devices with their start and end apart: 79 -> 51, of which waited for: 17 -> 17; matrix products, arithmetic and copies ran while one was open for 65% -> 3% of each run, Pallas kernels for 0% -> 31%
where the time goes in v2:
time: 506 us; the launch traced here: 496 us
  Pallas kernels  243 us (48%)
  waiting for transfers between devices  136 us (27%)
  starting transfers between devices  82 us (16%)
  local copies, waits for them, and re-layouts  18.2 us (4%)
  other arithmetic  12.7 us (3%)
    pallas_call x31, Pallas kernels, run(): pl.pallas_call(kernel, grid_spec=pltpu.PrefetchScalarGridSpec(num_scalar_...  243 us
    ppermute x19, waiting for transfers between devices, dp_swap(): lax.ppermute(value, 'dp', [(d, d ^ mask) for d in range(lax.axis_size('dp...  59.3 us
    all_to_all x6, waiting for transfers between devices, dp_turn(): lax.all_to_all(value, 'dp', split_axis=0, concat_axis=0, tiled=True, axis...  52.4 us
    all_to_all x6, starting transfers between devices, dp_turn(): lax.all_to_all(value, 'dp', split_axis=0, concat_axis=0, tiled=True, axis...  34.8 us
    ppermute x19, starting transfers between devices, dp_swap(): lax.ppermute(value, 'dp', [(d, d ^ mask) for d in range(lax.axis_size('dp...  31.2 us
    ppermute x26, waiting for transfers between devices, seq_swap(): lax.ppermute(value, 'seq', [(s, s ^ mask) for s in range(lax.axis_size('s...  24.4 us
    ppermute x26, starting transfers between devices, seq_swap(): lax.ppermute(value, 'seq', [(s, s ^ mask) for s in range(lax.axis_size('s...  16 us
  transfers between devices with their start and end apart: 51, of which 17 were waited for; matrix products, arithmetic and copies ran while one was open for 3% of the time, Pallas kernels for 31%

profile of v2, /device:TPU:0, one launch (start us, length us, event | category | flops | bytes accessed | tf_op | source)
XLA Modules:
  0.0 496.4 jit_solution(12497614543059078563)
XLA Ops:
  1.4 4.8 concatenate.23
  8.1 2.5 pack_in.1.refs_0_
  10.6 3.0 collective-permute-start.1
  13.6 2.6 collective-permute-start.2
  16.2 1.7 collective-permute-start.6
  19.5 8.0 %collective-permute-done.2.refs_2_ = bf16[112,576]{1,0:T(8,128)(2,1)S(1)} collective-permute-done((bf16[112,576]{1,0:T(8,128)(2,1)}, bf16[112,576]{1,0:T(8,128)(2,1)S(1)}, u32[]{:S(2)}, u32[]{:S(2)}) %collective-permute-start.2) | collective-permute-done | bytes 129056 | tf_op jit(solution)/shard_map/ppermute | solution.py:81
  28.2 1.8 pad_maximum_fusion.1
  31.6 2.9 pack_rest.1.refs_0_
  34.5 1.9 fusion
  39.0 3.6 collective-permute-done.4.refs_4_
  42.6 3.5 place_in.1
  46.2 8.4 %qkv.2.qa.refs_0_ = bf16[3,512,576]{2,1,0:T(8,128)(2,1)} custom-call(s32[7]{0:T(128)} %concatenate.22.meta, bf16[3,256,768]{2,1,0:T(8,128)(2,1)} %refs_0_.3, bf16[3,256,768]{2,1,0:T(8,128)(2,1)} %collective-permute-done.x1.refs_0_, f32[1,768]{1,0:T(1,128)} %get-tuple-element.148.gain.refs_8_.refs_5_, f32[1,768]{1,0:T(1,128)} %get-tuple-element.149.bias.refs_9_, ...), custom_call_target="tpu_custom_call" | custom-call | flops 1358954496 | bytes 5898240 | tf_op jit(solution)/shard_map/qkv/pallas_call | solution.py:118
  55.2 3.6 collective-permute-start.8
  61.5 3.4 all-to-all-start
  64.8 22.5 %collective-permute-done.8.refs_2_ = bf16[96,3456]{1,0:T(8,128)(2,1)} collective-permute-done((bf16[96,3456]{1,0:T(8,128)(2,1)}, bf16[96,3456]{1,0:T(8,128)(2,1)}, u32[]{:S(2)}, u32[]{:S(2)}) %collective-permute-start.8) | collective-permute-done | bytes 663584 | tf_op jit(solution)/shard_map/ppermute | solution.py:81
  87.3 2.5 collective-permute-start.11
  89.8 3.6 all-to-all-done
  94.4 2.6 collective-permute-start.16
  97.1 8.4 %qkv.3.qb.refs_1_ = bf16[3,512,576]{2,1,0:T(8,128)(2,1)} custom-call(s32[7]{0:T(128)} %concatenate.22.meta, bf16[3,256,768]{2,1,0:T(8,128)(2,1)} %copy-done.1, bf16[3,256,768]{2,1,0:T(8,128)(2,1)} %collective-permute-done.7.x1.refs_1_, f32[1,768]{1,0:T(1,128)} %get-tuple-element.148.gain.refs_8_.refs_5_, f32[1,768]{1,0:T(1,128)} %get-tuple-element.149.bias.refs_9_, ...), custom_call_target="tpu_custom_call" | custom-call | flops 1358954496 | bytes 5898240 | tf_op jit(solution)/shard_map/qkv/pallas_call | solution.py:118
  105.5 14.3 %attend.2 = (bf16[3,128,384]{2,1,0:T(8,128)(2,1)}, bf16[3,128,384]{2,1,0:T(8,128)(2,1)}, bf16[3,3,1024,1024]{3,2,1,0:T(8,128)(2,1)}, f32[3,1024,128]{2,1,0:T(8,128)}) custom-call(s32[7]{0:T(128)} %concatenate.22.meta, bf16[3,512,576]{2,1,0:T(8,128)(2,1)} %qkv.2.qa.refs_0_, bf16[3,512,576]{2,1,0:T(8,128)(2,1)} %qkv.3.qb.refs_1_), custom_call_target="tpu_custom_call" | custom-call | flops 4831838208 | bytes 9437184 | tf_op jit(solution)/shard_map/attend/pallas_call | solution.py:118
  119.9 14.5 %attend.3 = (bf16[3,128,384]{2,1,0:T(8,128)(2,1)}, bf16[3,128,384]{2,1,0:T(8,128)(2,1)}, bf16[3,3,1024,1024]{3,2,1,0:T(8,128)(2,1)}, f32[3,1024,128]{2,1,0:T(8,128)}) custom-call(s32[7]{0:T(128)} %concatenate.22.meta, bf16[3,512,576]{2,1,0:T(8,128)(2,1)} %qkv.2.qa.refs_0_, ...), custom_call_target="tpu_custom_call", output_to_operand_aliasing={{2}: (3, {}), {3}: (4, {})} | custom-call | flops 4831838208 | bytes 9437184 | tf_op jit(solution)/shard_map/attend/pallas_call | solution.py:118
  136.4 3.6 all-to-all-start.1
  141.7 25.6 %all-to-all-done.1 = f32[8,4,2304]{2,1,0:T(4,128)S(1)} async-done(((f32[8,4,2304]{2,1,0:T(4,128)}), f32[8,4,2304]{2,1,0:T(4,128)S(1)}, u32[]{:S(2)}, u32[]{:S(2)}) %all-to-all-start.1) | async-done | bytes 294944 | tf_op jit(solution)/shard_map/all_to_all | solution.py:99
  167.3 1.7 collective-permute-start.14
  169.0 5.9 %place_rest.1 = (bf16[768,1536]{1,0:T(8,128)(2,1)}, bf16[1536,768]{1,0:T(8,128)(2,1)}, bf16[768,384]{1,0:T(8,128)(2,1)}) custom-call(s32[7]{0:T(128)} %concatenate.22.meta, bf16[96,3456]{1,0:T(8,128)(2,1)} %pack_rest.1.refs_0_, bf16[96,3456]{1,0:T(8,128)(2,1)} %collective-permute-done.9.refs_1_, bf16[96,3456]{1,0:T(8,128)(2,1)} %collective-permute-done.8.refs_2_, ...), custom_call_target="tpu_custom_call" | custom-call | tf_op jit(solution)/shard_map/place_rest/pallas_call | solution.py:118
  177.2 6.4 %mix.1 = (f32[3,256,768]{2,1,0:T(8,128)}, bf16[3,256,768]{2,1,0:T(8,128)(2,1)}, bf16[768,768]{1,0:T(8,128)(2,1)}) custom-call(s32[7]{0:T(128)} %concatenate.22.meta, bf16[3,128,384]{2,1,0:T(8,128)(2,1)} %get-tuple-element.164.m0.o0, bf16[3,128,384]{2,1,0:T(8,128)(2,1)} %copy-done.11, bf16[3,128,384]{2,1,0:T(8,128)(2,1)} %copy-done.10, ...), custom_call_target="tpu_custom_call" | custom-call | flops 905969664 | bytes 7077888 | tf_op jit(solution)/shard_map/mix/pallas_call | solution.py:118
  183.8 2.9 collective-permute-done.19.x1
  187.7 38.1 %mlp.1 = (f32[3,256,768]{2,1,0:T(8,128)}, f32[3,256,768]{2,1,0:T(8,128)}, bf16[2,3,256,768]{3,2,1,0:T(8,128)(2,1)}, bf16[4,96,1536]{2,1,0:T(8,128)(2,1)}, bf16[4...) custom-call(s32[7]{0:T(128)} %concatenate.22.meta, ...), custom_call_target="tpu_custom_call" | custom-call | flops 21743271936 | bytes 11796480 | tf_op jit(solution)/shard_map/mlp/pallas_call | solution.py:118
  227.0 3.8 collective-permute-done.20.got
  230.8 12.4 %turn.1 = (bf16[3,256,768]{2,1,0:T(8,128)(2,1)}, f32[3,256,768]{2,1,0:T(8,128)}, bf16[3,128,384]{2,1,0:T(8,128)(2,1)}, bf16[3,128,384]{2,1,0:T(8,128)(2,1)}, bf1...) custom-call(s32[7]{0:T(128)} %concatenate.22.meta, ...), custom_call_target="tpu_custom_call" | custom-call | flops 1811939328 | bytes 14155776 | tf_op jit(solution)/shard_map/turn/pallas_call | solution.py:118
  247.8 2.9 split.1
  250.7 4.6 all-to-all-start.2
  256.5 3.4 half.2
  259.9 1.8 collective-permute-start.28
  261.7 2.4 collective-permute-start.29
  264.8 16.1 %attend_back.3.refs_2_.refs_3_ = bf16[1,1024,576]{2,1,0:T(8,128)(2,1)} custom-call(s32[7]{0:T(128)} %concatenate.22.meta, bf16[3,512,576]{2,1,0:T(8,128)(2,1)} %qkv.2.qa.refs_0_, bf16[3,512,576]{2,1,0:T(8,128)(2,1)} %qkv.3.qb.refs_1_, bf16[3,3,1024,1024]{3,2,1,0:T(8,128)(2,1)} %get-tuple-element.194.weights, f32[3,1024,128]{2,1,0:T(8,128)} %get-tuple-element.195.recips, ...), custom_call_target="tpu_custom_call" | custom-call | flops 6442450944 | bytes 6291456 | tf_op jit(solution)/shard_map/attend_back/pallas_call | solution.py:118
  280.9 5.7 %proj_back.6 = (bf16[2,1,256,768]{3,2,1,0:T(8,128)(2,1)}, f32[768,576]{1,0:T(8,128)}, f32[1,576]{1,0:T(1,128)}, f32[8,768]{1,0:T(8,128)}) custom-call(s32[7]{0:T(128)} %concatenate.22.meta, bf16[3,256,768]{2,1,0:T(8,128)(2,1)} %collective-permute-done.x1.refs_0_, bf16[3,256,768]{2,1,0:T(8,128)(2,1)} %collective-permute-done.7.x1.refs_1_, ...), custom_call_target="tpu_custom_call" | custom-call | flops 905969664 | bytes 2359296 | tf_op jit(solution)/shard_map/proj_back/pallas_call | solution.py:118
  286.7 4.7 collective-permute-done.29.refs_2_
  292.2 2.8 gather.3.refs_0_
  295.0 3.4 half.3
  298.3 16.4 %attend_back.4.refs_2_.refs_3_ = bf16[1,1024,576]{2,1,0:T(8,128)(2,1)} custom-call(s32[7]{0:T(128)} %concatenate.22.meta, bf16[3,512,576]{2,1,0:T(8,128)(2,1)} %qkv.2.qa.refs_0_, bf16[3,512,576]{2,1,0:T(8,128)(2,1)} %qkv.3.qb.refs_1_, bf16[3,3,1024,1024]{3,2,1,0:T(8,128)(2,1)} %get-tuple-element.194.weights, f32[3,1024,128]{2,1,0:T(8,128)} %get-tuple-element.195.recips, ...), custom_call_target="tpu_custom_call" | custom-call | flops 6442450944 | bytes 6291456 | tf_op jit(solution)/shard_map/attend_back/pallas_call | solution.py:118
  315.7 6.8 %proj_back.7 = (bf16[1,256,768]{2,1,0:T(8,128)(2,1)}, f32[1,256,768]{2,1,0:T(8,128)}, f32[768,576]{1,0:T(8,128)}, f32[1,576]{1,0:T(1,128)}, f32[8,768]{1,0:T(8,128)}) custom-call(s32[7]{0:T(128)} %concatenate.22.meta, bf16[3,256,768]{2,1,0:T(8,128)(2,1)} %copy-done.1, bf16[3,256,768]{2,1,0:T(8,128)(2,1)} %refs_0_.3, ...), custom_call_target="tpu_custom_call" | custom-call | flops 905969664 | bytes 2359296 | tf_op jit(solution)/shard_map/proj_back/pallas_call | solution.py:118
  322.5 6.4 %proj_back.8 = (bf16[2,1,256,768]{3,2,1,0:T(8,128)(2,1)}, f32[768,576]{1,0:T(8,128)}, f32[1,576]{1,0:T(1,128)}, f32[8,768]{1,0:T(8,128)}) custom-call(s32[7]{0:T(128)} %concatenate.22.meta, bf16[3,256,768]{2,1,0:T(8,128)(2,1)} %collective-permute-done.x1.refs_0_, bf16[3,256,768]{2,1,0:T(8,128)(2,1)} %collective-permute-done.7.x1.refs_1_, ...), custom_call_target="tpu_custom_call" | custom-call | flops 905969664 | bytes 2359296 | tf_op jit(solution)/shard_map/proj_back/pallas_call | solution.py:118
  329.6 7.7 %all-to-all-start.3 = ((f32[8,4,2304]{2,1,0:T(4,128)}), f32[8,4,2304]{2,1,0:T(4,128)S(1)}, u32[]{:S(2)}, u32[]{:S(2)}) async-start(f32[8,4,2304]{2,1,0:T(4,128)} %broadcast_in_dim.10), calls=%async_computation.3 | async-start | bytes 589824 | tf_op jit(solution)/shard_map/all_to_all | solution.py:99
  337.3 2.0 collective-permute-start.32
  339.3 2.4 collective-permute-start.33
  343.1 5.2 %all-to-all-done.3 = f32[8,4,2304]{2,1,0:T(4,128)S(1)} async-done(((f32[8,4,2304]{2,1,0:T(4,128)}), f32[8,4,2304]{2,1,0:T(4,128)S(1)}, u32[]{:S(2)}, u32[]{:S(2)}) %all-to-all-start.3) | async-done | bytes 294944 | tf_op jit(solution)/shard_map/all_to_all | solution.py:99
  348.4 8.6 %collective-permute-done.32.refs_2_ = bf16[96,1536]{1,0:T(8,128)(2,1)S(1)} collective-permute-done((bf16[96,1536]{1,0:T(8,128)(2,1)}, bf16[96,1536]{1,0:T(8,128)(2,1)S(1)}, u32[]{:S(2)}, u32[]{:S(2)}) %collective-permute-start.32) | collective-permute-done | bytes 294944 | tf_op jit(solution)/shard_map/ppermute | solution.py:81
  357.0 10.2 %collective-permute-done.33.refs_3_ = bf16[96,1536]{1,0:T(8,128)(2,1)S(1)} collective-permute-done((bf16[96,1536]{1,0:T(8,128)(2,1)}, bf16[96,1536]{1,0:T(8,128)(2,1)S(1)}, u32[]{:S(2)}, u32[]{:S(2)}) %collective-permute-start.33) | collective-permute-done | bytes 294944 | tf_op jit(solution)/shard_map/ppermute | solution.py:81
  368.6 3.3 gather.4.own
  372.5 6.8 %proj_back.9 = (bf16[1,256,768]{2,1,0:T(8,128)(2,1)}, f32[1,256,768]{2,1,0:T(8,128)}, f32[768,576]{1,0:T(8,128)}, f32[1,576]{1,0:T(1,128)}, f32[8,768]{1,0:T(8,128)}) custom-call(s32[7]{0:T(128)} %concatenate.22.meta, bf16[3,256,768]{2,1,0:T(8,128)(2,1)} %copy-done.1, bf16[3,256,768]{2,1,0:T(8,128)(2,1)} %refs_0_.3, ...), custom_call_target="tpu_custom_call" | custom-call | flops 905969664 | bytes 2359296 | tf_op jit(solution)/shard_map/proj_back/pallas_call | solution.py:118
  380.0 3.8 last.3.refs_6_
  383.9 16.3 %attend_back.5.refs_2_.refs_3_ = bf16[1,1024,576]{2,1,0:T(8,128)(2,1)} custom-call(s32[7]{0:T(128)} %concatenate.22.meta, bf16[3,512,576]{2,1,0:T(8,128)(2,1)} %qkv.2.qa.refs_0_, bf16[3,512,576]{2,1,0:T(8,128)(2,1)} %qkv.3.qb.refs_1_, bf16[3,3,1024,1024]{3,2,1,0:T(8,128)(2,1)} %get-tuple-element.194.weights, f32[3,1024,128]{2,1,0:T(8,128)} %get-tuple-element.195.recips, ...), custom_call_target="tpu_custom_call" | custom-call | flops 6442450944 | bytes 6291456 | tf_op jit(solution)/shard_map/attend_back/pallas_call | solution.py:118
  400.2 6.5 %proj_back.10 = (bf16[2,1,256,768]{3,2,1,0:T(8,128)(2,1)}, f32[768,576]{1,0:T(8,128)}, f32[1,576]{1,0:T(1,128)}, f32[8,768]{1,0:T(8,128)}) custom-call(s32[7]{0:T(128)} %concatenate.22.meta, bf16[3,256,768]{2,1,0:T(8,128)(2,1)} %collective-permute-done.x1.refs_0_, bf16[3,256,768]{2,1,0:T(8,128)(2,1)} %collective-permute-done.7.x1.refs_1_, ...), custom_call_target="tpu_custom_call" | custom-call | flops 905969664 | bytes 2359296 | tf_op jit(solution)/shard_map/proj_back/pallas_call | solution.py:118
  409.5 7.9 %all-to-all-start.5 = ((f32[8,32,96]{2,1,0:T(8,128)}), f32[8,32,96]{2,1,0:T(8,128)S(1)}, u32[]{:S(2)}, u32[]{:S(2)}) async-start(f32[8,32,96]{2,1,0:T(8,128)} %broadcast_in_dim.11), calls=%async_computation.5 | async-start | bytes 262144 | tf_op jit(solution)/shard_map/all_to_all | solution.py:99
  417.4 15.1 %collective-permute-done.38.refs_4_ = bf16[1,256,768]{2,1,0:T(8,128)(2,1)S(1)} collective-permute-done((bf16[1,256,768]{2,1,0:T(8,128)(2,1)}, bf16[1,256,768]{2,1,0:T(8,128)(2,1)S(1)}, u32[]{:S(2)}, u32[]{:S(2)}) %collective-permute-start.38) | collective-permute-done | bytes 393248 | tf_op jit(solution)/shard_map/ppermute | solution.py:77
  433.2 3.8 last.4.refs_6_
  437.0 6.7 %proj_back.11 = (bf16[1,256,768]{2,1,0:T(8,128)(2,1)}, f32[1,256,768]{2,1,0:T(8,128)}, bf16[8,112,576]{2,1,0:T(8,128)(2,1)}) custom-call(s32[7]{0:T(128)} %concatenate.22.meta, bf16[3,256,768]{2,1,0:T(8,128)(2,1)} %copy-done.1, bf16[3,256,768]{2,1,0:T(8,128)(2,1)} %refs_0_.3, bf16[1,1024,576]{2,1,0:T(8,128)(2,1)} %attend_back.5.refs_2_.refs_3_, ...), custom_call_target="tpu_custom_call" | custom-call | flops 905969664 | bytes 2359296 | tf_op jit(solution)/shard_map/proj_back/pallas_call | solution.py:118
  443.8 7.7 %all-to-all-start.4 = ((bf16[8,112,576]{2,1,0:T(8,128)(2,1)}), bf16[8,112,576]{2,1,0:T(8,128)(2,1)}, u32[]{:S(2)}, u32[]{:S(2)}) async-start(bf16[8,112,576]{2,1,0:T(8,128)(2,1)} %get-tuple-element.254), calls=%async_computation.4 | async-start | bytes 2293760 | tf_op jit(solution)/shard_map/all_to_all | solution.py:99
  457.0 4.2 close_rest.1
  461.2 18.0 %all-to-all-done.4.refs_0_ = bf16[8,112,576]{2,1,0:T(8,128)(2,1)} async-done(((bf16[8,112,576]{2,1,0:T(8,128)(2,1)}), bf16[8,112,576]{2,1,0:T(8,128)(2,1)}, u32[]{:S(2)}, u32[]{:S(2)}) %all-to-all-start.4) | async-done | bytes 1032224 | tf_op jit(solution)/shard_map/all_to_all | solution.py:99
  479.3 2.7 gather.5.own
  484.1 4.0 last.5
  490.4 3.2 close_in.1
  (171 shorter events, 50.8 us)
Async XLA Ops:
  0.6 92.8 %copy-start = (bf16[96,2304]{1,0:T(8,128)(2,1)S(1)}, bf16[96,2304]{1,0:T(8,128)(2,1)}, u32[]{:S(2)}) copy-start(bf16[96,2304]{1,0:T(8,128)(2,1)} %param.27) | copy-start | bytes 1327108
  10.6 8.9 %collective-permute-start.1 = (bf16[112,576]{1,0:T(8,128)(2,1)}, bf16[112,576]{1,0:T(8,128)(2,1)S(1)}, u32[]{:S(2)}, u32[]{:S(2)}) collective-permute-start(bf16[112,576]{1,0:T(8,128)(2,1)} %pack_in.1.refs_0_), channel_id=1, source_target_pairs={{0,8},{4,12},{8,0},{12,4},{16,24},{20,28},{24,16},{28,20},{1,9},{5... | collective-permute-start | bytes 387080 | tf_op jit(solution)/shard_map/ppermute | solution.py:81
  13.6 13.9 %collective-permute-start.2 = (bf16[112,576]{1,0:T(8,128)(2,1)}, bf16[112,576]{1,0:T(8,128)(2,1)S(1)}, u32[]{:S(2)}, u32[]{:S(2)}) collective-permute-start(bf16[112,576]{1,0:T(8,128)(2,1)} %pack_in.1.refs_0_), channel_id=1, source_target_pairs={{0,16},{4,20},{8,24},{12,28},{16,0},{20,4},{24,8},{28,12},{1,17},{... | collective-permute-start | bytes 387080 | tf_op jit(solution)/shard_map/ppermute | solution.py:81
  16.2 11.3 %collective-permute-start.3 = (bf16[112,576]{1,0:T(8,128)(2,1)}, bf16[112,576]{1,0:T(8,128)(2,1)S(1)}, u32[]{:S(2)}, u32[]{:S(2)}) collective-permute-start(bf16[112,576]{1,0:T(8,128)(2,1)} %pack_in.1.refs_0_), channel_id=1, source_target_pairs={{0,24},{4,28},{8,16},{12,20},{16,8},{20,12},{24,0},{28,4},{1,25},{... | collective-permute-start | bytes 387080 | tf_op jit(solution)/shard_map/ppermute | solution.py:81
  16.2 38.4 %collective-permute-start.6 = (bf16[3,256,768]{2,1,0:T(8,128)(2,1)}, bf16[3,256,768]{2,1,0:T(8,128)(2,1)S(1)}, u32[]{:S(2)}, u32[]{:S(2)}) collective-permute-start(bf16[3,256,768]{2,1,0:T(8,128)(2,1)} %refs_0_.3), channel_id=1, source_target_pairs={{0,2},{1,3},{2,0},{3,1},{4,6},{5,7},{6,4},{7,5},{8,10},{9,11},{10,... | collective-permute-start | bytes 3538952 | tf_op jit(solution)/shard_map/ppermute | solution.py:77
  17.9 28.3 %collective-permute-start = (bf16[3,256,768]{2,1,0:T(8,128)(2,1)}, bf16[3,256,768]{2,1,0:T(8,128)(2,1)}, u32[]{:S(2)}, u32[]{:S(2)}) collective-permute-start(bf16[3,256,768]{2,1,0:T(8,128)(2,1)} %refs_0_.3), channel_id=1, source_target_pairs={{0,1},{1,0},{2,3},{3,2},{4,5},{5,4},{6,7},{7,6},{8,9},{9,8},{10,11... | collective-permute-start | bytes 3538952 | tf_op jit(solution)/shard_map/ppermute | solution.py:77
  19.5 15.0 %copy-start.14 = (bf16[112,576]{1,0:T(8,128)(2,1)}, bf16[112,576]{1,0:T(8,128)(2,1)S(1)}, u32[]{:S(2)}) copy-start(bf16[112,576]{1,0:T(8,128)(2,1)S(1)} %collective-permute-done.1.refs_1_) | copy-start | bytes 387076
  27.5 7.0 %copy-start.15 = (bf16[112,576]{1,0:T(8,128)(2,1)}, bf16[112,576]{1,0:T(8,128)(2,1)S(1)}, u32[]{:S(2)}) copy-start(bf16[112,576]{1,0:T(8,128)(2,1)S(1)} %collective-permute-done.2.refs_2_) | copy-start | bytes 387076
  30.1 12.6 %collective-permute-start.4 = (bf16[4,112,576]{2,1,0:T(8,128)(2,1)}, bf16[4,112,576]{2,1,0:T(8,128)(2,1)}, u32[]{:S(2)}, u32[]{:S(2)}) collective-permute-start(bf16[4,112,576]{2,1,0:T(8,128)(2,1)} %pad_maximum_fusion.1), channel_id=1, source_target_pairs={{0,4},{4,0},{8,12},{12,8},{16,20},{20,16},{24,28},{28,24},{1,5},{5... | collective-permute-start | bytes 1548296 | tf_op jit(solution)/shard_map/ppermute | solution.py:81
  54.6 42.5 %copy-start.1 = (bf16[3,256,768]{2,1,0:T(8,128)(2,1)}, bf16[3,256,768]{2,1,0:T(8,128)(2,1)S(1)}, u32[]{:S(2)}) copy-start(bf16[3,256,768]{2,1,0:T(8,128)(2,1)S(1)} %collective-permute-done.6.x0.refs_0_) | copy-start | bytes 3538948
  54.6 42.4 %collective-permute-start.7 = (bf16[3,256,768]{2,1,0:T(8,128)(2,1)S(1)}, bf16[3,256,768]{2,1,0:T(8,128)(2,1)}, u32[]{:S(2)}, u32[]{:S(2)}) collective-permute-start(bf16[3,256,768]{2,1,0:T(8,128)(2,1)S(1)} %collective-permute-done.6.x0.refs_0_), channel_id=1, source_target_pairs={{0,1},{1,0},{2,3},{3,2},{4,5},{5,4},{6,7},{7,6},{8,9},{9,8},{10,11... | collective-permute-start | bytes 3538952 | tf_op jit(solution)/shard_map/ppermute | solution.py:77
  54.7 50.8 %collective-permute-start.10 = (bf16[3,256,768]{2,1,0:T(8,128)(2,1)}, bf16[3,256,768]{2,1,0:T(8,128)(2,1)}, u32[]{:S(2)}, u32[]{:S(2)}) collective-permute-start(bf16[3,256,768]{2,1,0:T(8,128)(2,1)} %out_grad.1), channel_id=1, source_target_pairs={{0,1},{1,0},{2,3},{3,2},{4,5},{5,4},{6,7},{7,6},{8,9},{9,8},{10,11... | collective-permute-start | bytes 3538952 | tf_op jit(solution)/shard_map/ppermute | solution.py:77
  55.2 32.1 %collective-permute-start.8 = (bf16[96,3456]{1,0:T(8,128)(2,1)}, bf16[96,3456]{1,0:T(8,128)(2,1)}, u32[]{:S(2)}, u32[]{:S(2)}) collective-permute-start(bf16[96,3456]{1,0:T(8,128)(2,1)} %pack_rest.1.refs_0_), channel_id=1, source_target_pairs={{0,8},{4,12},{8,0},{12,4},{16,24},{20,28},{24,16},{28,20},{1,9},{5... | collective-permute-start | bytes 1990664 | tf_op jit(solution)/shard_map/ppermute | solution.py:81
  58.8 35.7 %collective-permute-start.9 = (bf16[96,3456]{1,0:T(8,128)(2,1)}, bf16[96,3456]{1,0:T(8,128)(2,1)}, u32[]{:S(2)}, u32[]{:S(2)}) collective-permute-start(bf16[96,3456]{1,0:T(8,128)(2,1)} %pack_rest.1.refs_0_), channel_id=1, source_target_pairs={{0,4},{4,0},{8,12},{12,8},{16,20},{20,16},{24,28},{28,24},{1,5},{5... | collective-permute-start | bytes 1990664 | tf_op jit(solution)/shard_map/ppermute | solution.py:81
  60.3 45.2 %collective-permute-start.5 = (bf16[96,3456]{1,0:T(8,128)(2,1)}, bf16[96,3456]{1,0:T(8,128)(2,1)}, u32[]{:S(2)}, u32[]{:S(2)}) collective-permute-start(bf16[96,3456]{1,0:T(8,128)(2,1)} %pack_rest.1.refs_0_), channel_id=1, source_target_pairs={{0,16},{4,20},{8,24},{12,28},{16,0},{20,4},{24,8},{28,12},{1,17},{... | collective-permute-start | bytes 1990664 | tf_op jit(solution)/shard_map/ppermute | solution.py:81
  61.5 31.9 %all-to-all-start = ((bf16[8,32,96]{2,1,0:T(8,128)(2,1)}), bf16[8,32,96]{2,1,0:T(8,128)(2,1)S(1)}, u32[]{:S(2)}, u32[]{:S(2)}) async-start(bf16[8,32,96]{2,1,0:T(8,128)(2,1)} %get-tuple-element.154), calls=%async_computation | async-start | bytes 131072 | tf_op jit(solution)/shard_map/all_to_all | solution.py:99
  87.3 32.5 %collective-permute-start.11 = (bf16[96,3456]{1,0:T(8,128)(2,1)}, bf16[96,3456]{1,0:T(8,128)(2,1)}, u32[]{:S(2)}, u32[]{:S(2)}) collective-permute-start(bf16[96,3456]{1,0:T(8,128)(2,1)} %collective-permute-done.8.refs_2_), channel_id=1, source_target_pairs={{0,4},{4,0},{8,12},{12,8},{16,20},{20,16},{24,28},{28,24},{1,5},{5... | collective-permute-start | bytes 1990664 | tf_op jit(solution)/shard_map/ppermute | solution.py:81
  94.4 39.9 %collective-permute-start.16 = (bf16[96,3456]{1,0:T(8,128)(2,1)}, bf16[96,3456]{1,0:T(8,128)(2,1)}, u32[]{:S(2)}, u32[]{:S(2)}) collective-permute-start(bf16[96,3456]{1,0:T(8,128)(2,1)} %pack_rest.1.refs_0_), channel_id=1, source_target_pairs={{0,24},{4,28},{8,16},{12,20},{16,8},{20,12},{24,0},{28,4},{1,25},{... | collective-permute-start | bytes 1990664 | tf_op jit(solution)/shard_map/ppermute | solution.py:81
  119.8 20.2 %copy-start.27 = (f32[1,2304]{1,0:T(1,128)S(1)}, f32[1,2304]{1,0:T(1,128)}, u32[]{:S(2)}) copy-start(f32[1,2304]{1,0:T(1,128)} %get-tuple-element.172) | copy-start | bytes 27652
  119.8 20.2 %copy-start.4 = (bf16[3,128,384]{2,1,0:T(8,128)(2,1)S(1)}, bf16[3,128,384]{2,1,0:T(8,128)(2,1)}, u32[]{:S(2)}) copy-start(bf16[3,128,384]{2,1,0:T(8,128)(2,1)} %get-tuple-element.160.o2) | copy-start | bytes 884740
  119.9 47.4 %copy-start.5 = (bf16[3,128,384]{2,1,0:T(8,128)(2,1)S(1)}, bf16[3,128,384]{2,1,0:T(8,128)(2,1)}, u32[]{:S(2)}) copy-start(bf16[3,128,384]{2,1,0:T(8,128)(2,1)} %get-tuple-element.166.o3) | copy-start | bytes 884740
  134.3 34.7 %collective-permute-start.17 = (bf16[96,3456]{1,0:T(8,128)(2,1)}, bf16[96,3456]{1,0:T(8,128)(2,1)}, u32[]{:S(2)}, u32[]{:S(2)}) collective-permute-start(bf16[96,3456]{1,0:T(8,128)(2,1)} %collective-permute-done.16.refs_6_), channel_id=1, source_target_pairs={{0,4},{4,0},{8,12},{12,8},{16,20},{20,16},{24,28},{28,24},{1,5},{5... | collective-permute-start | bytes 1990664 | tf_op jit(solution)/shard_map/ppermute | solution.py:81
  135.9 33.1 %collective-permute-start.15 = (bf16[96,3456]{1,0:T(8,128)(2,1)}, bf16[96,3456]{1,0:T(8,128)(2,1)}, u32[]{:S(2)}, u32[]{:S(2)}) collective-permute-start(bf16[96,3456]{1,0:T(8,128)(2,1)} %collective-permute-done.5.refs_4_), channel_id=1, source_target_pairs={{0,4},{4,0},{8,12},{12,8},{16,20},{20,16},{24,28},{28,24},{1,5},{5... | collective-permute-start | bytes 1990664 | tf_op jit(solution)/shard_map/ppermute | solution.py:81
  136.4 30.8 %all-to-all-start.1 = ((f32[8,4,2304]{2,1,0:T(4,128)}), f32[8,4,2304]{2,1,0:T(4,128)S(1)}, u32[]{:S(2)}, u32[]{:S(2)}) async-start(f32[8,4,2304]{2,1,0:T(4,128)} %reshape.79), calls=%async_computation.1 | async-start | bytes 589824 | tf_op jit(solution)/shard_map/all_to_all | solution.py:99
  140.1 35.4 %collective-permute-start.13 = (bf16[3,128,384]{2,1,0:T(8,128)(2,1)S(1)}, bf16[3,128,384]{2,1,0:T(8,128)(2,1)S(1)}, u32[]{:S(2)}, u32[]{:S(2)}) collective-permute-start(bf16[3,128,384]{2,1,0:T(8,128)(2,1)S(1)} %copy-done.4), channel_id=1, source_target_pairs={{0,2},{1,3},{2,0},{3,1},{4,6},{5,7},{6,4},{7,5},{8,10},{9,11},{10,... | collective-permute-start | bytes 884744 | tf_op jit(solution)/shard_map/ppermute | solution.py:77
  167.3 8.2 %collective-permute-start.12 = (bf16[3,128,384]{2,1,0:T(8,128)(2,1)}, bf16[3,128,384]{2,1,0:T(8,128)(2,1)S(1)}, u32[]{:S(2)}, u32[]{:S(2)}) collective-permute-start(bf16[3,128,384]{2,1,0:T(8,128)(2,1)} %get-tuple-element.165.o1), channel_id=1, source_target_pairs={{0,1},{1,0},{2,3},{3,2},{4,5},{5,4},{6,7},{7,6},{8,9},{9,8},{10,11... | collective-permute-start | bytes 884744 | tf_op jit(solution)/shard_map/ppermute | solution.py:77
  167.3 8.7 %collective-permute-start.14 = (bf16[3,128,384]{2,1,0:T(8,128)(2,1)S(1)}, bf16[3,128,384]{2,1,0:T(8,128)(2,1)S(1)}, u32[]{:S(2)}, u32[]{:S(2)}) collective-permute-start(bf16[3,128,384]{2,1,0:T(8,128)(2,1)S(1)} %copy-done.5), channel_id=1, source_target_pairs={{0,3},{1,2},{2,1},{3,0},{4,7},{5,6},{6,5},{7,4},{8,11},{9,10},{10,... | collective-permute-start | bytes 884744 | tf_op jit(solution)/shard_map/ppermute | solution.py:77
  174.9 2.3 collective-permute-start.18
  183.7 3.1 collective-permute-start.19
  225.9 4.9 collective-permute-start.20
  226.1 29.2 %collective-permute-start.23 = (bf16[4,96,1536]{2,1,0:T(8,128)(2,1)}, bf16[4,96,1536]{2,1,0:T(8,128)(2,1)}, u32[]{:S(2)}, u32[]{:S(2)}) collective-permute-start(bf16[4,96,1536]{2,1,0:T(8,128)(2,1)} %get-tuple-element.191), channel_id=1, source_target_pairs={{0,4},{4,0},{8,12},{12,8},{16,20},{20,16},{24,28},{28,24},{1,5},{5... | collective-permute-start | bytes 3538952 | tf_op jit(solution)/shard_map/ppermute | solution.py:81
  243.2 3.8 collective-permute-start.21
  244.4 1.3 collective-permute-start.22
  244.9 50.1 %collective-permute-start.31 = (bf16[4,96,1536]{2,1,0:T(8,128)(2,1)}, bf16[4,96,1536]{2,1,0:T(8,128)(2,1)}, u32[]{:S(2)}, u32[]{:S(2)}) collective-permute-start(bf16[4,96,1536]{2,1,0:T(8,128)(2,1)} %get-tuple-element.212), channel_id=1, source_target_pairs={{0,4},{4,0},{8,12},{12,8},{16,20},{20,16},{24,28},{28,24},{1,5},{5... | collective-permute-start | bytes 3538952 | tf_op jit(solution)/shard_map/ppermute | solution.py:81
  245.8 14.1 %collective-permute-start.24 = (bf16[3,128,384]{2,1,0:T(8,128)(2,1)}, bf16[3,128,384]{2,1,0:T(8,128)(2,1)S(1)}, u32[]{:S(2)}, u32[]{:S(2)}) collective-permute-start(bf16[3,128,384]{2,1,0:T(8,128)(2,1)} %get-tuple-element.197), channel_id=1, source_target_pairs={{0,1},{1,0},{2,3},{3,2},{4,5},{5,4},{6,7},{7,6},{8,9},{9,8},{10,11... | collective-permute-start | bytes 884744 | tf_op jit(solution)/shard_map/ppermute | solution.py:77
  245.8 15.9 %collective-permute-start.25 = (bf16[3,128,384]{2,1,0:T(8,128)(2,1)}, bf16[3,128,384]{2,1,0:T(8,128)(2,1)S(1)}, u32[]{:S(2)}, u32[]{:S(2)}) collective-permute-start(bf16[3,128,384]{2,1,0:T(8,128)(2,1)} %get-tuple-element.198), channel_id=1, source_target_pairs={{0,2},{1,3},{2,0},{3,1},{4,6},{5,7},{6,4},{7,5},{8,10},{9,11},{10,... | collective-permute-start | bytes 884744 | tf_op jit(solution)/shard_map/ppermute | solution.py:77
  247.0 17.0 %collective-permute-start.26 = (bf16[3,128,384]{2,1,0:T(8,128)(2,1)}, bf16[3,128,384]{2,1,0:T(8,128)(2,1)S(1)}, u32[]{:S(2)}, u32[]{:S(2)}) collective-permute-start(bf16[3,128,384]{2,1,0:T(8,128)(2,1)} %get-tuple-element.199), channel_id=1, source_target_pairs={{0,3},{1,2},{2,1},{3,0},{4,7},{5,6},{6,5},{7,4},{8,11},{9,10},{10,... | collective-permute-start | bytes 884744 | tf_op jit(solution)/shard_map/ppermute | solution.py:77
  250.7 47.7 %all-to-all-start.2 = ((bf16[8,96,384]{2,1,0:T(8,128)(2,1)}), bf16[8,96,384]{2,1,0:T(8,128)(2,1)}, u32[]{:S(2)}, u32[]{:S(2)}) async-start(bf16[8,96,384]{2,1,0:T(8,128)(2,1)} %bitcast.28), calls=%async_computation.2 | async-start | bytes 1179648 | tf_op jit(solution)/shard_map/all_to_all | solution.py:99
  255.3 25.6 %collective-permute-start.27 = (f32[4,2304]{1,0:T(4,128)S(1)}, f32[4,2304]{1,0:T(4,128)S(1)}, u32[]{:S(2)}, u32[]{:S(2)}) collective-permute-start(f32[4,2304]{1,0:T(4,128)S(1)} %fusion.17), channel_id=1, source_target_pairs={{0,2},{1,3},{2,0},{3,1},{4,6},{5,7},{6,4},{7,5},{8,10},{9,11},{10,... | collective-permute-start | bytes 110600 | tf_op jit(solution)/shard_map/ppermute | solution.py:77
  259.9 4.4 copy-start.6
  259.9 26.8 %collective-permute-start.28 = (bf16[96,1536]{1,0:T(8,128)(2,1)}, bf16[96,1536]{1,0:T(8,128)(2,1)S(1)}, u32[]{:S(2)}, u32[]{:S(2)}) collective-permute-start(bf16[96,1536]{1,0:T(8,128)(2,1)} %get-tuple-element.204), channel_id=1, source_target_pairs={{0,8},{4,12},{8,0},{12,4},{16,24},{20,28},{24,16},{28,20},{1,9},{5... | collective-permute-start | bytes 884744 | tf_op jit(solution)/shard_map/ppermute | solution.py:81
  261.7 29.8 %collective-permute-start.29 = (bf16[96,1536]{1,0:T(8,128)(2,1)}, bf16[96,1536]{1,0:T(8,128)(2,1)S(1)}, u32[]{:S(2)}, u32[]{:S(2)}) collective-permute-start(bf16[96,1536]{1,0:T(8,128)(2,1)} %get-tuple-element.205), channel_id=1, source_target_pairs={{0,16},{4,20},{8,24},{12,28},{16,0},{20,4},{24,8},{28,12},{1,17},{... | collective-permute-start | bytes 884744 | tf_op jit(solution)/shard_map/ppermute | solution.py:81
  264.1 27.4 %collective-permute-start.30 = (bf16[96,1536]{1,0:T(8,128)(2,1)}, bf16[96,1536]{1,0:T(8,128)(2,1)}, u32[]{:S(2)}, u32[]{:S(2)}) collective-permute-start(bf16[96,1536]{1,0:T(8,128)(2,1)} %get-tuple-element.206), channel_id=1, source_target_pairs={{0,24},{4,28},{8,16},{12,20},{16,8},{20,12},{24,0},{28,4},{1,25},{... | collective-permute-start | bytes 884744 | tf_op jit(solution)/shard_map/ppermute | solution.py:81
  286.7 28.1 %collective-permute-start.35 = (bf16[2,1,256,768]{3,2,1,0:T(8,128)(2,1)}, bf16[2,1,256,768]{3,2,1,0:T(8,128)(2,1)S(1)}, u32[]{:S(2)}, u32[]{:S(2)}) collective-permute-start(bf16[2,1,256,768]{3,2,1,0:T(8,128)(2,1)} %get-tuple-element.202), channel_id=1, source_target_pairs={{0,1},{1,0},{2,3},{3,2},{4,5},{5,4},{6,7},{7,6},{8,9},{9,8},{10,11... | collective-permute-start | bytes 2359304 | tf_op jit(solution)/shard_map/ppermute | solution.py:77
  286.7 4.8 copy-start.24
  328.8 43.6 %collective-permute-start.36 = (bf16[2,1,256,768]{3,2,1,0:T(8,128)(2,1)}, bf16[2,1,256,768]{3,2,1,0:T(8,128)(2,1)}, u32[]{:S(2)}, u32[]{:S(2)}) collective-permute-start(bf16[2,1,256,768]{3,2,1,0:T(8,128)(2,1)} %get-tuple-element.228), channel_id=1, source_target_pairs={{0,1},{1,0},{2,3},{3,2},{4,5},{5,4},{6,7},{7,6},{8,9},{9,8},{10,11... | collective-permute-start | bytes 2359304 | tf_op jit(solution)/shard_map/ppermute | solution.py:77
  329.6 18.7 %all-to-all-start.3 = ((f32[8,4,2304]{2,1,0:T(4,128)}), f32[8,4,2304]{2,1,0:T(4,128)S(1)}, u32[]{:S(2)}, u32[]{:S(2)}) async-start(f32[8,4,2304]{2,1,0:T(4,128)} %broadcast_in_dim.10), calls=%async_computation.3 | async-start | bytes 589824 | tf_op jit(solution)/shard_map/all_to_all | solution.py:99
  337.3 19.7 %collective-permute-start.32 = (bf16[96,1536]{1,0:T(8,128)(2,1)}, bf16[96,1536]{1,0:T(8,128)(2,1)S(1)}, u32[]{:S(2)}, u32[]{:S(2)}) collective-permute-start(bf16[96,1536]{1,0:T(8,128)(2,1)} %get-tuple-element.216), channel_id=1, source_target_pairs={{0,8},{4,12},{8,0},{12,4},{16,24},{20,28},{24,16},{28,20},{1,9},{5... | collective-permute-start | bytes 884744 | tf_op jit(solution)/shard_map/ppermute | solution.py:81
  339.3 27.9 %collective-permute-start.33 = (bf16[96,1536]{1,0:T(8,128)(2,1)}, bf16[96,1536]{1,0:T(8,128)(2,1)S(1)}, u32[]{:S(2)}, u32[]{:S(2)}) collective-permute-start(bf16[96,1536]{1,0:T(8,128)(2,1)} %get-tuple-element.217), channel_id=1, source_target_pairs={{0,16},{4,20},{8,24},{12,28},{16,0},{20,4},{24,8},{28,12},{1,17},{... | collective-permute-start | bytes 884744 | tf_op jit(solution)/shard_map/ppermute | solution.py:81
  341.7 25.5 %collective-permute-start.34 = (bf16[96,1536]{1,0:T(8,128)(2,1)}, bf16[96,1536]{1,0:T(8,128)(2,1)S(1)}, u32[]{:S(2)}, u32[]{:S(2)}) collective-permute-start(bf16[96,1536]{1,0:T(8,128)(2,1)} %get-tuple-element.218), channel_id=1, source_target_pairs={{0,24},{4,28},{8,16},{12,20},{16,8},{20,12},{24,0},{28,4},{1,25},{... | collective-permute-start | bytes 884744 | tf_op jit(solution)/shard_map/ppermute | solution.py:81
  341.7 37.6 %collective-permute-start.37 = (bf16[1,256,768]{2,1,0:T(8,128)(2,1)}, bf16[1,256,768]{2,1,0:T(8,128)(2,1)S(1)}, u32[]{:S(2)}, u32[]{:S(2)}) collective-permute-start(bf16[1,256,768]{2,1,0:T(8,128)(2,1)} %get-tuple-element.223), channel_id=1, source_target_pairs={{0,2},{1,3},{2,0},{3,1},{4,6},{5,7},{6,4},{7,5},{8,10},{9,11},{10,... | collective-permute-start | bytes 1179656 | tf_op jit(solution)/shard_map/ppermute | solution.py:77
  357.0 10.2 %copy-start.21 = (bf16[96,1536]{1,0:T(8,128)(2,1)}, bf16[96,1536]{1,0:T(8,128)(2,1)S(1)}, u32[]{:S(2)}) copy-start(bf16[96,1536]{1,0:T(8,128)(2,1)S(1)} %collective-permute-done.32.refs_2_) | copy-start | bytes 884740
  400.2 6.5 %copy-start.2 = (bf16[96,3456]{1,0:T(8,128)(2,1)S(1)}, bf16[96,3456]{1,0:T(8,128)(2,1)}, u32[]{:S(2)}) copy-start(bf16[96,3456]{1,0:T(8,128)(2,1)} %gather.4.own) | copy-start | bytes 1990660
  406.7 30.3 %collective-permute-start.39 = (bf16[2,1,256,768]{3,2,1,0:T(8,128)(2,1)}, bf16[2,1,256,768]{3,2,1,0:T(8,128)(2,1)}, u32[]{:S(2)}, u32[]{:S(2)}) collective-permute-start(bf16[2,1,256,768]{3,2,1,0:T(8,128)(2,1)} %get-tuple-element.245), channel_id=1, source_target_pairs={{0,1},{1,0},{2,3},{3,2},{4,5},{5,4},{6,7},{7,6},{8,9},{9,8},{10,11... | collective-permute-start | bytes 2359304 | tf_op jit(solution)/shard_map/ppermute | solution.py:77
  406.7 37.1 %collective-permute-start.40 = (bf16[96,3456]{1,0:T(8,128)(2,1)S(1)}, bf16[96,3456]{1,0:T(8,128)(2,1)}, u32[]{:S(2)}, u32[]{:S(2)}) collective-permute-start(bf16[96,3456]{1,0:T(8,128)(2,1)S(1)} %copy-done.2), channel_id=1, source_target_pairs={{0,2},{1,3},{2,0},{3,1},{4,6},{5,7},{6,4},{7,5},{8,10},{9,11},{10,... | collective-permute-start | bytes 1990664 | tf_op jit(solution)/shard_map/ppermute | solution.py:77
  408.1 24.3 %collective-permute-start.38 = (bf16[1,256,768]{2,1,0:T(8,128)(2,1)}, bf16[1,256,768]{2,1,0:T(8,128)(2,1)S(1)}, u32[]{:S(2)}, u32[]{:S(2)}) collective-permute-start(bf16[1,256,768]{2,1,0:T(8,128)(2,1)} %get-tuple-element.238), channel_id=1, source_target_pairs={{0,2},{1,3},{2,0},{3,1},{4,6},{5,7},{6,4},{7,5},{8,10},{9,11},{10,... | collective-permute-start | bytes 1179656 | tf_op jit(solution)/shard_map/ppermute | solution.py:77
  409.5 34.3 %all-to-all-start.5 = ((f32[8,32,96]{2,1,0:T(8,128)}), f32[8,32,96]{2,1,0:T(8,128)S(1)}, u32[]{:S(2)}, u32[]{:S(2)}) async-start(f32[8,32,96]{2,1,0:T(8,128)} %broadcast_in_dim.11), calls=%async_computation.5 | async-start | bytes 262144 | tf_op jit(solution)/shard_map/all_to_all | solution.py:99
  443.8 35.5 %all-to-all-start.4 = ((bf16[8,112,576]{2,1,0:T(8,128)(2,1)}), bf16[8,112,576]{2,1,0:T(8,128)(2,1)}, u32[]{:S(2)}, u32[]{:S(2)}) async-start(bf16[8,112,576]{2,1,0:T(8,128)(2,1)} %get-tuple-element.254), calls=%async_computation.4 | async-start | bytes 2293760 | tf_op jit(solution)/shard_map/all_to_all | solution.py:99
  451.5 3.0 copy-start.28
  452.7 4.3 collective-permute-start.41
  453.0 30.3 %collective-permute-start.42 = (bf16[1,256,768]{2,1,0:T(8,128)(2,1)S(1)}, bf16[1,256,768]{2,1,0:T(8,128)(2,1)S(1)}, u32[]{:S(2)}, u32[]{:S(2)}) collective-permute-start(bf16[1,256,768]{2,1,0:T(8,128)(2,1)S(1)} %copy-done.30), channel_id=1, source_target_pairs={{0,2},{1,3},{2,0},{3,1},{4,6},{5,7},{6,4},{7,5},{8,10},{9,11},{10,... | collective-permute-start | bytes 1179656 | tf_op jit(solution)/shard_map/ppermute | solution.py:77
  482.0 6.0 %collective-permute-start.43 = (bf16[112,576]{1,0:T(8,128)(2,1)}, bf16[112,576]{1,0:T(8,128)(2,1)S(1)}, u32[]{:S(2)}, u32[]{:S(2)}) collective-permute-start(bf16[112,576]{1,0:T(8,128)(2,1)} %gather.5.own), channel_id=1, source_target_pairs={{0,2},{1,3},{2,0},{3,1},{4,6},{5,7},{6,4},{7,5},{8,10},{9,11},{10,... | collective-permute-start | bytes 387080 | tf_op jit(solution)/shard_map/ppermute | solution.py:77
  484.1 4.0 copy-start.9
  488.1 1.6 collective-permute-start.44
  (18 other events, 19.9 us)
